TPU v7x, 32 devices: a whole 2x2x4 slice. The times are simulated.
32 devices in a mesh: patch: 16 (over z, y, core), lag: 2 (over x).
Axes of the slice: x: 2, y: 2, z: 4, core: 2. Of those that a mesh axis runs over, the one named last changes fastest.
Arguments:
- interaction: bfloat16 [30, 4096, 1280], P('lag', 'patch'), may hold values from -0.046875 to 0.046875
- history: bfloat16 [30, 4096, 128], P('lag', 'patch'), may hold values from -6 to 6
- near_inverse: bfloat16 [4096, 256], P('patch'), may hold values from -0.375 to 0.375
- lag_ranges: int32 [16, 10], P('patch'), may hold values from 1 to 31, as said below
- receiver_tile: int32 [4096, 1], P('patch'), may hold values from 0 to 15; in each aligned block of 256 rows (0 to 255, 256 to 511, ...) at most 16 rows name the same one
- receiver_panel: int32 [4096], P('patch'), may hold values from 0 to 255
- residuals: bfloat16 [4096, 4, 128], P('patch'), may hold values from -6 to 6
Outputs:
- densities: bfloat16 [4, 4096, 128], P(None, 'patch')
Inputs may be any that keep to these rules, and one draw needn't show every extreme that they name: `lag_ranges`: columns 0 to 4 hold the first active lag, columns 5 to 9 one past the last; every range holds at least 7 lags. `receiver_tile`: among the 256 receivers of one patch index, at most 16 lie on one patch.
All inputs are finite; a program needn't handle non-finite values.
Results may differ from a plain program's by a relative error of at most 0.0049.
Values may be sent and summed in bfloat16 or wider, within the bound.
No kernel may reach another device: no remote copies, remote signals or barrier semaphores. Data moves between devices by JAX's collectives and lax.ppermute only.
A program may use at most 64 MiB of HBM per device.

v0:
```python
import functools

import jax
import jax.numpy as jnp
from jax import lax
from jax.experimental import pallas as pl
from jax.experimental.pallas import tpu as pltpu
from jax.sharding import PartitionSpec as P

NEAR = 5
CAP = 16
HALF = NEAR // 2
LANES = 128
VMEM = pltpu.VMEM


def dot(left, right):
    return jnp.dot(left, right, preferred_element_type=jnp.float32)


def slot_offsets(patch):
    odd = lax.rem(patch, 2)
    high = lax.rem(lax.div(patch, 2), 2)
    return [4 * high, 1 + 2 * odd, 4 - 4 * high, 3 - 2 * odd, HALF]


def pairings(patches):
    far = [(i + 2 if i & 2 else i - 2) % patches for i in range(patches)]
    odd_even = [(i + 1 if i & 1 else i - 1) % patches for i in range(patches)]
    near = [i ^ 2 for i in range(patches)]
    core = [i ^ 1 for i in range(patches)]
    return [list(enumerate(p)) for p in (far, odd_even, near, core)]


def pack_kernel(tile_ref, panel_ref, rows_ref, out_ref):
    recv = rows_ref.shape[0]
    width = rows_ref.shape[1]
    slots = out_ref.shape[0]
    patches = slots // CAP
    tile = tile_ref[...]
    hot = lax.broadcasted_iota(jnp.int32, (patches, recv), 0) == tile
    before = lax.broadcasted_iota(jnp.int32, (recv, recv), 0) < lax.broadcasted_iota(
        jnp.int32, (recv, recv), 1
    )
    hot = jnp.where(hot, 1.0, 0.0)
    ahead = dot(hot.astype(jnp.bfloat16), jnp.where(before, 1.0, 0.0).astype(jnp.bfloat16))
    earlier = jnp.sum(hot * ahead, axis=0, keepdims=True).astype(jnp.int32)
    slot = tile * CAP + earlier
    placed = lax.broadcasted_iota(jnp.int32, (slots, recv), 0) == slot
    placer = jnp.where(placed, 1.0, 0.0).astype(jnp.bfloat16)
    out_ref[:, :width] = dot(placer, rows_ref[...]).astype(jnp.bfloat16)
    marks = jnp.where(placed, (panel_ref[...] + 1).astype(jnp.float32), 0.0)
    label = jnp.sum(marks, axis=1, keepdims=True)
    out_ref[:, width:] = jnp.broadcast_to(label, (slots, LANES)).astype(jnp.bfloat16)


def source_kernel(arrived_ref, *outs):
    slots = arrived_ref.shape[0]
    shots, tile_len = outs[0].shape
    width = len(outs) * shots
    label = arrived_ref[:, width:].astype(jnp.float32)
    lane = lax.broadcasted_iota(jnp.int32, (slots, LANES), 1)
    picker = jnp.concatenate(
        [
            jnp.where(label == (lane + (1 + first)).astype(jnp.float32), 1.0, 0.0)
            for first in range(0, tile_len, LANES)
        ],
        axis=1,
    ).astype(jnp.bfloat16)
    for step, out in enumerate(outs):
        out[...] = lax.dot_general(
            arrived_ref[:, step * shots : (step + 1) * shots],
            picker,
            (((0,), (0,)), ((), ())),
            preferred_element_type=jnp.float32,
        )


def older_kernel(steps, sizes, ranges, rim, history, inverse_hbm, weights, *refs):
    outs, (rows, blocks, sems, out_sems) = refs[:-4], refs[-4:]
    messages, outs = outs[: NEAR - 1], outs[NEAR - 1 :]
    own, stage, recent, inverse = outs[:4]
    rest = outs[4:]
    band, tile_len, shots = history.shape
    lag = lax.axis_index("lag")
    offsets = slot_offsets(lax.axis_index("patch"))

    def bounds(offset):
        base = lag * band + 1
        first = jnp.clip(ranges[0, offset] - base, 0, band)
        last = jnp.clip(ranges[0, NEAR + offset] - base, 0, band)
        return first, last

    def fetch(slot, offset, k):
        columns = pl.ds(pl.multiple_of(offset * tile_len, tile_len), tile_len)
        return pltpu.make_async_copy(
            weights.at[k, :, columns], blocks.at[slot, k], sems.at[slot, k]
        )

    def send(slot, step, target):
        return pltpu.make_async_copy(
            stage.at[slot, pl.ds(step * shots, shots)], target, out_sems.at[slot, step]
        )

    for slot, offset in enumerate(offsets):
        first, last = bounds(offset)
        lax.fori_loop(first, last, lambda k, c, s=slot, o=offset: fetch(s, o, k).start(), None)
    keep = [
        pltpu.make_async_copy(weights.at[pl.ds(0, steps - 1)], recent, out_sems.at[NEAR, 0]),
        pltpu.make_async_copy(inverse_hbm, inverse, out_sems.at[NEAR, 1]),
    ]
    for copy in keep:
        copy.start()
    for k in range(band):
        rows[(band - 1 - k) * shots : (band - k) * shots, :] = history[k].T

    @pl.when(lag > 0)
    def _():
        for k in range(steps - 1):
            at = (band + steps - 2 - k) * shots
            rows[at : at + shots, :] = rim[k].T

    @pl.when(lag == 0)
    def _():
        rows[band * shots :, :] = jnp.zeros(((steps - 1) * shots, tile_len), jnp.bfloat16)

    def window(k):
        return rows[pl.ds(pl.multiple_of((band - 1 - k) * shots, shots), steps * shots), :]

    def one_slot(slot, carry):
        offset = offsets[-1]
        for j in range(NEAR - 1):
            offset = jnp.where(slot == j, offsets[j], offset)
        first, last = bounds(offset)
        lax.fori_loop(first, last, lambda k, c: fetch(slot, offset, k).wait(), None)

        def emit(total):
            stage[slot] = total.astype(jnp.bfloat16)

            @pl.when(slot == NEAR - 1)
            def _():
                own[...] = total[:shots]

        def branch(size):
            def run():
                start = jnp.minimum(first, band - size)
                left, right = [], []
                for i in range(size):
                    k = start + i
                    live = (k >= first) & (k < last)
                    tile = blocks[slot, k]
                    left.append(window(k))
                    right.append(jnp.where(live, tile, jnp.zeros_like(tile)))
                emit(dot(jnp.concatenate(left, axis=1), jnp.concatenate(right, axis=0)))

            return run

        count = last - first
        which = jnp.where(count > 0, 1, 0)
        for i, size in enumerate(sizes[:-1]):
            which = jnp.where(count > size, i + 2, which)
        lax.switch(
            which,
            [lambda: emit(jnp.zeros((steps * shots, tile_len), jnp.float32))]
            + [branch(size) for size in sizes],
        )
        for j in range(NEAR - 1):
            pl.when(slot == j)(lambda j=j: send(j, 0, messages[j]).start())
        for step in range(1, steps):
            send(slot, step, rest[step - 1].at[pl.ds(slot * shots, shots)]).start()
        return carry

    lax.fori_loop(0, NEAR, one_slot, None)
    for copy in keep:
        copy.wait()
    for slot in range(NEAR):
        if slot < NEAR - 1:
            send(slot, 0, messages[slot]).wait()
        for step in range(1, steps):
            send(slot, step, rest[step - 1].at[pl.ds(slot * shots, shots)]).wait()


def step_kernel(step, last_step, ranges, source, inverse, own, *refs):
    shots = own.shape[0]
    tile_len = own.shape[1]
    refs = list(refs)
    received = [refs.pop(0) for _ in range(1 if step == 0 else NEAR - 1)]
    right = source[...] - own[...]
    for block in received:
        right = right - block[...].astype(jnp.float32)
    density = dot(right.astype(jnp.bfloat16), inverse[...])
    if last_step:
        (natural,) = refs
        natural[...] = density.T.astype(jnp.bfloat16)
        return
    weights, stage, rest_far = refs[:3]
    olders, outs = refs[3 : 3 + step], refs[3 + step :]
    density_ref, next_own = outs[:2]
    messages = outs[2:]
    rounded = density.astype(jnp.bfloat16)
    density_ref[...] = rounded
    band_zero = lax.axis_index("lag") == 0
    recent = [rounded] + [ref[...] for ref in olders]
    nxt = step + 1
    for slot, offset in enumerate(slot_offsets(lax.axis_index("patch"))):
        terms = stage[slot, nxt * shots : (nxt + 1) * shots, :].astype(jnp.float32)
        terms = terms + rest_far[slot * shots : (slot + 1) * shots, :].astype(jnp.float32)
        columns = pl.ds(pl.multiple_of(offset * tile_len, tile_len), tile_len)
        for k, block in enumerate(recent):
            lag = k + 1
            live = band_zero & (ranges[0, offset] <= lag) & (lag < ranges[0, NEAR + offset])
            scale = jnp.where(live, 1.0, 0.0).astype(jnp.float32)
            terms = terms + scale * dot(block, weights[k, :, columns])
        if slot < NEAR - 1:
            messages[slot][...] = terms.astype(jnp.bfloat16)
        else:
            next_own[...] = terms


def natural_kernel(*refs):
    blocks, out = refs[:-1], refs[-1]
    for k, block in enumerate(blocks):
        out[k] = block[...].astype(jnp.float32).T.astype(jnp.bfloat16)


def early_kernel(near_lags, mine, far, out, sem):
    def move(block):
        copy = pltpu.make_async_copy(block, out.at[pl.ds(0, block.shape[0])], sem)
        copy.start()
        copy.wait()

    keeps = lax.axis_index("lag") < near_lags
    pl.when(keeps)(lambda: move(mine))
    pl.when(jnp.logical_not(keeps))(lambda: move(far))


def late_kernel(near_lags, begun, mine, far, out, sem):
    del begun

    def move(block):
        copy = pltpu.make_async_copy(block, out.at[out.shape[0] - 1], sem)
        copy.start()
        copy.wait()

    keeps = lax.axis_index("lag") < near_lags
    pl.when(keeps)(lambda: move(mine))
    pl.when(jnp.logical_not(keeps))(lambda: move(far))


def call(kernel, outs, specs, scratch=(), out_specs=None, aliases=None, limit=8 << 20):
    made = []
    for shape, dtype, *space in outs:
        made.append(space[0](shape, dtype) if space else jax.ShapeDtypeStruct(shape, dtype))
    return pl.pallas_call(
        kernel,
        out_shape=made,
        in_specs=[pl.BlockSpec(memory_space=space) for space in specs],
        out_specs=[pl.BlockSpec(memory_space=s) for s in (out_specs or [VMEM] * len(made))],
        scratch_shapes=list(scratch),
        input_output_aliases=aliases or {},
        compiler_params=pltpu.CompilerParams(vmem_limit_bytes=limit),
    )


def near_memory(array):
    return pltpu.with_memory_space_constraint(array, VMEM)


def lag_partners(lags, distance):
    return [(i, i ^ distance) for i in range(lags)]


def lag_sum(block, lags):
    far, distance = None, 1
    while distance < lags:
        if far is not None:
            block = block + far.astype(block.dtype)
        far = lax.ppermute(block.astype(jnp.bfloat16), "lag", lag_partners(lags, distance))
        distance *= 2
    return block, far


def from_band_zero(block, lags):
    index = lax.axis_index("lag")
    distance = 1
    far = block
    while distance < lags:
        if distance > 1:
            block = jnp.where(index < distance // 2, block, far)
        far = lax.ppermute(block, "lag", lag_partners(lags, distance))
        distance *= 2
    return block, far


def local(interaction, history, near_inverse, lag_ranges, receiver_tile, receiver_panel, residuals):
    tile_len = near_inverse.shape[1]
    band, _, shots = history.shape
    recv, steps, _ = residuals.shape
    patches, lags = lax.axis_size("patch"), lax.axis_size("lag")
    width = steps * shots
    f32, bf16 = jnp.float32, jnp.bfloat16
    block = (shots, tile_len)
    routes = pairings(patches)

    rim = lax.ppermute(
        history[band - steps + 1 :], "lag", [(i, (i + 1) % lags) for i in range(lags)]
    )
    (outgoing,) = call(
        pack_kernel, [((patches * CAP, width + LANES), bf16)], [VMEM] * 3
    )(receiver_tile.reshape(1, recv), receiver_panel.reshape(1, recv), residuals.reshape(recv, width))
    arrived = lax.all_to_all(
        outgoing.reshape(patches, CAP, width + LANES),
        "patch",
        split_axis=0,
        concat_axis=0,
        tiled=True,
    ).reshape(patches * CAP, width + LANES)
    source = call(source_kernel, [(block, f32, VMEM)] * steps, [VMEM])(arrived)
    source = [near_memory(s) for s in source]

    sizes = sorted({-(-band // 4), -(-band // 2), band})
    older = call(
        functools.partial(older_kernel, steps, sizes),
        [(block, bf16)] * (NEAR - 1)
        + [
            (block, f32, VMEM),
            ((NEAR, width, tile_len), bf16, VMEM),
            ((steps - 1, tile_len, NEAR * tile_len), bf16, VMEM),
            ((tile_len, tile_len), bf16, VMEM),
        ]
        + [((NEAR * shots, tile_len), bf16)] * (steps - 1),
        [pltpu.SMEM, VMEM, VMEM, pltpu.HBM, pltpu.HBM],
        [
            VMEM(((band + steps - 1) * shots, tile_len), bf16),
            VMEM((NEAR, band, tile_len, tile_len), bf16),
            pltpu.SemaphoreType.DMA((NEAR, band)),
            pltpu.SemaphoreType.DMA((NEAR + 1, steps)),
        ],
        out_specs=[pl.ANY] * (NEAR - 1) + [VMEM] * 4 + [pl.ANY] * (steps - 1),
        limit=54 << 20,
    )(lag_ranges, rim, history, near_inverse, interaction)
    messages, (own, stage, recent, inverse), rest = older[: NEAR - 1], older[NEAR - 1 : NEAR + 3], older[NEAR + 3 :]
    stage, recent, inverse = near_memory(stage), near_memory(recent), near_memory(inverse)

    def exchange(blocks):
        gone = []
        for b, r in zip(blocks, routes):
            gone.append(lax.ppermute(b, "patch", r))
        return gone

    for incoming in exchange(messages):
        own = own + incoming.astype(f32)
    own, far = lag_sum(own, lags)
    received = [far]
    pairs = []
    for r in rest:
        pairs.append(lag_sum(r, lags))

    densities = []
    for step in range(steps):
        last_step = step == steps - 1
        inputs = [lag_ranges, source[step], inverse, own, *received]
        if last_step:
            outs = [((tile_len, shots), bf16)]
        else:
            here, there = pairs[step]
            if lags > 2:
                there = there + (here - rest[step])
            inputs += [recent, stage, there, *densities[::-1]]
            outs = [(block, bf16, VMEM), (block, f32, VMEM)] + [(block, bf16)] * (NEAR - 1)
        results = call(
            functools.partial(step_kernel, step, last_step),
            outs,
            [pltpu.SMEM] + [VMEM] * (len(inputs) - 1),
        )(*inputs)
        if not last_step:
            densities.append(near_memory(results[0]))
            own = near_memory(results[1])
            received = exchange(results[2:])
    (early,) = call(
        natural_kernel, [((steps - 1, tile_len, shots), bf16)], [VMEM] * (steps - 1)
    )(*densities)
    early = from_band_zero(early, lags)
    late = from_band_zero(results[0], lags)
    whole = ((steps, tile_len, shots), bf16)
    (begun,) = call(
        functools.partial(early_kernel, lags // 2),
        [whole],
        [pl.ANY] * 2,
        [pltpu.SemaphoreType.DMA],
        out_specs=[pl.ANY],
    )(*early)
    (out,) = call(
        functools.partial(late_kernel, lags // 2),
        [whole],
        [pl.ANY] * 3,
        [pltpu.SemaphoreType.DMA],
        out_specs=[pl.ANY],
        aliases={0: 0},
    )(begun, *late)
    return out


def solution(mesh):
    in_specs = (
        P("lag", "patch", None),
        P("lag", "patch", None),
        P("patch", None),
        P("patch", None),
        P("patch", None),
        P("patch"),
        P("patch", None, None),
    )
    out_specs = P(None, "patch", None)

    return jax.shard_map(local, mesh=mesh, in_specs=in_specs, out_specs=out_specs, check_vma=False)
```

profile of v0, /device:TPU:0, one launch (start us, length us, event | category | flops | bytes accessed | tf_op | source)
XLA Modules:
  0.0 98.2 jit_solution(9580711757276937494)
XLA Ops:
  0.0 1.0 %copy.11 = bf16[32,8,4,128]{3,1,2,0:T(8,128)(2,1)S(1)} copy(bf16[32,8,4,128]{3,2,1,0:T(4,128)(2,1)} %bitcast.11) | data formatting | bytes 524288
  2.4 1.1 %shard_map.73 = bf16[256,640]{1,0:T(8,128)(2,1)} custom-call(s32[1,256]{1,0:T(1,128)S(1)} %bitcast.9, s32[1,256]{1,0:T(1,128)S(1)} %bitcast.10, bf16[256,512]{1,0:T(8,128)(2,1)S(1)} %bitcast.8), custom_call_target="tpu_custom_call" | custom-call | tf_op jit(solution)/shard_map/pallas_call | solution.py:308
  3.5 7.5 %all-to-all-start = ((bf16[16,16,640]{2,1,0:T(8,128)(2,1)}), bf16[16,16,640]{2,1,0:T(8,128)(2,1)}, u32[]{:S(2)}, u32[]{:S(2)}) async-start(bf16[16,16,640]{2,1,0:T(8,128)(2,1)} %bitcast.2), calls=%async_computation | async-start | bytes 655360 | tf_op jit(solution)/shard_map/all_to_all | solution.py:311
  10.9 0.9 slice.3
  11.9 1.6 %collective-permute-start = (bf16[3,256,128]{2,1,0:T(8,128)(2,1)S(1)}, bf16[3,256,128]{2,1,0:T(8,128)(2,1)S(1)}, u32[]{:S(2)}, u32[]{:S(2)}) collective-permute-start(bf16[3,256,128]{2,1,0:T(8,128)(2,1)S(1)} %slice.3), channel_id=1, source_target_pairs={{0,1},{1,0},{2,3},{3,2},{4,5},{5,4},{6,7},{7,6},{8,9},{9,8},{10,11... | collective-permute-start | bytes 589832 | tf_op jit(solution)/shard_map/ppermute | solution.py:305
  13.4 5.7 %collective-permute-done.rim = bf16[3,256,128]{2,1,0:T(8,128)(2,1)S(1)} collective-permute-done((bf16[3,256,128]{2,1,0:T(8,128)(2,1)S(1)}, bf16[3,256,128]{2,1,0:T(8,128)(2,1)S(1)}, u32[]{:S(2)}, u32[]{:S(2)}) %collective-permute-start) | collective-permute-done | bytes 196640 | tf_op jit(solution)/shard_map/ppermute | solution.py:305
  19.8 10.1 %shard_map.75 = (bf16[128,256]{1,0:T(8,128)(2,1)}, bf16[128,256]{1,0:T(8,128)(2,1)}, bf16[128,256]{1,0:T(8,128)(2,1)}, bf16[128,256]{1,0:T(8,128)(2,1)}, f32[128...) custom-call(s32[1,10]{1,0:T(1,128)} %ranges.9, ...), custom_call_target="tpu_custom_call" | custom-call | tf_op jit(solution)/shard_map/pallas_call | solution.py:322
  29.9 3.4 %collective-permute-start.1 = (bf16[128,256]{1,0:T(8,128)(2,1)}, bf16[128,256]{1,0:T(8,128)(2,1)S(1)}, u32[]{:S(2)}, u32[]{:S(2)}) collective-permute-start(bf16[128,256]{1,0:T(8,128)(2,1)} %get-tuple-element.41), channel_id=1, source_target_pairs={{0,28},{2,30},{4,8},{6,10},{8,4},{10,6},{12,16},{14,18},{16,12},{1... | collective-permute-start | bytes 196616 | tf_op jit(solution)/shard_map/ppermute | solution.py:348
  33.9 1.4 %collective-permute-start.6 = (bf16[640,256]{1,0:T(8,128)(2,1)}, bf16[640,256]{1,0:T(8,128)(2,1)}, u32[]{:S(2)}, u32[]{:S(2)}) collective-permute-start(bf16[640,256]{1,0:T(8,128)(2,1)} %get-tuple-element.47), channel_id=1, source_target_pairs={{0,1},{1,0},{2,3},{3,2},{4,5},{5,4},{6,7},{7,6},{8,9},{9,8},{10,11... | collective-permute-start | bytes 983048 | tf_op jit(solution)/shard_map/ppermute | solution.py:278
  35.3 1.9 %collective-permute-done.1 = bf16[128,256]{1,0:T(8,128)(2,1)S(1)} collective-permute-done((bf16[128,256]{1,0:T(8,128)(2,1)}, bf16[128,256]{1,0:T(8,128)(2,1)S(1)}, u32[]{:S(2)}, u32[]{:S(2)}) %collective-permute-start.1) | collective-permute-done | bytes 65568 | tf_op jit(solution)/shard_map/ppermute | solution.py:348
  37.2 2.7 %collective-permute-done.2 = bf16[128,256]{1,0:T(8,128)(2,1)S(1)} collective-permute-done((bf16[128,256]{1,0:T(8,128)(2,1)}, bf16[128,256]{1,0:T(8,128)(2,1)S(1)}, u32[]{:S(2)}, u32[]{:S(2)}) %collective-permute-start.2) | collective-permute-done | bytes 65568 | tf_op jit(solution)/shard_map/ppermute | solution.py:348
  40.5 2.0 %collective-permute-start.5 = (bf16[128,256]{1,0:T(8,128)(2,1)}, bf16[128,256]{1,0:T(8,128)(2,1)}, u32[]{:S(2)}, u32[]{:S(2)}) collective-permute-start(bf16[128,256]{1,0:T(8,128)(2,1)} %get-tuple-element.71), channel_id=1, source_target_pairs={{0,1},{1,0},{2,3},{3,2},{4,5},{5,4},{6,7},{7,6},{8,9},{9,8},{10,11... | collective-permute-start | bytes 196616 | tf_op jit(solution)/shard_map/ppermute | solution.py:278
  42.6 1.2 %shard_map.74 = (f32[128,256]{1,0:T(8,128)S(1)}, f32[128,256]{1,0:T(8,128)S(1)}, f32[128,256]{1,0:T(8,128)S(1)}, f32[128,256]{1,0:T(8,128)S(1)}) custom-call(bf16[256,640]{1,0:T(8,128)(2,1)} %bitcast.3.arrived_ref), custom_call_target="tpu_custom_call" | custom-call | tf_op jit(solution)/shard_map/pallas_call | solution.py:318
  43.8 15.9 %collective-permute-done.5.refs_0_ = bf16[128,256]{1,0:T(8,128)(2,1)} collective-permute-done((bf16[128,256]{1,0:T(8,128)(2,1)}, bf16[128,256]{1,0:T(8,128)(2,1)}, u32[]{:S(2)}, u32[]{:S(2)}) %collective-permute-start.5) | collective-permute-done | bytes 65568 | tf_op jit(solution)/shard_map/ppermute | solution.py:278
  59.7 1.4 %shard_map.76 = (bf16[128,256]{1,0:T(8,128)(2,1)S(1)}, f32[128,256]{1,0:T(8,128)S(1)}, bf16[128,256]{1,0:T(8,128)(2,1)S(1)}, bf16[128,256]{1,0:T(8,128)(2,1)S(1)...) custom-call(s32[1,10]{1,0:T(1,128)S(1)} %copy-done, f32[128,256]{1,0:T(8,128)S(1)} %get-tuple-element.38.source, ...), custom_call_target="tpu_custom_call" | custom-call | tf_op jit(solution)/shard_map/pallas_call | solution.py:371
  61.1 3.9 %collective-permute-start.7 = (bf16[128,256]{1,0:T(8,128)(2,1)S(1)}, bf16[128,256]{1,0:T(8,128)(2,1)S(1)}, u32[]{:S(2)}, u32[]{:S(2)}) collective-permute-start(bf16[128,256]{1,0:T(8,128)(2,1)S(1)} %get-tuple-element.51), channel_id=1, source_target_pairs={{0,28},{2,30},{4,8},{6,10},{8,4},{10,6},{12,16},{14,18},{16,12},{1... | collective-permute-start | bytes 196616 | tf_op jit(solution)/shard_map/ppermute | solution.py:348
  65.5 2.8 %collective-permute-done.7.refs_0_ = bf16[128,256]{1,0:T(8,128)(2,1)S(1)} collective-permute-done((bf16[128,256]{1,0:T(8,128)(2,1)S(1)}, bf16[128,256]{1,0:T(8,128)(2,1)S(1)}, u32[]{:S(2)}, u32[]{:S(2)}) %collective-permute-start.7) | collective-permute-done | bytes 65568 | tf_op jit(solution)/shard_map/ppermute | solution.py:348
  68.2 3.1 %collective-permute-done.8.refs_1_ = bf16[128,256]{1,0:T(8,128)(2,1)S(1)} collective-permute-done((bf16[128,256]{1,0:T(8,128)(2,1)S(1)}, bf16[128,256]{1,0:T(8,128)(2,1)S(1)}, u32[]{:S(2)}, u32[]{:S(2)}) %collective-permute-start.8) | collective-permute-done | bytes 65568 | tf_op jit(solution)/shard_map/ppermute | solution.py:348
  71.4 1.5 %shard_map.77 = (bf16[128,256]{1,0:T(8,128)(2,1)S(1)}, f32[128,256]{1,0:T(8,128)S(1)}, bf16[128,256]{1,0:T(8,128)(2,1)S(1)}, bf16[128,256]{1,0:T(8,128)(2,1)S(1)...) custom-call(s32[1,10]{1,0:T(1,128)S(1)} %copy-done, f32[128,256]{1,0:T(8,128)S(1)} %get-tuple-element.49.source, ...), custom_call_target="tpu_custom_call" | custom-call | tf_op jit(solution)/shard_map/pallas_call | solution.py:371
  73.5 0.9 collective-permute-start.13
  74.4 1.7 %collective-permute-start.14 = (bf16[128,256]{1,0:T(8,128)(2,1)S(1)}, bf16[128,256]{1,0:T(8,128)(2,1)S(1)}, u32[]{:S(2)}, u32[]{:S(2)}) collective-permute-start(bf16[128,256]{1,0:T(8,128)(2,1)S(1)} %get-tuple-element.61), channel_id=1, source_target_pairs={{0,4},{2,6},{4,0},{6,2},{8,12},{10,14},{12,8},{14,10},{16,20},{18,... | collective-permute-start | bytes 196616 | tf_op jit(solution)/shard_map/ppermute | solution.py:348
  76.0 4.5 %collective-permute-done.12.refs_0_ = bf16[128,256]{1,0:T(8,128)(2,1)S(1)} collective-permute-done((bf16[128,256]{1,0:T(8,128)(2,1)S(1)}, bf16[128,256]{1,0:T(8,128)(2,1)S(1)}, u32[]{:S(2)}, u32[]{:S(2)}) %collective-permute-start.12) | collective-permute-done | bytes 65568 | tf_op jit(solution)/shard_map/ppermute | solution.py:348
  80.6 1.6 %shard_map.78 = (bf16[128,256]{1,0:T(8,128)(2,1)S(1)}, f32[128,256]{1,0:T(8,128)S(1)}, bf16[128,256]{1,0:T(8,128)(2,1)S(1)}, bf16[128,256]{1,0:T(8,128)(2,1)S(1)...) custom-call(s32[1,10]{1,0:T(1,128)S(1)} %copy-done, f32[128,256]{1,0:T(8,128)S(1)} %get-tuple-element.57.source, ...), custom_call_target="tpu_custom_call" | custom-call | tf_op jit(solution)/shard_map/pallas_call | solution.py:371
  82.3 1.0 %collective-permute-start.17 = (bf16[3,256,128]{2,1,0:T(8,128)(2,1)S(1)}, bf16[3,256,128]{2,1,0:T(8,128)(2,1)S(1)}, u32[]{:S(2)}, u32[]{:S(2)}) collective-permute-start(bf16[3,256,128]{2,1,0:T(8,128)(2,1)S(1)} %shard_map.79.mine), channel_id=1, source_target_pairs={{0,1},{1,0},{2,3},{3,2},{4,5},{5,4},{6,7},{7,6},{8,9},{9,8},{10,11... | collective-permute-start | bytes 589832 | tf_op jit(solution)/shard_map/ppermute | solution.py:290
  83.3 2.8 %collective-permute-start.18 = (bf16[128,256]{1,0:T(8,128)(2,1)S(1)}, bf16[128,256]{1,0:T(8,128)(2,1)S(1)}, u32[]{:S(2)}, u32[]{:S(2)}) collective-permute-start(bf16[128,256]{1,0:T(8,128)(2,1)S(1)} %get-tuple-element.67), channel_id=1, source_target_pairs={{0,28},{2,30},{4,8},{6,10},{8,4},{10,6},{12,16},{14,18},{16,12},{1... | collective-permute-start | bytes 196616 | tf_op jit(solution)/shard_map/ppermute | solution.py:348
  86.0 1.5 %collective-permute-start.20 = (bf16[128,256]{1,0:T(8,128)(2,1)S(1)}, bf16[128,256]{1,0:T(8,128)(2,1)S(1)}, u32[]{:S(2)}, u32[]{:S(2)}) collective-permute-start(bf16[128,256]{1,0:T(8,128)(2,1)S(1)} %get-tuple-element.69), channel_id=1, source_target_pairs={{0,4},{2,6},{4,0},{6,2},{8,12},{10,14},{12,8},{14,10},{16,20},{18,... | collective-permute-start | bytes 196616 | tf_op jit(solution)/shard_map/ppermute | solution.py:348
  87.6 2.7 %collective-permute-done.18.refs_0_ = bf16[128,256]{1,0:T(8,128)(2,1)S(1)} collective-permute-done((bf16[128,256]{1,0:T(8,128)(2,1)S(1)}, bf16[128,256]{1,0:T(8,128)(2,1)S(1)}, u32[]{:S(2)}, u32[]{:S(2)}) %collective-permute-start.18) | collective-permute-done | bytes 65568 | tf_op jit(solution)/shard_map/ppermute | solution.py:348
  90.3 2.1 %collective-permute-done.19.refs_1_ = bf16[128,256]{1,0:T(8,128)(2,1)S(1)} collective-permute-done((bf16[128,256]{1,0:T(8,128)(2,1)S(1)}, bf16[128,256]{1,0:T(8,128)(2,1)S(1)}, u32[]{:S(2)}, u32[]{:S(2)}) %collective-permute-start.19) | collective-permute-done | bytes 65568 | tf_op jit(solution)/shard_map/ppermute | solution.py:348
  92.4 0.8 shard_map.81.mine
  93.2 1.1 %collective-permute-start.22 = (bf16[256,128]{1,0:T(8,128)(2,1)S(1)}, bf16[256,128]{1,0:T(8,128)(2,1)S(1)}, u32[]{:S(2)}, u32[]{:S(2)}) collective-permute-start(bf16[256,128]{1,0:T(8,128)(2,1)S(1)} %shard_map.81.mine), channel_id=1, source_target_pairs={{0,1},{1,0},{2,3},{3,2},{4,5},{5,4},{6,7},{7,6},{8,9},{9,8},{10,11... | collective-permute-start | bytes 196616 | tf_op jit(solution)/shard_map/ppermute | solution.py:290
  94.4 0.7 shard_map.80.begun
  95.1 2.5 %collective-permute-done.22.far = bf16[256,128]{1,0:T(8,128)(2,1)S(1)} collective-permute-done((bf16[256,128]{1,0:T(8,128)(2,1)S(1)}, bf16[256,128]{1,0:T(8,128)(2,1)S(1)}, u32[]{:S(2)}, u32[]{:S(2)}) %collective-permute-start.22) | collective-permute-done | bytes 65568 | tf_op jit(solution)/shard_map/ppermute | solution.py:290
  (37 shorter events, 5.3 us)
Async XLA Ops:
  1.0 0.7 copy-start.1
  1.7 0.7 copy-start.2
  3.5 39.1 %all-to-all-start = ((bf16[16,16,640]{2,1,0:T(8,128)(2,1)}), bf16[16,16,640]{2,1,0:T(8,128)(2,1)}, u32[]{:S(2)}, u32[]{:S(2)}) async-start(bf16[16,16,640]{2,1,0:T(8,128)(2,1)} %bitcast.2), calls=%async_computation | async-start | bytes 655360 | tf_op jit(solution)/shard_map/all_to_all | solution.py:311
  11.9 47.8 %copy-start = (s32[1,10]{1,0:T(1,128)S(1)}, s32[1,10]{1,0:T(1,128)}, u32[]{:S(2)}) copy-start(s32[1,10]{1,0:T(1,128)} %ranges.9) | copy-start | bytes 124
  11.9 7.2 %collective-permute-start = (bf16[3,256,128]{2,1,0:T(8,128)(2,1)S(1)}, bf16[3,256,128]{2,1,0:T(8,128)(2,1)S(1)}, u32[]{:S(2)}, u32[]{:S(2)}) collective-permute-start(bf16[3,256,128]{2,1,0:T(8,128)(2,1)S(1)} %slice.3), channel_id=1, source_target_pairs={{0,1},{1,0},{2,3},{3,2},{4,5},{5,4},{6,7},{7,6},{8,9},{9,8},{10,11... | collective-permute-start | bytes 589832 | tf_op jit(solution)/shard_map/ppermute | solution.py:305
  19.1 0.7 copy-start.3
  29.9 7.3 %collective-permute-start.1 = (bf16[128,256]{1,0:T(8,128)(2,1)}, bf16[128,256]{1,0:T(8,128)(2,1)S(1)}, u32[]{:S(2)}, u32[]{:S(2)}) collective-permute-start(bf16[128,256]{1,0:T(8,128)(2,1)} %get-tuple-element.41), channel_id=1, source_target_pairs={{0,28},{2,30},{4,8},{6,10},{8,4},{10,6},{12,16},{14,18},{16,12},{1... | collective-permute-start | bytes 196616 | tf_op jit(solution)/shard_map/ppermute | solution.py:348
  33.3 6.6 %collective-permute-start.2 = (bf16[128,256]{1,0:T(8,128)(2,1)}, bf16[128,256]{1,0:T(8,128)(2,1)S(1)}, u32[]{:S(2)}, u32[]{:S(2)}) collective-permute-start(bf16[128,256]{1,0:T(8,128)(2,1)} %get-tuple-element.42), channel_id=1, source_target_pairs={{0,30},{2,4},{4,2},{6,8},{8,6},{10,12},{12,10},{14,16},{16,14},{18... | collective-permute-start | bytes 196616 | tf_op jit(solution)/shard_map/ppermute | solution.py:348
  33.3 6.6 %collective-permute-start.3 = (bf16[128,256]{1,0:T(8,128)(2,1)}, bf16[128,256]{1,0:T(8,128)(2,1)S(1)}, u32[]{:S(2)}, u32[]{:S(2)}) collective-permute-start(bf16[128,256]{1,0:T(8,128)(2,1)} %get-tuple-element.43), channel_id=1, source_target_pairs={{0,4},{2,6},{4,0},{6,2},{8,12},{10,14},{12,8},{14,10},{16,20},{18,... | collective-permute-start | bytes 196616 | tf_op jit(solution)/shard_map/ppermute | solution.py:348
  33.8 6.1 %collective-permute-start.4 = (bf16[128,256]{1,0:T(8,128)(2,1)}, bf16[128,256]{1,0:T(8,128)(2,1)S(1)}, u32[]{:S(2)}, u32[]{:S(2)}) collective-permute-start(bf16[128,256]{1,0:T(8,128)(2,1)} %get-tuple-element.44), channel_id=1, source_target_pairs={{0,2},{2,0},{4,6},{6,4},{8,10},{10,8},{12,14},{14,12},{16,18},{18,... | collective-permute-start | bytes 196616 | tf_op jit(solution)/shard_map/ppermute | solution.py:348
  33.9 25.8 %collective-permute-start.6 = (bf16[640,256]{1,0:T(8,128)(2,1)}, bf16[640,256]{1,0:T(8,128)(2,1)}, u32[]{:S(2)}, u32[]{:S(2)}) collective-permute-start(bf16[640,256]{1,0:T(8,128)(2,1)} %get-tuple-element.47), channel_id=1, source_target_pairs={{0,1},{1,0},{2,3},{3,2},{4,5},{5,4},{6,7},{7,6},{8,9},{9,8},{10,11... | collective-permute-start | bytes 983048 | tf_op jit(solution)/shard_map/ppermute | solution.py:278
  37.2 28.3 %collective-permute-start.11 = (bf16[640,256]{1,0:T(8,128)(2,1)}, bf16[640,256]{1,0:T(8,128)(2,1)}, u32[]{:S(2)}, u32[]{:S(2)}) collective-permute-start(bf16[640,256]{1,0:T(8,128)(2,1)} %get-tuple-element.55), channel_id=1, source_target_pairs={{0,1},{1,0},{2,3},{3,2},{4,5},{5,4},{6,7},{7,6},{8,9},{9,8},{10,11... | collective-permute-start | bytes 983048 | tf_op jit(solution)/shard_map/ppermute | solution.py:278
  39.9 36.2 %collective-permute-start.16 = (bf16[640,256]{1,0:T(8,128)(2,1)}, bf16[640,256]{1,0:T(8,128)(2,1)}, u32[]{:S(2)}, u32[]{:S(2)}) collective-permute-start(bf16[640,256]{1,0:T(8,128)(2,1)} %get-tuple-element.63), channel_id=1, source_target_pairs={{0,1},{1,0},{2,3},{3,2},{4,5},{5,4},{6,7},{7,6},{8,9},{9,8},{10,11... | collective-permute-start | bytes 983048 | tf_op jit(solution)/shard_map/ppermute | solution.py:278
  40.5 19.1 %collective-permute-start.5 = (bf16[128,256]{1,0:T(8,128)(2,1)}, bf16[128,256]{1,0:T(8,128)(2,1)}, u32[]{:S(2)}, u32[]{:S(2)}) collective-permute-start(bf16[128,256]{1,0:T(8,128)(2,1)} %get-tuple-element.71), channel_id=1, source_target_pairs={{0,1},{1,0},{2,3},{3,2},{4,5},{5,4},{6,7},{7,6},{8,9},{9,8},{10,11... | collective-permute-start | bytes 196616 | tf_op jit(solution)/shard_map/ppermute | solution.py:278
  61.1 7.1 %collective-permute-start.7 = (bf16[128,256]{1,0:T(8,128)(2,1)S(1)}, bf16[128,256]{1,0:T(8,128)(2,1)S(1)}, u32[]{:S(2)}, u32[]{:S(2)}) collective-permute-start(bf16[128,256]{1,0:T(8,128)(2,1)S(1)} %get-tuple-element.51), channel_id=1, source_target_pairs={{0,28},{2,30},{4,8},{6,10},{8,4},{10,6},{12,16},{14,18},{16,12},{1... | collective-permute-start | bytes 196616 | tf_op jit(solution)/shard_map/ppermute | solution.py:348
  65.0 6.4 %collective-permute-start.8 = (bf16[128,256]{1,0:T(8,128)(2,1)S(1)}, bf16[128,256]{1,0:T(8,128)(2,1)S(1)}, u32[]{:S(2)}, u32[]{:S(2)}) collective-permute-start(bf16[128,256]{1,0:T(8,128)(2,1)S(1)} %get-tuple-element.52), channel_id=1, source_target_pairs={{0,30},{2,4},{4,2},{6,8},{8,6},{10,12},{12,10},{14,16},{16,14},{18... | collective-permute-start | bytes 196616 | tf_op jit(solution)/shard_map/ppermute | solution.py:348
  65.0 6.4 %collective-permute-start.9 = (bf16[128,256]{1,0:T(8,128)(2,1)S(1)}, bf16[128,256]{1,0:T(8,128)(2,1)S(1)}, u32[]{:S(2)}, u32[]{:S(2)}) collective-permute-start(bf16[128,256]{1,0:T(8,128)(2,1)S(1)} %get-tuple-element.53), channel_id=1, source_target_pairs={{0,4},{2,6},{4,0},{6,2},{8,12},{10,14},{12,8},{14,10},{16,20},{18,... | collective-permute-start | bytes 196616 | tf_op jit(solution)/shard_map/ppermute | solution.py:348
  65.5 5.9 %collective-permute-start.10 = (bf16[128,256]{1,0:T(8,128)(2,1)S(1)}, bf16[128,256]{1,0:T(8,128)(2,1)S(1)}, u32[]{:S(2)}, u32[]{:S(2)}) collective-permute-start(bf16[128,256]{1,0:T(8,128)(2,1)S(1)} %get-tuple-element.54), channel_id=1, source_target_pairs={{0,2},{2,0},{4,6},{6,4},{8,10},{10,8},{12,14},{14,12},{16,18},{18,... | collective-permute-start | bytes 196616 | tf_op jit(solution)/shard_map/ppermute | solution.py:348
  72.8 7.7 %collective-permute-start.12 = (bf16[128,256]{1,0:T(8,128)(2,1)S(1)}, bf16[128,256]{1,0:T(8,128)(2,1)S(1)}, u32[]{:S(2)}, u32[]{:S(2)}) collective-permute-start(bf16[128,256]{1,0:T(8,128)(2,1)S(1)} %get-tuple-element.59), channel_id=1, source_target_pairs={{0,28},{2,30},{4,8},{6,10},{8,4},{10,6},{12,16},{14,18},{16,12},{1... | collective-permute-start | bytes 196616 | tf_op jit(solution)/shard_map/ppermute | solution.py:348
  73.5 7.1 %collective-permute-start.13 = (bf16[128,256]{1,0:T(8,128)(2,1)S(1)}, bf16[128,256]{1,0:T(8,128)(2,1)S(1)}, u32[]{:S(2)}, u32[]{:S(2)}) collective-permute-start(bf16[128,256]{1,0:T(8,128)(2,1)S(1)} %get-tuple-element.60), channel_id=1, source_target_pairs={{0,30},{2,4},{4,2},{6,8},{8,6},{10,12},{12,10},{14,16},{16,14},{18... | collective-permute-start | bytes 196616 | tf_op jit(solution)/shard_map/ppermute | solution.py:348
  74.4 6.2 %collective-permute-start.14 = (bf16[128,256]{1,0:T(8,128)(2,1)S(1)}, bf16[128,256]{1,0:T(8,128)(2,1)S(1)}, u32[]{:S(2)}, u32[]{:S(2)}) collective-permute-start(bf16[128,256]{1,0:T(8,128)(2,1)S(1)} %get-tuple-element.61), channel_id=1, source_target_pairs={{0,4},{2,6},{4,0},{6,2},{8,12},{10,14},{12,8},{14,10},{16,20},{18,... | collective-permute-start | bytes 196616 | tf_op jit(solution)/shard_map/ppermute | solution.py:348
  76.0 4.5 %collective-permute-start.15 = (bf16[128,256]{1,0:T(8,128)(2,1)S(1)}, bf16[128,256]{1,0:T(8,128)(2,1)S(1)}, u32[]{:S(2)}, u32[]{:S(2)}) collective-permute-start(bf16[128,256]{1,0:T(8,128)(2,1)S(1)} %get-tuple-element.62), channel_id=1, source_target_pairs={{0,2},{2,0},{4,6},{6,4},{8,10},{10,8},{12,14},{14,12},{16,18},{18,... | collective-permute-start | bytes 196616 | tf_op jit(solution)/shard_map/ppermute | solution.py:348
  82.3 12.1 %collective-permute-start.17 = (bf16[3,256,128]{2,1,0:T(8,128)(2,1)S(1)}, bf16[3,256,128]{2,1,0:T(8,128)(2,1)S(1)}, u32[]{:S(2)}, u32[]{:S(2)}) collective-permute-start(bf16[3,256,128]{2,1,0:T(8,128)(2,1)S(1)} %shard_map.79.mine), channel_id=1, source_target_pairs={{0,1},{1,0},{2,3},{3,2},{4,5},{5,4},{6,7},{7,6},{8,9},{9,8},{10,11... | collective-permute-start | bytes 589832 | tf_op jit(solution)/shard_map/ppermute | solution.py:290
  83.3 7.1 %collective-permute-start.18 = (bf16[128,256]{1,0:T(8,128)(2,1)S(1)}, bf16[128,256]{1,0:T(8,128)(2,1)S(1)}, u32[]{:S(2)}, u32[]{:S(2)}) collective-permute-start(bf16[128,256]{1,0:T(8,128)(2,1)S(1)} %get-tuple-element.67), channel_id=1, source_target_pairs={{0,28},{2,30},{4,8},{6,10},{8,4},{10,6},{12,16},{14,18},{16,12},{1... | collective-permute-start | bytes 196616 | tf_op jit(solution)/shard_map/ppermute | solution.py:348
  86.0 6.4 %collective-permute-start.19 = (bf16[128,256]{1,0:T(8,128)(2,1)S(1)}, bf16[128,256]{1,0:T(8,128)(2,1)S(1)}, u32[]{:S(2)}, u32[]{:S(2)}) collective-permute-start(bf16[128,256]{1,0:T(8,128)(2,1)S(1)} %get-tuple-element.68), channel_id=1, source_target_pairs={{0,30},{2,4},{4,2},{6,8},{8,6},{10,12},{12,10},{14,16},{16,14},{18... | collective-permute-start | bytes 196616 | tf_op jit(solution)/shard_map/ppermute | solution.py:348
  86.0 6.4 %collective-permute-start.20 = (bf16[128,256]{1,0:T(8,128)(2,1)S(1)}, bf16[128,256]{1,0:T(8,128)(2,1)S(1)}, u32[]{:S(2)}, u32[]{:S(2)}) collective-permute-start(bf16[128,256]{1,0:T(8,128)(2,1)S(1)} %get-tuple-element.69), channel_id=1, source_target_pairs={{0,4},{2,6},{4,0},{6,2},{8,12},{10,14},{12,8},{14,10},{16,20},{18,... | collective-permute-start | bytes 196616 | tf_op jit(solution)/shard_map/ppermute | solution.py:348
  87.6 4.8 %collective-permute-start.21 = (bf16[128,256]{1,0:T(8,128)(2,1)S(1)}, bf16[128,256]{1,0:T(8,128)(2,1)S(1)}, u32[]{:S(2)}, u32[]{:S(2)}) collective-permute-start(bf16[128,256]{1,0:T(8,128)(2,1)S(1)} %get-tuple-element.70), channel_id=1, source_target_pairs={{0,2},{2,0},{4,6},{6,4},{8,10},{10,8},{12,14},{14,12},{16,18},{18,... | collective-permute-start | bytes 196616 | tf_op jit(solution)/shard_map/ppermute | solution.py:348
  93.2 4.3 %collective-permute-start.22 = (bf16[256,128]{1,0:T(8,128)(2,1)S(1)}, bf16[256,128]{1,0:T(8,128)(2,1)S(1)}, u32[]{:S(2)}, u32[]{:S(2)}) collective-permute-start(bf16[256,128]{1,0:T(8,128)(2,1)S(1)} %shard_map.81.mine), channel_id=1, source_target_pairs={{0,1},{1,0},{2,3},{3,2},{4,5},{5,4},{6,7},{7,6},{8,9},{9,8},{10,11... | collective-permute-start | bytes 196616 | tf_op jit(solution)/shard_map/ppermute | solution.py:290
where the time goes:
time: 98.7 us; the launch traced here: 98.2 us
  waiting for transfers between devices  43.9 us (44%)
  starting transfers between devices  30.4 us (31%)
  Pallas kernels  19.1 us (19%)
  local copies, waits for them, and re-layouts  3.97 us (4%)
    ppermute x16, waiting for transfers between devices, exchange(): gone.append(lax.ppermute(b, 'patch', r))  19.8 us
    ppermute x16, starting transfers between devices, exchange(): gone.append(lax.ppermute(b, 'patch', r))  15.9 us
    ppermute x4, waiting for transfers between devices, lag_sum(): lax.ppermute(block.astype(jnp.bfloat16), 'lag', lag_partners(lags, distan...  15.9 us
    pallas_call x1, Pallas kernels, local(): call(functools.partial(older_kernel, steps, sizes), [(block, bf16)] * (NE...  10.1 us
    all_to_all x1, starting transfers between devices, local(): lax.all_to_all(outgoing.reshape(patches, CAP, width + LANES), 'patch', sp...  7.46 us
    ppermute x1, waiting for transfers between devices, local(): lax.ppermute(history[band - steps + 1:], 'lag', [(i, (i + 1) % lags) for...  5.68 us
    pallas_call x4, Pallas kernels, local(): call(functools.partial(step_kernel, step, last_step), outs, [pltpu.SMEM]...  5.22 us
    ppermute x4, starting transfers between devices, lag_sum(): lax.ppermute(block.astype(jnp.bfloat16), 'lag', lag_partners(lags, distan...  3.39 us
  transfers between devices with their start and end apart: 24, of which 10 were waited for; matrix products, arithmetic and copies ran while one was open for 2% of the time, Pallas kernels for 16%

commit v1 on v0

--- a/solution.py
+++ b/solution.py
@@ -12,6 +12,8 @@
 HALF = NEAR // 2
 LANES = 128
 VMEM = pltpu.VMEM
+PREPARE_LIMIT = 97 << 19
+OLDER_LIMIT = 97 << 19
 
 
 def dot(left, right):
@@ -32,10 +34,17 @@
     return [list(enumerate(p)) for p in (far, odd_even, near, core)]
 
 
-def pack_kernel(tile_ref, panel_ref, rows_ref, out_ref):
+def active(ranges, offset, lag, band):
+    base = lag * band + 1
+    first = jnp.clip(ranges[0, offset] - base, 0, band)
+    last = jnp.clip(ranges[0, NEAR + offset] - base, 0, band)
+    return first, last
+
+
+def pack(tile_ref, panel_ref, rows_ref, out_ref):
     recv = rows_ref.shape[0]
-    width = rows_ref.shape[1]
-    slots = out_ref.shape[0]
+    slots, width = out_ref.shape
+    width = width - LANES
     patches = slots // CAP
     tile = tile_ref[...]
     hot = lax.broadcasted_iota(jnp.int32, (patches, recv), 0) == tile
@@ -48,16 +57,47 @@
     slot = tile * CAP + earlier
     placed = lax.broadcasted_iota(jnp.int32, (slots, recv), 0) == slot
     placer = jnp.where(placed, 1.0, 0.0).astype(jnp.bfloat16)
-    out_ref[:, :width] = dot(placer, rows_ref[...]).astype(jnp.bfloat16)
+    piece = lax.rem(lax.axis_index("lag"), rows_ref.shape[1] // width)
+    rows = rows_ref[:, pl.ds(pl.multiple_of(piece * width, width), width)]
+    out_ref[:, :width] = dot(placer, rows).astype(jnp.bfloat16)
     marks = jnp.where(placed, (panel_ref[...] + 1).astype(jnp.float32), 0.0)
     label = jnp.sum(marks, axis=1, keepdims=True)
     out_ref[:, width:] = jnp.broadcast_to(label, (slots, LANES)).astype(jnp.bfloat16)
 
 
-def source_kernel(arrived_ref, *outs):
+def prepare_kernel(ranges, tile, panel, residuals, history, inverse, weights, *refs):
+    outgoing, blocks, near_history, recent, near_inverse, sems, keep_sems = refs
+    _, band, tile_len, _ = blocks.shape
+    lag = lax.axis_index("lag")
+
+    def fetch(slot, offset, k):
+        columns = pl.ds(pl.multiple_of(offset * tile_len, tile_len), tile_len)
+        return pltpu.make_async_copy(
+            weights.at[k, :, columns], blocks.at[slot, k], sems.at[slot, k]
+        )
+
+    offsets = slot_offsets(lax.axis_index("patch"))
+    for slot, offset in enumerate(offsets):
+        first, last = active(ranges, offset, lag, band)
+        lax.fori_loop(first, last, lambda k, c, s=slot, o=offset: fetch(s, o, k).start(), None)
+    keep = [
+        pltpu.make_async_copy(history, near_history, keep_sems.at[0]),
+        pltpu.make_async_copy(weights.at[pl.ds(0, recent.shape[0])], recent, keep_sems.at[1]),
+        pltpu.make_async_copy(inverse, near_inverse, keep_sems.at[2]),
+    ]
+    for copy in keep:
+        copy.start()
+    pack(tile, panel, residuals, outgoing)
+    for copy in keep:
+        copy.wait()
+    for slot, offset in enumerate(offsets):
+        first, last = active(ranges, offset, lag, band)
+        lax.fori_loop(first, last, lambda k, c, s=slot, o=offset: fetch(s, o, k).wait(), None)
+
+
+def source_kernel(shots, arrived_ref, out):
     slots = arrived_ref.shape[0]
-    shots, tile_len = outs[0].shape
-    width = len(outs) * shots
+    width, tile_len = out.shape
     label = arrived_ref[:, width:].astype(jnp.float32)
     lane = lax.broadcasted_iota(jnp.int32, (slots, LANES), 1)
     picker = jnp.concatenate(
@@ -67,50 +107,29 @@
         ],
         axis=1,
     ).astype(jnp.bfloat16)
-    for step, out in enumerate(outs):
-        out[...] = lax.dot_general(
-            arrived_ref[:, step * shots : (step + 1) * shots],
+    for first in range(0, width, shots):
+        out[first : first + shots, :] = lax.dot_general(
+            arrived_ref[:, first : first + shots],
             picker,
             (((0,), (0,)), ((), ())),
             preferred_element_type=jnp.float32,
         )
 
 
-def older_kernel(steps, sizes, ranges, rim, history, inverse_hbm, weights, *refs):
-    outs, (rows, blocks, sems, out_sems) = refs[:-4], refs[-4:]
+def older_kernel(steps, sizes, ranges, rim, history, blocks, *refs):
+    outs, (rows, out_sems) = refs[:-2], refs[-2:]
     messages, outs = outs[: NEAR - 1], outs[NEAR - 1 :]
-    own, stage, recent, inverse = outs[:4]
-    rest = outs[4:]
+    own, stage = outs[:2]
+    rest = outs[2:]
     band, tile_len, shots = history.shape
     lag = lax.axis_index("lag")
     offsets = slot_offsets(lax.axis_index("patch"))
-
-    def bounds(offset):
-        base = lag * band + 1
-        first = jnp.clip(ranges[0, offset] - base, 0, band)
-        last = jnp.clip(ranges[0, NEAR + offset] - base, 0, band)
-        return first, last
-
-    def fetch(slot, offset, k):
-        columns = pl.ds(pl.multiple_of(offset * tile_len, tile_len), tile_len)
-        return pltpu.make_async_copy(
-            weights.at[k, :, columns], blocks.at[slot, k], sems.at[slot, k]
-        )
 
     def send(slot, step, target):
         return pltpu.make_async_copy(
             stage.at[slot, pl.ds(step * shots, shots)], target, out_sems.at[slot, step]
         )
 
-    for slot, offset in enumerate(offsets):
-        first, last = bounds(offset)
-        lax.fori_loop(first, last, lambda k, c, s=slot, o=offset: fetch(s, o, k).start(), None)
-    keep = [
-        pltpu.make_async_copy(weights.at[pl.ds(0, steps - 1)], recent, out_sems.at[NEAR, 0]),
-        pltpu.make_async_copy(inverse_hbm, inverse, out_sems.at[NEAR, 1]),
-    ]
-    for copy in keep:
-        copy.start()
     for k in range(band):
         rows[(band - 1 - k) * shots : (band - k) * shots, :] = history[k].T
 
@@ -131,8 +150,7 @@
         offset = offsets[-1]
         for j in range(NEAR - 1):
             offset = jnp.where(slot == j, offsets[j], offset)
-        first, last = bounds(offset)
-        lax.fori_loop(first, last, lambda k, c: fetch(slot, offset, k).wait(), None)
+        first, last = active(ranges, offset, lag, band)
 
         def emit(total):
             stage[slot] = total.astype(jnp.bfloat16)
@@ -171,8 +189,6 @@
         return carry
 
     lax.fori_loop(0, NEAR, one_slot, None)
-    for copy in keep:
-        copy.wait()
     for slot in range(NEAR):
         if slot < NEAR - 1:
             send(slot, 0, messages[slot]).wait()
@@ -185,7 +201,8 @@
     tile_len = own.shape[1]
     refs = list(refs)
     received = [refs.pop(0) for _ in range(1 if step == 0 else NEAR - 1)]
-    right = source[...] - own[...]
+    at = step % (source.shape[0] // shots) * shots
+    right = source[at : at + shots, :] - own[...]
     for block in received:
         right = right - block[...].astype(jnp.float32)
     density = dot(right.astype(jnp.bfloat16), inverse[...])
@@ -305,42 +322,62 @@
     rim = lax.ppermute(
         history[band - steps + 1 :], "lag", [(i, (i + 1) % lags) for i in range(lags)]
     )
-    (outgoing,) = call(
-        pack_kernel, [((patches * CAP, width + LANES), bf16)], [VMEM] * 3
-    )(receiver_tile.reshape(1, recv), receiver_panel.reshape(1, recv), residuals.reshape(recv, width))
+    pieces = min(lags, steps)
+    piece = width // pieces
+    outgoing, blocks, near_history, recent, inverse = call(
+        prepare_kernel,
+        [
+            ((patches * CAP, piece + LANES), bf16),
+            ((NEAR, band, tile_len, tile_len), bf16, VMEM),
+            ((band, tile_len, shots), bf16, VMEM),
+            ((steps - 1, tile_len, NEAR * tile_len), bf16, VMEM),
+            ((tile_len, tile_len), bf16, VMEM),
+        ],
+        [pltpu.SMEM] + [VMEM] * 3 + [pltpu.HBM] * 3,
+        [pltpu.SemaphoreType.DMA((NEAR, band)), pltpu.SemaphoreType.DMA((3,))],
+        limit=PREPARE_LIMIT,
+    )(
+        lag_ranges,
+        receiver_tile.reshape(1, recv),
+        receiver_panel.reshape(1, recv),
+        residuals.reshape(recv, width),
+        history,
+        near_inverse,
+        interaction,
+    )
+    blocks, near_history = near_memory(blocks), near_memory(near_history)
+    recent, inverse = near_memory(recent), near_memory(inverse)
+
+    sizes = sorted({-(-band // 4), -(-band // 2), band})
+    older = call(
+        functools.partial(older_kernel, steps, sizes),
+        [(block, bf16)] * (NEAR - 1)
+        + [(block, f32), ((NEAR, width, tile_len), bf16, VMEM)]
+        + [((NEAR * shots, tile_len), bf16)] * (steps - 1),
+        [pltpu.SMEM] + [VMEM] * 3,
+        [
+            VMEM(((band + steps - 1) * shots, tile_len), bf16),
+            pltpu.SemaphoreType.DMA((NEAR, steps)),
+        ],
+        out_specs=[pl.ANY] * (NEAR - 1) + [VMEM] * 2 + [pl.ANY] * (steps - 1),
+        limit=OLDER_LIMIT,
+    )(lag_ranges, rim, near_history, blocks)
+    messages, (own, stage), rest = older[: NEAR - 1], older[NEAR - 1 : NEAR + 1], older[NEAR + 1 :]
+    stage = near_memory(stage)
+
     arrived = lax.all_to_all(
-        outgoing.reshape(patches, CAP, width + LANES),
+        outgoing.reshape(patches, CAP, piece + LANES),
         "patch",
         split_axis=0,
         concat_axis=0,
         tiled=True,
-    ).reshape(patches * CAP, width + LANES)
-    source = call(source_kernel, [(block, f32, VMEM)] * steps, [VMEM])(arrived)
-    source = [near_memory(s) for s in source]
-
-    sizes = sorted({-(-band // 4), -(-band // 2), band})
-    older = call(
-        functools.partial(older_kernel, steps, sizes),
-        [(block, bf16)] * (NEAR - 1)
-        + [
-            (block, f32, VMEM),
-            ((NEAR, width, tile_len), bf16, VMEM),
-            ((steps - 1, tile_len, NEAR * tile_len), bf16, VMEM),
-            ((tile_len, tile_len), bf16, VMEM),
-        ]
-        + [((NEAR * shots, tile_len), bf16)] * (steps - 1),
-        [pltpu.SMEM, VMEM, VMEM, pltpu.HBM, pltpu.HBM],
-        [
-            VMEM(((band + steps - 1) * shots, tile_len), bf16),
-            VMEM((NEAR, band, tile_len, tile_len), bf16),
-            pltpu.SemaphoreType.DMA((NEAR, band)),
-            pltpu.SemaphoreType.DMA((NEAR + 1, steps)),
-        ],
-        out_specs=[pl.ANY] * (NEAR - 1) + [VMEM] * 4 + [pl.ANY] * (steps - 1),
-        limit=54 << 20,
-    )(lag_ranges, rim, history, near_inverse, interaction)
-    messages, (own, stage, recent, inverse), rest = older[: NEAR - 1], older[NEAR - 1 : NEAR + 3], older[NEAR + 3 :]
-    stage, recent, inverse = near_memory(stage), near_memory(recent), near_memory(inverse)
+    ).reshape(patches * CAP, piece + LANES)
+    (mine,) = call(
+        functools.partial(source_kernel, shots), [((piece, tile_len), f32)], [VMEM]
+    )(arrived)
+    source = [mine]
+    for k in range(1, pieces):
+        source.append(lax.ppermute(mine, "lag", [(i, (i - k) % lags) for i in range(lags)]))
 
     def exchange(blocks):
         gone = []
@@ -359,7 +396,7 @@
     densities = []
     for step in range(steps):
         last_step = step == steps - 1
-        inputs = [lag_ranges, source[step], inverse, own, *received]
+        inputs = [lag_ranges, source[step * pieces // steps], inverse, own, *received]
         if last_step:
             outs = [((tile_len, shots), bf16)]
         else:

time: 98.7 us -> 108 us (1.094)
  local copies, waits for them, and re-layouts: 3.97 us -> 13.9 us
  waiting for transfers between devices: 43.9 us -> 37.4 us
  Pallas kernels: 19.1 us -> 22.9 us
    unnamed x9 -> x15, local copies, waits for them, and re-layouts: 3.02 us -> 13 us
    ppermute x1, waiting for transfers between devices: 5.68 us -> 0.01 us  [local(): lax.ppermute(history[band - steps + 1:], 'lag', [(i, (i + 1) % lags) for...]
    pallas_call x2, Pallas kernels: 2.34 us -> 7.76 us  [the longest x1 6.62 us: local(): call(prepare_kernel, [((patches * CAP, piece + LANES), bf16), ((NEAR, ban...]
    ppermute x16, starting transfers between devices: 15.9 us -> 18.6 us  [exchange(): gone.append(lax.ppermute(b, 'patch', r))]
    all_to_all x1, starting transfers between devices: 7.46 us -> 5.5 us  [local(): lax.all_to_all(outgoing.reshape(patches, CAP, piece + LANES), 'patch', sp...]
    pallas_call x1, Pallas kernels: 10.1 us -> 8.46 us  [local(): call(functools.partial(older_kernel, steps, sizes), [(block, bf16)] * (NE...]
    ppermute x1, starting transfers between devices: 1.55 us -> 3.03 us  [local(): lax.ppermute(history[band - steps + 1:], 'lag', [(i, (i + 1) % lags) for...]
    ppermute x4, starting transfers between devices: 3.39 us -> 2.03 us  [lag_sum(): lax.ppermute(block.astype(jnp.bfloat16), 'lag', lag_partners(lags, distan...]
  transfers between devices with their start and end apart: 24 -> 25, of which waited for: 10 -> 10; matrix products, arithmetic and copies ran while one was open for 2% -> 3% of each run, Pallas kernels for 16% -> 19%
where the time goes in v1:
time: 108 us; the launch traced here: 107 us
  waiting for transfers between devices  37.4 us (35%)
  starting transfers between devices  31.3 us (29%)
  Pallas kernels  22.9 us (21%)
  local copies, waits for them, and re-layouts  13.9 us (13%)
  other arithmetic  1.62 us (2%)
    ppermute x16, waiting for transfers between devices, exchange(): gone.append(lax.ppermute(b, 'patch', r))  20.5 us
    ppermute x16, starting transfers between devices, exchange(): gone.append(lax.ppermute(b, 'patch', r))  18.6 us
    ppermute x4, waiting for transfers between devices, lag_sum(): lax.ppermute(block.astype(jnp.bfloat16), 'lag', lag_partners(lags, distan...  15.3 us
    unnamed x15, local copies, waits for them, and re-layouts  13 us
    pallas_call x1, Pallas kernels, local(): call(functools.partial(older_kernel, steps, sizes), [(block, bf16)] * (NE...  8.46 us
    pallas_call x1, Pallas kernels, local(): call(prepare_kernel, [((patches * CAP, piece + LANES), bf16), ((NEAR, ban...  6.62 us
    all_to_all x1, starting transfers between devices, local(): lax.all_to_all(outgoing.reshape(patches, CAP, piece + LANES), 'patch', sp...  5.5 us
    pallas_call x4, Pallas kernels, local(): call(functools.partial(step_kernel, step, last_step), outs, [pltpu.SMEM]...  5.18 us
  transfers between devices with their start and end apart: 25, of which 10 were waited for; matrix products, arithmetic and copies ran while one was open for 3% of the time, Pallas kernels for 19%

profile of v1, /device:TPU:0, one launch (start us, length us, event | category | flops | bytes accessed | tf_op | source)
XLA Modules:
  0.0 107.4 jit_solution(15302998509554268005)
XLA Ops:
  0.9 3.0 %collective-permute-start = (bf16[3,256,128]{2,1,0:T(8,128)(2,1)S(1)}, bf16[3,256,128]{2,1,0:T(8,128)(2,1)S(1)}, u32[]{:S(2)}, u32[]{:S(2)}) collective-permute-start(bf16[3,256,128]{2,1,0:T(8,128)(2,1)S(1)} %slice.3), channel_id=1, source_target_pairs={{0,1},{1,0},{2,3},{3,2},{4,5},{5,4},{6,7},{7,6},{8,9},{9,8},{10,11... | collective-permute-start | bytes 589832 | tf_op jit(solution)/shard_map/ppermute | solution.py:322
  4.0 1.7 %copy.11 = bf16[32,8,4,128]{3,1,2,0:T(8,128)(2,1)} copy(bf16[32,8,4,128]{3,2,1,0:T(4,128)(2,1)} %bitcast.9) | data formatting | bytes 524288
  5.7 6.6 %shard_map.73 = (bf16[256,384]{1,0:T(8,128)(2,1)}, bf16[5,15,256,256]{3,2,1,0:T(8,128)(2,1)S(1)}, bf16[15,256,128]{2,1,0:T(8,128)(2,1)S(1)}, bf16[3,256,1280]{2,1,0:T(8,128)(2,1)S(1)}, bf16[256,256]{1,0:T(8,128)(2,1)S(1)}) custom-call(s32[1,10]{1,0:T(1,128)} %ranges.11, s32[1,256]{1,0:T(1,128)} %bitcast.11, s32[1,256]{1,0:T(1,128)} %bitcast.12, ...), custom_call_target="tpu_custom_call" | custom-call | tf_op jit(solution)/shard_map/pallas_call | solution.py:327
  12.3 3.8 %copy-done = bf16[5,15,256,256]{3,2,1,0:T(8,128)(2,1)} copy-done((bf16[5,15,256,256]{3,2,1,0:T(8,128)(2,1)}, bf16[5,15,256,256]{3,2,1,0:T(8,128)(2,1)S(1)}, u32[]{:S(2)}) %copy-start) | copy-done | bytes 9830424
  17.0 5.5 %all-to-all-start = ((bf16[16,16,384]{2,1,0:T(8,128)(2,1)}), bf16[16,16,384]{2,1,0:T(8,128)(2,1)}, u32[]{:S(2)}, u32[]{:S(2)}) async-start(bf16[16,16,384]{2,1,0:T(8,128)(2,1)} %bitcast.10), calls=%async_computation | async-start | bytes 393216 | tf_op jit(solution)/shard_map/all_to_all | solution.py:368
  23.2 3.8 %copy-done.1 = bf16[5,15,256,256]{3,2,1,0:T(8,128)(2,1)S(1)} copy-done((bf16[5,15,256,256]{3,2,1,0:T(8,128)(2,1)S(1)}, bf16[5,15,256,256]{3,2,1,0:T(8,128)(2,1)}, u32[]{:S(2)}) %copy-start.1) | copy-done | bytes 9830424
  27.0 1.2 %copy-done.3 = bf16[15,256,128]{2,1,0:T(8,128)(2,1)S(1)} copy-done((bf16[15,256,128]{2,1,0:T(8,128)(2,1)S(1)}, bf16[15,256,128]{2,1,0:T(8,128)(2,1)}, u32[]{:S(2)}) %copy-start.3) | copy-done | bytes 983064
  28.2 8.5 %shard_map.75 = (bf16[128,256]{1,0:T(8,128)(2,1)}, bf16[128,256]{1,0:T(8,128)(2,1)}, bf16[128,256]{1,0:T(8,128)(2,1)}, bf16[128,256]{1,0:T(8,128)(2,1)}, f32[128...) custom-call(s32[1,10]{1,0:T(1,128)} %ranges.11, ...), custom_call_target="tpu_custom_call" | custom-call | tf_op jit(solution)/shard_map/pallas_call | solution.py:352
  36.7 3.4 %collective-permute-start.1 = (bf16[128,256]{1,0:T(8,128)(2,1)}, bf16[128,256]{1,0:T(8,128)(2,1)S(1)}, u32[]{:S(2)}, u32[]{:S(2)}) collective-permute-start(bf16[128,256]{1,0:T(8,128)(2,1)} %get-tuple-element.42), channel_id=1, source_target_pairs={{0,28},{2,30},{4,8},{6,10},{8,4},{10,6},{12,16},{14,18},{16,12},{1... | collective-permute-start | bytes 196616 | tf_op jit(solution)/shard_map/ppermute | solution.py:385
  40.7 3.3 %collective-permute-done.1 = bf16[128,256]{1,0:T(8,128)(2,1)S(1)} collective-permute-done((bf16[128,256]{1,0:T(8,128)(2,1)}, bf16[128,256]{1,0:T(8,128)(2,1)S(1)}, u32[]{:S(2)}, u32[]{:S(2)}) %collective-permute-start.1) | collective-permute-done | bytes 65568 | tf_op jit(solution)/shard_map/ppermute | solution.py:385
  44.0 2.8 %collective-permute-done.2 = bf16[128,256]{1,0:T(8,128)(2,1)S(1)} collective-permute-done((bf16[128,256]{1,0:T(8,128)(2,1)}, bf16[128,256]{1,0:T(8,128)(2,1)S(1)}, u32[]{:S(2)}, u32[]{:S(2)}) %collective-permute-start.2) | collective-permute-done | bytes 65568 | tf_op jit(solution)/shard_map/ppermute | solution.py:385
  46.8 1.6 %fusion = (bf16[128,256]{1,0:T(8,128)(2,1)}, f32[128,256]{1,0:T(8,128)}) fusion(bf16[128,256]{1,0:T(8,128)(2,1)S(1)} %collective-permute-done.4, bf16[128,256]{1,0:T(8,128)(2,1)S(1)} %collective-permute-done.3, bf16[128,256]{1,0:T(8,128)(2,1)S(1)} %collective-permute-done.2, f32[128,256]{1,0:T(8,128)} %get-tuple-element.41, ...), kind=kLoop, calls=%fused_computation.2 | loop fusion | flops 294912 | bytes 589824 | tf_op jit(solution)/shard_map/convert_element_type | solution.py:295
  48.4 2.0 %collective-permute-start.5 = (bf16[128,256]{1,0:T(8,128)(2,1)}, bf16[128,256]{1,0:T(8,128)(2,1)S(1)}, u32[]{:S(2)}, u32[]{:S(2)}) collective-permute-start(bf16[128,256]{1,0:T(8,128)(2,1)} %get-tuple-element.69), channel_id=1, source_target_pairs={{0,1},{1,0},{2,3},{3,2},{4,5},{5,4},{6,7},{7,6},{8,9},{9,8},{10,11... | collective-permute-start | bytes 196616 | tf_op jit(solution)/shard_map/ppermute | solution.py:295
  50.4 1.1 %shard_map.74.source = f32[256,256]{1,0:T(8,128)S(1)} custom-call(bf16[256,384]{1,0:T(8,128)(2,1)} %bitcast.3.arrived_ref), custom_call_target="tpu_custom_call" | custom-call | tf_op jit(solution)/shard_map/pallas_call | solution.py:375
  51.6 15.3 %collective-permute-done.5.refs_0_ = bf16[128,256]{1,0:T(8,128)(2,1)S(1)} collective-permute-done((bf16[128,256]{1,0:T(8,128)(2,1)}, bf16[128,256]{1,0:T(8,128)(2,1)S(1)}, u32[]{:S(2)}, u32[]{:S(2)}) %collective-permute-start.5) | collective-permute-done | bytes 65568 | tf_op jit(solution)/shard_map/ppermute | solution.py:295
  67.9 1.4 %shard_map.76 = (bf16[128,256]{1,0:T(8,128)(2,1)S(1)}, f32[128,256]{1,0:T(8,128)S(1)}, bf16[128,256]{1,0:T(8,128)(2,1)S(1)}, bf16[128,256]{1,0:T(8,128)(2,1)S(1)...) custom-call(s32[1,10]{1,0:T(1,128)S(1)} %copy-done.5, f32[256,256]{1,0:T(8,128)S(1)} %shard_map.74.source, ...), custom_call_target="tpu_custom_call" | custom-call | tf_op jit(solution)/shard_map/pallas_call | solution.py:408
  69.3 4.4 %collective-permute-start.7 = (bf16[128,256]{1,0:T(8,128)(2,1)S(1)}, bf16[128,256]{1,0:T(8,128)(2,1)S(1)}, u32[]{:S(2)}, u32[]{:S(2)}) collective-permute-start(bf16[128,256]{1,0:T(8,128)(2,1)S(1)} %get-tuple-element.51), channel_id=1, source_target_pairs={{0,28},{2,30},{4,8},{6,10},{8,4},{10,6},{12,16},{14,18},{16,12},{1... | collective-permute-start | bytes 196616 | tf_op jit(solution)/shard_map/ppermute | solution.py:385
  73.9 1.6 %collective-permute-start.9 = (bf16[128,256]{1,0:T(8,128)(2,1)S(1)}, bf16[128,256]{1,0:T(8,128)(2,1)S(1)}, u32[]{:S(2)}, u32[]{:S(2)}) collective-permute-start(bf16[128,256]{1,0:T(8,128)(2,1)S(1)} %get-tuple-element.53), channel_id=1, source_target_pairs={{0,4},{2,6},{4,0},{6,2},{8,12},{10,14},{12,8},{14,10},{16,20},{18,... | collective-permute-start | bytes 196616 | tf_op jit(solution)/shard_map/ppermute | solution.py:385
  75.5 1.0 collective-permute-done.7.refs_0_
  76.5 3.6 %collective-permute-done.8.refs_1_ = bf16[128,256]{1,0:T(8,128)(2,1)S(1)} collective-permute-done((bf16[128,256]{1,0:T(8,128)(2,1)S(1)}, bf16[128,256]{1,0:T(8,128)(2,1)S(1)}, u32[]{:S(2)}, u32[]{:S(2)}) %collective-permute-start.8) | collective-permute-done | bytes 65568 | tf_op jit(solution)/shard_map/ppermute | solution.py:385
  80.1 1.4 %shard_map.77 = (bf16[128,256]{1,0:T(8,128)(2,1)S(1)}, f32[128,256]{1,0:T(8,128)S(1)}, bf16[128,256]{1,0:T(8,128)(2,1)S(1)}, bf16[128,256]{1,0:T(8,128)(2,1)S(1)...) custom-call(s32[1,10]{1,0:T(1,128)S(1)} %copy-done.5, f32[256,256]{1,0:T(8,128)S(1)} %shard_map.74.source, ...), custom_call_target="tpu_custom_call" | custom-call | tf_op jit(solution)/shard_map/pallas_call | solution.py:408
  81.5 2.8 %collective-permute-start.13 = (bf16[128,256]{1,0:T(8,128)(2,1)S(1)}, bf16[128,256]{1,0:T(8,128)(2,1)S(1)}, u32[]{:S(2)}, u32[]{:S(2)}) collective-permute-start(bf16[128,256]{1,0:T(8,128)(2,1)S(1)} %get-tuple-element.58), channel_id=1, source_target_pairs={{0,28},{2,30},{4,8},{6,10},{8,4},{10,6},{12,16},{14,18},{16,12},{1... | collective-permute-start | bytes 196616 | tf_op jit(solution)/shard_map/ppermute | solution.py:385
  84.3 1.5 %collective-permute-start.15 = (bf16[128,256]{1,0:T(8,128)(2,1)S(1)}, bf16[128,256]{1,0:T(8,128)(2,1)S(1)}, u32[]{:S(2)}, u32[]{:S(2)}) collective-permute-start(bf16[128,256]{1,0:T(8,128)(2,1)S(1)} %get-tuple-element.60), channel_id=1, source_target_pairs={{0,4},{2,6},{4,0},{6,2},{8,12},{10,14},{12,8},{14,10},{16,20},{18,... | collective-permute-start | bytes 196616 | tf_op jit(solution)/shard_map/ppermute | solution.py:385
  85.8 2.8 %collective-permute-done.13.refs_0_ = bf16[128,256]{1,0:T(8,128)(2,1)S(1)} collective-permute-done((bf16[128,256]{1,0:T(8,128)(2,1)S(1)}, bf16[128,256]{1,0:T(8,128)(2,1)S(1)}, u32[]{:S(2)}, u32[]{:S(2)}) %collective-permute-start.13) | collective-permute-done | bytes 65568 | tf_op jit(solution)/shard_map/ppermute | solution.py:385
  88.7 2.1 %collective-permute-done.14.refs_1_ = bf16[128,256]{1,0:T(8,128)(2,1)S(1)} collective-permute-done((bf16[128,256]{1,0:T(8,128)(2,1)S(1)}, bf16[128,256]{1,0:T(8,128)(2,1)S(1)}, u32[]{:S(2)}, u32[]{:S(2)}) %collective-permute-start.14) | collective-permute-done | bytes 65568 | tf_op jit(solution)/shard_map/ppermute | solution.py:385
  90.7 1.6 %shard_map.78 = (bf16[128,256]{1,0:T(8,128)(2,1)S(1)}, f32[128,256]{1,0:T(8,128)S(1)}, bf16[128,256]{1,0:T(8,128)(2,1)S(1)}, bf16[128,256]{1,0:T(8,128)(2,1)S(1)...) custom-call(s32[1,10]{1,0:T(1,128)S(1)} %copy-done.5, f32[256,256]{1,0:T(8,128)S(1)} %collective-permute-done.12.source, ...), custom_call_target="tpu_custom_call" | custom-call | tf_op jit(solution)/shard_map/pallas_call | solution.py:408
  92.5 2.7 %collective-permute-start.19 = (bf16[128,256]{1,0:T(8,128)(2,1)S(1)}, bf16[128,256]{1,0:T(8,128)(2,1)S(1)}, u32[]{:S(2)}, u32[]{:S(2)}) collective-permute-start(bf16[128,256]{1,0:T(8,128)(2,1)S(1)} %get-tuple-element.65), channel_id=1, source_target_pairs={{0,28},{2,30},{4,8},{6,10},{8,4},{10,6},{12,16},{14,18},{16,12},{1... | collective-permute-start | bytes 196616 | tf_op jit(solution)/shard_map/ppermute | solution.py:385
  95.2 1.5 %collective-permute-start.21 = (bf16[128,256]{1,0:T(8,128)(2,1)S(1)}, bf16[128,256]{1,0:T(8,128)(2,1)S(1)}, u32[]{:S(2)}, u32[]{:S(2)}) collective-permute-start(bf16[128,256]{1,0:T(8,128)(2,1)S(1)} %get-tuple-element.67), channel_id=1, source_target_pairs={{0,4},{2,6},{4,0},{6,2},{8,12},{10,14},{12,8},{14,10},{16,20},{18,... | collective-permute-start | bytes 196616 | tf_op jit(solution)/shard_map/ppermute | solution.py:385
  96.7 3.0 %collective-permute-done.19.refs_0_ = bf16[128,256]{1,0:T(8,128)(2,1)S(1)} collective-permute-done((bf16[128,256]{1,0:T(8,128)(2,1)S(1)}, bf16[128,256]{1,0:T(8,128)(2,1)S(1)}, u32[]{:S(2)}, u32[]{:S(2)}) %collective-permute-start.19) | collective-permute-done | bytes 65568 | tf_op jit(solution)/shard_map/ppermute | solution.py:385
  99.6 1.9 %collective-permute-done.20.refs_1_ = bf16[128,256]{1,0:T(8,128)(2,1)S(1)} collective-permute-done((bf16[128,256]{1,0:T(8,128)(2,1)S(1)}, bf16[128,256]{1,0:T(8,128)(2,1)S(1)}, u32[]{:S(2)}, u32[]{:S(2)}) %collective-permute-start.20) | collective-permute-done | bytes 65568 | tf_op jit(solution)/shard_map/ppermute | solution.py:385
  102.4 2.0 %collective-permute-start.23 = (bf16[256,128]{1,0:T(8,128)(2,1)S(1)}, bf16[256,128]{1,0:T(8,128)(2,1)S(1)}, u32[]{:S(2)}, u32[]{:S(2)}) collective-permute-start(bf16[256,128]{1,0:T(8,128)(2,1)S(1)} %shard_map.81.mine), channel_id=1, source_target_pairs={{0,1},{1,0},{2,3},{3,2},{4,5},{5,4},{6,7},{7,6},{8,9},{9,8},{10,11... | collective-permute-start | bytes 196616 | tf_op jit(solution)/shard_map/ppermute | solution.py:307
  105.1 1.6 %collective-permute-done.23.far = bf16[256,128]{1,0:T(8,128)(2,1)S(1)} collective-permute-done((bf16[256,128]{1,0:T(8,128)(2,1)S(1)}, bf16[256,128]{1,0:T(8,128)(2,1)S(1)}, u32[]{:S(2)}, u32[]{:S(2)}) %collective-permute-start.23) | collective-permute-done | bytes 65568 | tf_op jit(solution)/shard_map/ppermute | solution.py:307
  (45 shorter events, 6.7 us)
Async XLA Ops:
  0.9 21.6 %collective-permute-start = (bf16[3,256,128]{2,1,0:T(8,128)(2,1)S(1)}, bf16[3,256,128]{2,1,0:T(8,128)(2,1)S(1)}, u32[]{:S(2)}, u32[]{:S(2)}) collective-permute-start(bf16[3,256,128]{2,1,0:T(8,128)(2,1)S(1)} %slice.3), channel_id=1, source_target_pairs={{0,1},{1,0},{2,3},{3,2},{4,5},{5,4},{6,7},{7,6},{8,9},{9,8},{10,11... | collective-permute-start | bytes 589832 | tf_op jit(solution)/shard_map/ppermute | solution.py:322
  5.7 61.3 %copy-start.5 = (s32[1,10]{1,0:T(1,128)S(1)}, s32[1,10]{1,0:T(1,128)}, u32[]{:S(2)}) copy-start(s32[1,10]{1,0:T(1,128)} %ranges.11) | copy-start | bytes 124
  12.3 3.8 %copy-start = (bf16[5,15,256,256]{3,2,1,0:T(8,128)(2,1)}, bf16[5,15,256,256]{3,2,1,0:T(8,128)(2,1)S(1)}, u32[]{:S(2)}) copy-start(bf16[5,15,256,256]{3,2,1,0:T(8,128)(2,1)S(1)} %get-tuple-element.40.blocks) | copy-start | bytes 29491204
  16.1 1.0 copy-start.2
  17.0 33.4 %all-to-all-start = ((bf16[16,16,384]{2,1,0:T(8,128)(2,1)}), bf16[16,16,384]{2,1,0:T(8,128)(2,1)}, u32[]{:S(2)}, u32[]{:S(2)}) async-start(bf16[16,16,384]{2,1,0:T(8,128)(2,1)} %bitcast.10), calls=%async_computation | async-start | bytes 393216 | tf_op jit(solution)/shard_map/all_to_all | solution.py:368
  22.6 0.7 copy-start.6
  23.2 3.8 %copy-start.1 = (bf16[5,15,256,256]{3,2,1,0:T(8,128)(2,1)S(1)}, bf16[5,15,256,256]{3,2,1,0:T(8,128)(2,1)}, u32[]{:S(2)}) copy-start(bf16[5,15,256,256]{3,2,1,0:T(8,128)(2,1)} %copy-done) | copy-start | bytes 29491204
  27.0 1.2 %copy-start.3 = (bf16[15,256,128]{2,1,0:T(8,128)(2,1)S(1)}, bf16[15,256,128]{2,1,0:T(8,128)(2,1)}, u32[]{:S(2)}) copy-start(bf16[15,256,128]{2,1,0:T(8,128)(2,1)} %copy-done.2) | copy-start | bytes 2949124
  36.7 7.3 %collective-permute-start.1 = (bf16[128,256]{1,0:T(8,128)(2,1)}, bf16[128,256]{1,0:T(8,128)(2,1)S(1)}, u32[]{:S(2)}, u32[]{:S(2)}) collective-permute-start(bf16[128,256]{1,0:T(8,128)(2,1)} %get-tuple-element.42), channel_id=1, source_target_pairs={{0,28},{2,30},{4,8},{6,10},{8,4},{10,6},{12,16},{14,18},{16,12},{1... | collective-permute-start | bytes 196616 | tf_op jit(solution)/shard_map/ppermute | solution.py:385
  40.1 6.6 %collective-permute-start.2 = (bf16[128,256]{1,0:T(8,128)(2,1)}, bf16[128,256]{1,0:T(8,128)(2,1)S(1)}, u32[]{:S(2)}, u32[]{:S(2)}) collective-permute-start(bf16[128,256]{1,0:T(8,128)(2,1)} %get-tuple-element.43), channel_id=1, source_target_pairs={{0,30},{2,4},{4,2},{6,8},{8,6},{10,12},{12,10},{14,16},{16,14},{18... | collective-permute-start | bytes 196616 | tf_op jit(solution)/shard_map/ppermute | solution.py:385
  40.2 6.6 %collective-permute-start.3 = (bf16[128,256]{1,0:T(8,128)(2,1)}, bf16[128,256]{1,0:T(8,128)(2,1)S(1)}, u32[]{:S(2)}, u32[]{:S(2)}) collective-permute-start(bf16[128,256]{1,0:T(8,128)(2,1)} %get-tuple-element.44), channel_id=1, source_target_pairs={{0,4},{2,6},{4,0},{6,2},{8,12},{10,14},{12,8},{14,10},{16,20},{18,... | collective-permute-start | bytes 196616 | tf_op jit(solution)/shard_map/ppermute | solution.py:385
  40.6 6.2 %collective-permute-start.4 = (bf16[128,256]{1,0:T(8,128)(2,1)}, bf16[128,256]{1,0:T(8,128)(2,1)S(1)}, u32[]{:S(2)}, u32[]{:S(2)}) collective-permute-start(bf16[128,256]{1,0:T(8,128)(2,1)} %get-tuple-element.45), channel_id=1, source_target_pairs={{0,2},{2,0},{4,6},{6,4},{8,10},{10,8},{12,14},{14,12},{16,18},{18,... | collective-permute-start | bytes 196616 | tf_op jit(solution)/shard_map/ppermute | solution.py:385
  40.7 26.2 %collective-permute-start.6 = (bf16[640,256]{1,0:T(8,128)(2,1)}, bf16[640,256]{1,0:T(8,128)(2,1)}, u32[]{:S(2)}, u32[]{:S(2)}) collective-permute-start(bf16[640,256]{1,0:T(8,128)(2,1)} %get-tuple-element.48), channel_id=1, source_target_pairs={{0,1},{1,0},{2,3},{3,2},{4,5},{5,4},{6,7},{7,6},{8,9},{9,8},{10,11... | collective-permute-start | bytes 983048 | tf_op jit(solution)/shard_map/ppermute | solution.py:295
  44.0 29.7 %collective-permute-start.11 = (bf16[640,256]{1,0:T(8,128)(2,1)}, bf16[640,256]{1,0:T(8,128)(2,1)}, u32[]{:S(2)}, u32[]{:S(2)}) collective-permute-start(bf16[640,256]{1,0:T(8,128)(2,1)} %get-tuple-element.55), channel_id=1, source_target_pairs={{0,1},{1,0},{2,3},{3,2},{4,5},{5,4},{6,7},{7,6},{8,9},{9,8},{10,11... | collective-permute-start | bytes 983048 | tf_op jit(solution)/shard_map/ppermute | solution.py:295
  46.7 39.0 %collective-permute-start.17 = (bf16[640,256]{1,0:T(8,128)(2,1)}, bf16[640,256]{1,0:T(8,128)(2,1)}, u32[]{:S(2)}, u32[]{:S(2)}) collective-permute-start(bf16[640,256]{1,0:T(8,128)(2,1)} %get-tuple-element.62), channel_id=1, source_target_pairs={{0,1},{1,0},{2,3},{3,2},{4,5},{5,4},{6,7},{7,6},{8,9},{9,8},{10,11... | collective-permute-start | bytes 983048 | tf_op jit(solution)/shard_map/ppermute | solution.py:295
  48.4 18.6 %collective-permute-start.5 = (bf16[128,256]{1,0:T(8,128)(2,1)}, bf16[128,256]{1,0:T(8,128)(2,1)S(1)}, u32[]{:S(2)}, u32[]{:S(2)}) collective-permute-start(bf16[128,256]{1,0:T(8,128)(2,1)} %get-tuple-element.69), channel_id=1, source_target_pairs={{0,1},{1,0},{2,3},{3,2},{4,5},{5,4},{6,7},{7,6},{8,9},{9,8},{10,11... | collective-permute-start | bytes 196616 | tf_op jit(solution)/shard_map/ppermute | solution.py:295
  51.6 34.2 %collective-permute-start.12 = (f32[256,256]{1,0:T(8,128)S(1)}, f32[256,256]{1,0:T(8,128)S(1)}, u32[]{:S(2)}, u32[]{:S(2)}) collective-permute-start(f32[256,256]{1,0:T(8,128)S(1)} %shard_map.74.source), channel_id=1, source_target_pairs={{0,1},{1,0},{2,3},{3,2},{4,5},{5,4},{6,7},{7,6},{8,9},{9,8},{10,11... | collective-permute-start | bytes 786440 | tf_op jit(solution)/shard_map/ppermute | solution.py:380
  67.0 0.9 copy-start.4
  69.2 4.6 %collective-permute-start.10 = (bf16[128,256]{1,0:T(8,128)(2,1)S(1)}, bf16[128,256]{1,0:T(8,128)(2,1)S(1)}, u32[]{:S(2)}, u32[]{:S(2)}) collective-permute-start(bf16[128,256]{1,0:T(8,128)(2,1)S(1)} %get-tuple-element.54), channel_id=1, source_target_pairs={{0,2},{2,0},{4,6},{6,4},{8,10},{10,8},{12,14},{14,12},{16,18},{18,... | collective-permute-start | bytes 196616 | tf_op jit(solution)/shard_map/ppermute | solution.py:385
  69.3 7.2 %collective-permute-start.7 = (bf16[128,256]{1,0:T(8,128)(2,1)S(1)}, bf16[128,256]{1,0:T(8,128)(2,1)S(1)}, u32[]{:S(2)}, u32[]{:S(2)}) collective-permute-start(bf16[128,256]{1,0:T(8,128)(2,1)S(1)} %get-tuple-element.51), channel_id=1, source_target_pairs={{0,28},{2,30},{4,8},{6,10},{8,4},{10,6},{12,16},{14,18},{16,12},{1... | collective-permute-start | bytes 196616 | tf_op jit(solution)/shard_map/ppermute | solution.py:385
  73.7 6.4 %collective-permute-start.8 = (bf16[128,256]{1,0:T(8,128)(2,1)S(1)}, bf16[128,256]{1,0:T(8,128)(2,1)S(1)}, u32[]{:S(2)}, u32[]{:S(2)}) collective-permute-start(bf16[128,256]{1,0:T(8,128)(2,1)S(1)} %get-tuple-element.52), channel_id=1, source_target_pairs={{0,30},{2,4},{4,2},{6,8},{8,6},{10,12},{12,10},{14,16},{16,14},{18... | collective-permute-start | bytes 196616 | tf_op jit(solution)/shard_map/ppermute | solution.py:385
  73.9 6.2 %collective-permute-start.9 = (bf16[128,256]{1,0:T(8,128)(2,1)S(1)}, bf16[128,256]{1,0:T(8,128)(2,1)S(1)}, u32[]{:S(2)}, u32[]{:S(2)}) collective-permute-start(bf16[128,256]{1,0:T(8,128)(2,1)S(1)} %get-tuple-element.53), channel_id=1, source_target_pairs={{0,4},{2,6},{4,0},{6,2},{8,12},{10,14},{12,8},{14,10},{16,20},{18,... | collective-permute-start | bytes 196616 | tf_op jit(solution)/shard_map/ppermute | solution.py:385
  81.5 7.1 %collective-permute-start.13 = (bf16[128,256]{1,0:T(8,128)(2,1)S(1)}, bf16[128,256]{1,0:T(8,128)(2,1)S(1)}, u32[]{:S(2)}, u32[]{:S(2)}) collective-permute-start(bf16[128,256]{1,0:T(8,128)(2,1)S(1)} %get-tuple-element.58), channel_id=1, source_target_pairs={{0,28},{2,30},{4,8},{6,10},{8,4},{10,6},{12,16},{14,18},{16,12},{1... | collective-permute-start | bytes 196616 | tf_op jit(solution)/shard_map/ppermute | solution.py:385
  84.3 6.4 %collective-permute-start.14 = (bf16[128,256]{1,0:T(8,128)(2,1)S(1)}, bf16[128,256]{1,0:T(8,128)(2,1)S(1)}, u32[]{:S(2)}, u32[]{:S(2)}) collective-permute-start(bf16[128,256]{1,0:T(8,128)(2,1)S(1)} %get-tuple-element.59), channel_id=1, source_target_pairs={{0,30},{2,4},{4,2},{6,8},{8,6},{10,12},{12,10},{14,16},{16,14},{18... | collective-permute-start | bytes 196616 | tf_op jit(solution)/shard_map/ppermute | solution.py:385
  84.3 6.4 %collective-permute-start.15 = (bf16[128,256]{1,0:T(8,128)(2,1)S(1)}, bf16[128,256]{1,0:T(8,128)(2,1)S(1)}, u32[]{:S(2)}, u32[]{:S(2)}) collective-permute-start(bf16[128,256]{1,0:T(8,128)(2,1)S(1)} %get-tuple-element.60), channel_id=1, source_target_pairs={{0,4},{2,6},{4,0},{6,2},{8,12},{10,14},{12,8},{14,10},{16,20},{18,... | collective-permute-start | bytes 196616 | tf_op jit(solution)/shard_map/ppermute | solution.py:385
  85.8 4.9 %collective-permute-start.16 = (bf16[128,256]{1,0:T(8,128)(2,1)S(1)}, bf16[128,256]{1,0:T(8,128)(2,1)S(1)}, u32[]{:S(2)}, u32[]{:S(2)}) collective-permute-start(bf16[128,256]{1,0:T(8,128)(2,1)S(1)} %get-tuple-element.61), channel_id=1, source_target_pairs={{0,2},{2,0},{4,6},{6,4},{8,10},{10,8},{12,14},{14,12},{16,18},{18,... | collective-permute-start | bytes 196616 | tf_op jit(solution)/shard_map/ppermute | solution.py:385
  92.4 12.0 %collective-permute-start.18 = (bf16[3,256,128]{2,1,0:T(8,128)(2,1)S(1)}, bf16[3,256,128]{2,1,0:T(8,128)(2,1)S(1)}, u32[]{:S(2)}, u32[]{:S(2)}) collective-permute-start(bf16[3,256,128]{2,1,0:T(8,128)(2,1)S(1)} %shard_map.79.mine), channel_id=1, source_target_pairs={{0,1},{1,0},{2,3},{3,2},{4,5},{5,4},{6,7},{7,6},{8,9},{9,8},{10,11... | collective-permute-start | bytes 589832 | tf_op jit(solution)/shard_map/ppermute | solution.py:307
  92.5 7.1 %collective-permute-start.19 = (bf16[128,256]{1,0:T(8,128)(2,1)S(1)}, bf16[128,256]{1,0:T(8,128)(2,1)S(1)}, u32[]{:S(2)}, u32[]{:S(2)}) collective-permute-start(bf16[128,256]{1,0:T(8,128)(2,1)S(1)} %get-tuple-element.65), channel_id=1, source_target_pairs={{0,28},{2,30},{4,8},{6,10},{8,4},{10,6},{12,16},{14,18},{16,12},{1... | collective-permute-start | bytes 196616 | tf_op jit(solution)/shard_map/ppermute | solution.py:385
  95.2 6.4 %collective-permute-start.20 = (bf16[128,256]{1,0:T(8,128)(2,1)S(1)}, bf16[128,256]{1,0:T(8,128)(2,1)S(1)}, u32[]{:S(2)}, u32[]{:S(2)}) collective-permute-start(bf16[128,256]{1,0:T(8,128)(2,1)S(1)} %get-tuple-element.66), channel_id=1, source_target_pairs={{0,30},{2,4},{4,2},{6,8},{8,6},{10,12},{12,10},{14,16},{16,14},{18... | collective-permute-start | bytes 196616 | tf_op jit(solution)/shard_map/ppermute | solution.py:385
  95.2 6.4 %collective-permute-start.21 = (bf16[128,256]{1,0:T(8,128)(2,1)S(1)}, bf16[128,256]{1,0:T(8,128)(2,1)S(1)}, u32[]{:S(2)}, u32[]{:S(2)}) collective-permute-start(bf16[128,256]{1,0:T(8,128)(2,1)S(1)} %get-tuple-element.67), channel_id=1, source_target_pairs={{0,4},{2,6},{4,0},{6,2},{8,12},{10,14},{12,8},{14,10},{16,20},{18,... | collective-permute-start | bytes 196616 | tf_op jit(solution)/shard_map/ppermute | solution.py:385
  96.7 4.9 %collective-permute-start.22 = (bf16[128,256]{1,0:T(8,128)(2,1)S(1)}, bf16[128,256]{1,0:T(8,128)(2,1)S(1)}, u32[]{:S(2)}, u32[]{:S(2)}) collective-permute-start(bf16[128,256]{1,0:T(8,128)(2,1)S(1)} %get-tuple-element.68), channel_id=1, source_target_pairs={{0,2},{2,0},{4,6},{6,4},{8,10},{10,8},{12,14},{14,12},{16,18},{18,... | collective-permute-start | bytes 196616 | tf_op jit(solution)/shard_map/ppermute | solution.py:385
  102.4 4.3 %collective-permute-start.23 = (bf16[256,128]{1,0:T(8,128)(2,1)S(1)}, bf16[256,128]{1,0:T(8,128)(2,1)S(1)}, u32[]{:S(2)}, u32[]{:S(2)}) collective-permute-start(bf16[256,128]{1,0:T(8,128)(2,1)S(1)} %shard_map.81.mine), channel_id=1, source_target_pairs={{0,1},{1,0},{2,3},{3,2},{4,5},{5,4},{6,7},{7,6},{8,9},{9,8},{10,11... | collective-permute-start | bytes 196616 | tf_op jit(solution)/shard_map/ppermute | solution.py:307

commit v2 on v0

--- a/solution.py
+++ b/solution.py
@@ -32,7 +32,18 @@
     return [list(enumerate(p)) for p in (far, odd_even, near, core)]
 
 
-def pack_kernel(tile_ref, panel_ref, rows_ref, out_ref):
+def pack_kernel(tile_hbm, panel_hbm, history, rows_ref, out_ref, edge, tile_ref, panel_ref, sems):
+    copies = [
+        pltpu.make_async_copy(tile_hbm, tile_ref, sems.at[0]),
+        pltpu.make_async_copy(panel_hbm, panel_ref, sems.at[1]),
+        pltpu.make_async_copy(
+            history.at[pl.ds(history.shape[0] - edge.shape[0], edge.shape[0])], edge, sems.at[2]
+        ),
+    ]
+    for copy in copies:
+        copy.start()
+    for copy in copies[:2]:
+        copy.wait()
     recv = rows_ref.shape[0]
     width = rows_ref.shape[1]
     slots = out_ref.shape[0]
@@ -52,6 +63,7 @@
     marks = jnp.where(placed, (panel_ref[...] + 1).astype(jnp.float32), 0.0)
     label = jnp.sum(marks, axis=1, keepdims=True)
     out_ref[:, width:] = jnp.broadcast_to(label, (slots, LANES)).astype(jnp.bfloat16)
+    copies[2].wait()
 
 
 def source_kernel(arrived_ref, *outs):
@@ -266,6 +278,10 @@
     return pltpu.with_memory_space_constraint(array, VMEM)
 
 
+def far_memory(array):
+    return pltpu.with_memory_space_constraint(array, pltpu.HBM)
+
+
 def lag_partners(lags, distance):
     return [(i, i ^ distance) for i in range(lags)]
 
@@ -302,12 +318,19 @@
     block = (shots, tile_len)
     routes = pairings(patches)
 
-    rim = lax.ppermute(
-        history[band - steps + 1 :], "lag", [(i, (i + 1) % lags) for i in range(lags)]
+    outgoing, edge = call(
+        pack_kernel,
+        [((patches * CAP, width + LANES), bf16), ((steps - 1, tile_len, shots), bf16)],
+        [pltpu.HBM] * 3 + [VMEM],
+        [VMEM((1, recv), jnp.int32)] * 2 + [pltpu.SemaphoreType.DMA((3,))],
+        out_specs=[VMEM, pl.ANY],
+    )(
+        far_memory(receiver_tile.reshape(1, recv)),
+        far_memory(receiver_panel.reshape(1, recv)),
+        far_memory(history),
+        residuals.reshape(recv, width),
     )
-    (outgoing,) = call(
-        pack_kernel, [((patches * CAP, width + LANES), bf16)], [VMEM] * 3
-    )(receiver_tile.reshape(1, recv), receiver_panel.reshape(1, recv), residuals.reshape(recv, width))
+    rim = lax.ppermute(edge, "lag", [(i, (i + 1) % lags) for i in range(lags)])
     arrived = lax.all_to_all(
         outgoing.reshape(patches, CAP, width + LANES),
         "patch",
@@ -318,7 +341,7 @@
     source = call(source_kernel, [(block, f32, VMEM)] * steps, [VMEM])(arrived)
     source = [near_memory(s) for s in source]
 
-    sizes = sorted({-(-band // 4), -(-band // 2), band})
+    sizes = [*range(2, band, 2), band]
     older = call(
         functools.partial(older_kernel, steps, sizes),
         [(block, bf16)] * (NEAR - 1)
@@ -338,7 +361,7 @@
         ],
         out_specs=[pl.ANY] * (NEAR - 1) + [VMEM] * 4 + [pl.ANY] * (steps - 1),
         limit=54 << 20,
-    )(lag_ranges, rim, history, near_inverse, interaction)
+    )(lag_ranges, rim, history, far_memory(near_inverse), far_memory(interaction))
     messages, (own, stage, recent, inverse), rest = older[: NEAR - 1], older[NEAR - 1 : NEAR + 3], older[NEAR + 3 :]
     stage, recent, inverse = near_memory(stage), near_memory(recent), near_memory(inverse)
 

time: 98.7 us -> 96.5 us (0.978)
  local copies, waits for them, and re-layouts: 3.97 us -> 1.67 us
    unnamed x9 -> x5, local copies, waits for them, and re-layouts: 3.02 us -> 1.67 us
    pallas_call x1, Pallas kernels: 10.1 us -> 9.07 us  [local(): call(functools.partial(older_kernel, steps, sizes), [(block, bf16)] * (NE...]
  transfers between devices with their start and end apart: 24 -> 24, of which waited for: 10 -> 10; matrix products, arithmetic and copies ran while one was open for 2% -> 1% of each run, Pallas kernels for 16% -> 15%
where the time goes in v2:
time: 96.5 us; the launch traced here: 96.1 us
  waiting for transfers between devices  43.9 us (45%)
  starting transfers between devices  30.9 us (32%)
  Pallas kernels  18.8 us (19%)
  local copies, waits for them, and re-layouts  1.67 us (2%)
    ppermute x16, waiting for transfers between devices, exchange(): gone.append(lax.ppermute(b, 'patch', r))  20 us
    ppermute x16, starting transfers between devices, exchange(): gone.append(lax.ppermute(b, 'patch', r))  16.4 us
    ppermute x4, waiting for transfers between devices, lag_sum(): lax.ppermute(block.astype(jnp.bfloat16), 'lag', lag_partners(lags, distan...  15.6 us
    pallas_call x1, Pallas kernels, local(): call(functools.partial(older_kernel, steps, sizes), [(block, bf16)] * (NE...  9.07 us
    all_to_all x1, starting transfers between devices, local(): lax.all_to_all(outgoing.reshape(patches, CAP, width + LANES), 'patch', sp...  7.47 us
    ppermute x1, waiting for transfers between devices, local(): rim = lax.ppermute(edge, 'lag', [(i, (i + 1) % lags) for i in range(lags)])  5.68 us
    pallas_call x4, Pallas kernels, local(): call(functools.partial(step_kernel, step, last_step), outs, [pltpu.SMEM]...  5.22 us
    ppermute x4, starting transfers between devices, lag_sum(): lax.ppermute(block.astype(jnp.bfloat16), 'lag', lag_partners(lags, distan...  3.48 us
  transfers between devices with their start and end apart: 24, of which 10 were waited for; matrix products, arithmetic and copies ran while one was open for 1% of the time, Pallas kernels for 15%

profile of v2, /device:TPU:0, one launch (start us, length us, event | category | flops | bytes accessed | tf_op | source)
XLA Modules:
  0.0 96.1 jit_solution(5958064645949331083)
XLA Ops:
  0.0 1.0 %copy.11 = bf16[32,8,4,128]{3,1,2,0:T(8,128)(2,1)S(1)} copy(bf16[32,8,4,128]{3,2,1,0:T(4,128)(2,1)} %bitcast.9) | data formatting | bytes 524288
  1.0 1.8 %shard_map.73 = (bf16[256,640]{1,0:T(8,128)(2,1)}, bf16[3,256,128]{2,1,0:T(8,128)(2,1)S(1)}) custom-call(s32[1,256]{1,0:T(1,128)} %bitcast.10, s32[1,256]{1,0:T(1,128)} %bitcast.11, bf16[15,256,128]{2,1,0:T(8,128)(2,1)} %history.3, bf16[256,512]{1,0:T(8,128)(2,1)S(1)} %bitcast.8), custom_call_target="tpu_custom_call" | custom-call | tf_op jit(solution)/shard_map/pallas_call | solution.py:321
  2.8 7.5 %all-to-all-start = ((bf16[16,16,640]{2,1,0:T(8,128)(2,1)}), bf16[16,16,640]{2,1,0:T(8,128)(2,1)}, u32[]{:S(2)}, u32[]{:S(2)}) async-start(bf16[16,16,640]{2,1,0:T(8,128)(2,1)} %bitcast.2), calls=%async_computation | async-start | bytes 655360 | tf_op jit(solution)/shard_map/all_to_all | solution.py:334
  10.3 1.6 %collective-permute-start = (bf16[3,256,128]{2,1,0:T(8,128)(2,1)S(1)}, bf16[3,256,128]{2,1,0:T(8,128)(2,1)S(1)}, u32[]{:S(2)}, u32[]{:S(2)}) collective-permute-start(bf16[3,256,128]{2,1,0:T(8,128)(2,1)S(1)} %get-tuple-element.42), channel_id=1, source_target_pairs={{0,1},{1,0},{2,3},{3,2},{4,5},{5,4},{6,7},{7,6},{8,9},{9,8},{10,11... | collective-permute-start | bytes 589832 | tf_op jit(solution)/shard_map/ppermute | solution.py:333
  11.9 5.7 %collective-permute-done.rim = bf16[3,256,128]{2,1,0:T(8,128)(2,1)S(1)} collective-permute-done((bf16[3,256,128]{2,1,0:T(8,128)(2,1)S(1)}, bf16[3,256,128]{2,1,0:T(8,128)(2,1)S(1)}, u32[]{:S(2)}, u32[]{:S(2)}) %collective-permute-start) | collective-permute-done | bytes 196640 | tf_op jit(solution)/shard_map/ppermute | solution.py:333
  17.6 0.7 copy-done.1
  18.2 9.1 %shard_map.75 = (bf16[128,256]{1,0:T(8,128)(2,1)}, bf16[128,256]{1,0:T(8,128)(2,1)}, bf16[128,256]{1,0:T(8,128)(2,1)}, bf16[128,256]{1,0:T(8,128)(2,1)}, f32[128...) custom-call(s32[1,10]{1,0:T(1,128)} %ranges.9, ...), custom_call_target="tpu_custom_call" | custom-call | tf_op jit(solution)/shard_map/pallas_call | solution.py:345
  27.3 3.7 %collective-permute-start.1 = (bf16[128,256]{1,0:T(8,128)(2,1)}, bf16[128,256]{1,0:T(8,128)(2,1)S(1)}, u32[]{:S(2)}, u32[]{:S(2)}) collective-permute-start(bf16[128,256]{1,0:T(8,128)(2,1)} %get-tuple-element.45), channel_id=1, source_target_pairs={{0,28},{2,30},{4,8},{6,10},{8,4},{10,6},{12,16},{14,18},{16,12},{1... | collective-permute-start | bytes 196616 | tf_op jit(solution)/shard_map/ppermute | solution.py:371
  31.4 1.5 %collective-permute-start.6 = (bf16[640,256]{1,0:T(8,128)(2,1)}, bf16[640,256]{1,0:T(8,128)(2,1)}, u32[]{:S(2)}, u32[]{:S(2)}) collective-permute-start(bf16[640,256]{1,0:T(8,128)(2,1)} %get-tuple-element.51), channel_id=1, source_target_pairs={{0,1},{1,0},{2,3},{3,2},{4,5},{5,4},{6,7},{7,6},{8,9},{9,8},{10,11... | collective-permute-start | bytes 983048 | tf_op jit(solution)/shard_map/ppermute | solution.py:294
  32.9 1.7 %collective-permute-done.1 = bf16[128,256]{1,0:T(8,128)(2,1)S(1)} collective-permute-done((bf16[128,256]{1,0:T(8,128)(2,1)}, bf16[128,256]{1,0:T(8,128)(2,1)S(1)}, u32[]{:S(2)}, u32[]{:S(2)}) %collective-permute-start.1) | collective-permute-done | bytes 65568 | tf_op jit(solution)/shard_map/ppermute | solution.py:371
  34.6 3.0 %collective-permute-done.2 = bf16[128,256]{1,0:T(8,128)(2,1)S(1)} collective-permute-done((bf16[128,256]{1,0:T(8,128)(2,1)}, bf16[128,256]{1,0:T(8,128)(2,1)S(1)}, u32[]{:S(2)}, u32[]{:S(2)}) %collective-permute-start.2) | collective-permute-done | bytes 65568 | tf_op jit(solution)/shard_map/ppermute | solution.py:371
  38.3 2.0 %collective-permute-start.5 = (bf16[128,256]{1,0:T(8,128)(2,1)}, bf16[128,256]{1,0:T(8,128)(2,1)}, u32[]{:S(2)}, u32[]{:S(2)}) collective-permute-start(bf16[128,256]{1,0:T(8,128)(2,1)} %get-tuple-element.75), channel_id=1, source_target_pairs={{0,1},{1,0},{2,3},{3,2},{4,5},{5,4},{6,7},{7,6},{8,9},{9,8},{10,11... | collective-permute-start | bytes 196616 | tf_op jit(solution)/shard_map/ppermute | solution.py:294
  40.3 1.2 %shard_map.74 = (f32[128,256]{1,0:T(8,128)S(1)}, f32[128,256]{1,0:T(8,128)S(1)}, f32[128,256]{1,0:T(8,128)S(1)}, f32[128,256]{1,0:T(8,128)S(1)}) custom-call(bf16[256,640]{1,0:T(8,128)(2,1)} %bitcast.3.arrived_ref), custom_call_target="tpu_custom_call" | custom-call | tf_op jit(solution)/shard_map/pallas_call | solution.py:341
  41.6 15.6 %collective-permute-done.5.refs_0_ = bf16[128,256]{1,0:T(8,128)(2,1)} collective-permute-done((bf16[128,256]{1,0:T(8,128)(2,1)}, bf16[128,256]{1,0:T(8,128)(2,1)}, u32[]{:S(2)}, u32[]{:S(2)}) %collective-permute-start.5) | collective-permute-done | bytes 65568 | tf_op jit(solution)/shard_map/ppermute | solution.py:294
  57.2 1.4 %shard_map.76 = (bf16[128,256]{1,0:T(8,128)(2,1)S(1)}, f32[128,256]{1,0:T(8,128)S(1)}, bf16[128,256]{1,0:T(8,128)(2,1)S(1)}, bf16[128,256]{1,0:T(8,128)(2,1)S(1)...) custom-call(s32[1,10]{1,0:T(1,128)S(1)} %copy-done, f32[128,256]{1,0:T(8,128)S(1)} %get-tuple-element.41.source, ...), custom_call_target="tpu_custom_call" | custom-call | tf_op jit(solution)/shard_map/pallas_call | solution.py:394
  58.6 4.1 %collective-permute-start.7 = (bf16[128,256]{1,0:T(8,128)(2,1)S(1)}, bf16[128,256]{1,0:T(8,128)(2,1)S(1)}, u32[]{:S(2)}, u32[]{:S(2)}) collective-permute-start(bf16[128,256]{1,0:T(8,128)(2,1)S(1)} %get-tuple-element.55), channel_id=1, source_target_pairs={{0,28},{2,30},{4,8},{6,10},{8,4},{10,6},{12,16},{14,18},{16,12},{1... | collective-permute-start | bytes 196616 | tf_op jit(solution)/shard_map/ppermute | solution.py:371
  63.2 2.5 %collective-permute-done.7.refs_0_ = bf16[128,256]{1,0:T(8,128)(2,1)S(1)} collective-permute-done((bf16[128,256]{1,0:T(8,128)(2,1)S(1)}, bf16[128,256]{1,0:T(8,128)(2,1)S(1)}, u32[]{:S(2)}, u32[]{:S(2)}) %collective-permute-start.7) | collective-permute-done | bytes 65568 | tf_op jit(solution)/shard_map/ppermute | solution.py:371
  65.7 3.4 %collective-permute-done.8.refs_1_ = bf16[128,256]{1,0:T(8,128)(2,1)S(1)} collective-permute-done((bf16[128,256]{1,0:T(8,128)(2,1)S(1)}, bf16[128,256]{1,0:T(8,128)(2,1)S(1)}, u32[]{:S(2)}, u32[]{:S(2)}) %collective-permute-start.8) | collective-permute-done | bytes 65568 | tf_op jit(solution)/shard_map/ppermute | solution.py:371
  69.1 1.5 %shard_map.77 = (bf16[128,256]{1,0:T(8,128)(2,1)S(1)}, f32[128,256]{1,0:T(8,128)S(1)}, bf16[128,256]{1,0:T(8,128)(2,1)S(1)}, bf16[128,256]{1,0:T(8,128)(2,1)S(1)...) custom-call(s32[1,10]{1,0:T(1,128)S(1)} %copy-done, f32[128,256]{1,0:T(8,128)S(1)} %get-tuple-element.53.source, ...), custom_call_target="tpu_custom_call" | custom-call | tf_op jit(solution)/shard_map/pallas_call | solution.py:394
  71.2 0.9 collective-permute-start.13
  72.1 1.7 %collective-permute-start.14 = (bf16[128,256]{1,0:T(8,128)(2,1)S(1)}, bf16[128,256]{1,0:T(8,128)(2,1)S(1)}, u32[]{:S(2)}, u32[]{:S(2)}) collective-permute-start(bf16[128,256]{1,0:T(8,128)(2,1)S(1)} %get-tuple-element.65), channel_id=1, source_target_pairs={{0,4},{2,6},{4,0},{6,2},{8,12},{10,14},{12,8},{14,10},{16,20},{18,... | collective-permute-start | bytes 196616 | tf_op jit(solution)/shard_map/ppermute | solution.py:371
  73.8 4.5 %collective-permute-done.12.refs_0_ = bf16[128,256]{1,0:T(8,128)(2,1)S(1)} collective-permute-done((bf16[128,256]{1,0:T(8,128)(2,1)S(1)}, bf16[128,256]{1,0:T(8,128)(2,1)S(1)}, u32[]{:S(2)}, u32[]{:S(2)}) %collective-permute-start.12) | collective-permute-done | bytes 65568 | tf_op jit(solution)/shard_map/ppermute | solution.py:371
  78.3 1.6 %shard_map.78 = (bf16[128,256]{1,0:T(8,128)(2,1)S(1)}, f32[128,256]{1,0:T(8,128)S(1)}, bf16[128,256]{1,0:T(8,128)(2,1)S(1)}, bf16[128,256]{1,0:T(8,128)(2,1)S(1)...) custom-call(s32[1,10]{1,0:T(1,128)S(1)} %copy-done, f32[128,256]{1,0:T(8,128)S(1)} %get-tuple-element.61.source, ...), custom_call_target="tpu_custom_call" | custom-call | tf_op jit(solution)/shard_map/pallas_call | solution.py:394
  80.0 1.0 collective-permute-start.17
  81.0 2.9 %collective-permute-start.18 = (bf16[128,256]{1,0:T(8,128)(2,1)S(1)}, bf16[128,256]{1,0:T(8,128)(2,1)S(1)}, u32[]{:S(2)}, u32[]{:S(2)}) collective-permute-start(bf16[128,256]{1,0:T(8,128)(2,1)S(1)} %get-tuple-element.71), channel_id=1, source_target_pairs={{0,28},{2,30},{4,8},{6,10},{8,4},{10,6},{12,16},{14,18},{16,12},{1... | collective-permute-start | bytes 196616 | tf_op jit(solution)/shard_map/ppermute | solution.py:371
  83.9 1.5 %collective-permute-start.20 = (bf16[128,256]{1,0:T(8,128)(2,1)S(1)}, bf16[128,256]{1,0:T(8,128)(2,1)S(1)}, u32[]{:S(2)}, u32[]{:S(2)}) collective-permute-start(bf16[128,256]{1,0:T(8,128)(2,1)S(1)} %get-tuple-element.73), channel_id=1, source_target_pairs={{0,4},{2,6},{4,0},{6,2},{8,12},{10,14},{12,8},{14,10},{16,20},{18,... | collective-permute-start | bytes 196616 | tf_op jit(solution)/shard_map/ppermute | solution.py:371
  85.5 2.6 %collective-permute-done.18.refs_0_ = bf16[128,256]{1,0:T(8,128)(2,1)S(1)} collective-permute-done((bf16[128,256]{1,0:T(8,128)(2,1)S(1)}, bf16[128,256]{1,0:T(8,128)(2,1)S(1)}, u32[]{:S(2)}, u32[]{:S(2)}) %collective-permute-start.18) | collective-permute-done | bytes 65568 | tf_op jit(solution)/shard_map/ppermute | solution.py:371
  88.0 2.3 %collective-permute-done.19.refs_1_ = bf16[128,256]{1,0:T(8,128)(2,1)S(1)} collective-permute-done((bf16[128,256]{1,0:T(8,128)(2,1)S(1)}, bf16[128,256]{1,0:T(8,128)(2,1)S(1)}, u32[]{:S(2)}, u32[]{:S(2)}) %collective-permute-start.19) | collective-permute-done | bytes 65568 | tf_op jit(solution)/shard_map/ppermute | solution.py:371
  90.3 0.8 shard_map.81.mine
  91.1 1.0 %collective-permute-start.22 = (bf16[256,128]{1,0:T(8,128)(2,1)S(1)}, bf16[256,128]{1,0:T(8,128)(2,1)S(1)}, u32[]{:S(2)}, u32[]{:S(2)}) collective-permute-start(bf16[256,128]{1,0:T(8,128)(2,1)S(1)} %shard_map.81.mine), channel_id=1, source_target_pairs={{0,1},{1,0},{2,3},{3,2},{4,5},{5,4},{6,7},{7,6},{8,9},{9,8},{10,11... | collective-permute-start | bytes 196616 | tf_op jit(solution)/shard_map/ppermute | solution.py:306
  92.1 0.7 shard_map.80.begun
  92.8 2.6 %collective-permute-done.22.far = bf16[256,128]{1,0:T(8,128)(2,1)S(1)} collective-permute-done((bf16[256,128]{1,0:T(8,128)(2,1)S(1)}, bf16[256,128]{1,0:T(8,128)(2,1)S(1)}, u32[]{:S(2)}, u32[]{:S(2)}) %collective-permute-start.22) | collective-permute-done | bytes 65568 | tf_op jit(solution)/shard_map/ppermute | solution.py:306
  (32 shorter events, 3.1 us)
Async XLA Ops:
  2.8 37.5 %all-to-all-start = ((bf16[16,16,640]{2,1,0:T(8,128)(2,1)}), bf16[16,16,640]{2,1,0:T(8,128)(2,1)}, u32[]{:S(2)}, u32[]{:S(2)}) async-start(bf16[16,16,640]{2,1,0:T(8,128)(2,1)} %bitcast.2), calls=%async_computation | async-start | bytes 655360 | tf_op jit(solution)/shard_map/all_to_all | solution.py:334
  10.3 46.9 %copy-start = (s32[1,10]{1,0:T(1,128)S(1)}, s32[1,10]{1,0:T(1,128)}, u32[]{:S(2)}) copy-start(s32[1,10]{1,0:T(1,128)} %ranges.9) | copy-start | bytes 124
  10.3 7.2 %collective-permute-start = (bf16[3,256,128]{2,1,0:T(8,128)(2,1)S(1)}, bf16[3,256,128]{2,1,0:T(8,128)(2,1)S(1)}, u32[]{:S(2)}, u32[]{:S(2)}) collective-permute-start(bf16[3,256,128]{2,1,0:T(8,128)(2,1)S(1)} %get-tuple-element.42), channel_id=1, source_target_pairs={{0,1},{1,0},{2,3},{3,2},{4,5},{5,4},{6,7},{7,6},{8,9},{9,8},{10,11... | collective-permute-start | bytes 589832 | tf_op jit(solution)/shard_map/ppermute | solution.py:333
  17.6 0.7 copy-start.1
  27.3 7.3 %collective-permute-start.1 = (bf16[128,256]{1,0:T(8,128)(2,1)}, bf16[128,256]{1,0:T(8,128)(2,1)S(1)}, u32[]{:S(2)}, u32[]{:S(2)}) collective-permute-start(bf16[128,256]{1,0:T(8,128)(2,1)} %get-tuple-element.45), channel_id=1, source_target_pairs={{0,28},{2,30},{4,8},{6,10},{8,4},{10,6},{12,16},{14,18},{16,12},{1... | collective-permute-start | bytes 196616 | tf_op jit(solution)/shard_map/ppermute | solution.py:371
  31.0 6.6 %collective-permute-start.2 = (bf16[128,256]{1,0:T(8,128)(2,1)}, bf16[128,256]{1,0:T(8,128)(2,1)S(1)}, u32[]{:S(2)}, u32[]{:S(2)}) collective-permute-start(bf16[128,256]{1,0:T(8,128)(2,1)} %get-tuple-element.46), channel_id=1, source_target_pairs={{0,30},{2,4},{4,2},{6,8},{8,6},{10,12},{12,10},{14,16},{16,14},{18... | collective-permute-start | bytes 196616 | tf_op jit(solution)/shard_map/ppermute | solution.py:371
  31.0 6.6 %collective-permute-start.3 = (bf16[128,256]{1,0:T(8,128)(2,1)}, bf16[128,256]{1,0:T(8,128)(2,1)S(1)}, u32[]{:S(2)}, u32[]{:S(2)}) collective-permute-start(bf16[128,256]{1,0:T(8,128)(2,1)} %get-tuple-element.47), channel_id=1, source_target_pairs={{0,4},{2,6},{4,0},{6,2},{8,12},{10,14},{12,8},{14,10},{16,20},{18,... | collective-permute-start | bytes 196616 | tf_op jit(solution)/shard_map/ppermute | solution.py:371
  31.3 6.3 %collective-permute-start.4 = (bf16[128,256]{1,0:T(8,128)(2,1)}, bf16[128,256]{1,0:T(8,128)(2,1)S(1)}, u32[]{:S(2)}, u32[]{:S(2)}) collective-permute-start(bf16[128,256]{1,0:T(8,128)(2,1)} %get-tuple-element.48), channel_id=1, source_target_pairs={{0,2},{2,0},{4,6},{6,4},{8,10},{10,8},{12,14},{14,12},{16,18},{18,... | collective-permute-start | bytes 196616 | tf_op jit(solution)/shard_map/ppermute | solution.py:371
  31.4 25.8 %collective-permute-start.6 = (bf16[640,256]{1,0:T(8,128)(2,1)}, bf16[640,256]{1,0:T(8,128)(2,1)}, u32[]{:S(2)}, u32[]{:S(2)}) collective-permute-start(bf16[640,256]{1,0:T(8,128)(2,1)} %get-tuple-element.51), channel_id=1, source_target_pairs={{0,1},{1,0},{2,3},{3,2},{4,5},{5,4},{6,7},{7,6},{8,9},{9,8},{10,11... | collective-permute-start | bytes 983048 | tf_op jit(solution)/shard_map/ppermute | solution.py:294
  34.6 28.7 %collective-permute-start.11 = (bf16[640,256]{1,0:T(8,128)(2,1)}, bf16[640,256]{1,0:T(8,128)(2,1)}, u32[]{:S(2)}, u32[]{:S(2)}) collective-permute-start(bf16[640,256]{1,0:T(8,128)(2,1)} %get-tuple-element.59), channel_id=1, source_target_pairs={{0,1},{1,0},{2,3},{3,2},{4,5},{5,4},{6,7},{7,6},{8,9},{9,8},{10,11... | collective-permute-start | bytes 983048 | tf_op jit(solution)/shard_map/ppermute | solution.py:294
  37.6 36.2 %collective-permute-start.16 = (bf16[640,256]{1,0:T(8,128)(2,1)}, bf16[640,256]{1,0:T(8,128)(2,1)}, u32[]{:S(2)}, u32[]{:S(2)}) collective-permute-start(bf16[640,256]{1,0:T(8,128)(2,1)} %get-tuple-element.67), channel_id=1, source_target_pairs={{0,1},{1,0},{2,3},{3,2},{4,5},{5,4},{6,7},{7,6},{8,9},{9,8},{10,11... | collective-permute-start | bytes 983048 | tf_op jit(solution)/shard_map/ppermute | solution.py:294
  38.3 18.9 %collective-permute-start.5 = (bf16[128,256]{1,0:T(8,128)(2,1)}, bf16[128,256]{1,0:T(8,128)(2,1)}, u32[]{:S(2)}, u32[]{:S(2)}) collective-permute-start(bf16[128,256]{1,0:T(8,128)(2,1)} %get-tuple-element.75), channel_id=1, source_target_pairs={{0,1},{1,0},{2,3},{3,2},{4,5},{5,4},{6,7},{7,6},{8,9},{9,8},{10,11... | collective-permute-start | bytes 196616 | tf_op jit(solution)/shard_map/ppermute | solution.py:294
  58.6 7.1 %collective-permute-start.7 = (bf16[128,256]{1,0:T(8,128)(2,1)S(1)}, bf16[128,256]{1,0:T(8,128)(2,1)S(1)}, u32[]{:S(2)}, u32[]{:S(2)}) collective-permute-start(bf16[128,256]{1,0:T(8,128)(2,1)S(1)} %get-tuple-element.55), channel_id=1, source_target_pairs={{0,28},{2,30},{4,8},{6,10},{8,4},{10,6},{12,16},{14,18},{16,12},{1... | collective-permute-start | bytes 196616 | tf_op jit(solution)/shard_map/ppermute | solution.py:371
  62.7 6.4 %collective-permute-start.8 = (bf16[128,256]{1,0:T(8,128)(2,1)S(1)}, bf16[128,256]{1,0:T(8,128)(2,1)S(1)}, u32[]{:S(2)}, u32[]{:S(2)}) collective-permute-start(bf16[128,256]{1,0:T(8,128)(2,1)S(1)} %get-tuple-element.56), channel_id=1, source_target_pairs={{0,30},{2,4},{4,2},{6,8},{8,6},{10,12},{12,10},{14,16},{16,14},{18... | collective-permute-start | bytes 196616 | tf_op jit(solution)/shard_map/ppermute | solution.py:371
  62.7 6.4 %collective-permute-start.9 = (bf16[128,256]{1,0:T(8,128)(2,1)S(1)}, bf16[128,256]{1,0:T(8,128)(2,1)S(1)}, u32[]{:S(2)}, u32[]{:S(2)}) collective-permute-start(bf16[128,256]{1,0:T(8,128)(2,1)S(1)} %get-tuple-element.57), channel_id=1, source_target_pairs={{0,4},{2,6},{4,0},{6,2},{8,12},{10,14},{12,8},{14,10},{16,20},{18,... | collective-permute-start | bytes 196616 | tf_op jit(solution)/shard_map/ppermute | solution.py:371
  63.2 5.9 %collective-permute-start.10 = (bf16[128,256]{1,0:T(8,128)(2,1)S(1)}, bf16[128,256]{1,0:T(8,128)(2,1)S(1)}, u32[]{:S(2)}, u32[]{:S(2)}) collective-permute-start(bf16[128,256]{1,0:T(8,128)(2,1)S(1)} %get-tuple-element.58), channel_id=1, source_target_pairs={{0,2},{2,0},{4,6},{6,4},{8,10},{10,8},{12,14},{14,12},{16,18},{18,... | collective-permute-start | bytes 196616 | tf_op jit(solution)/shard_map/ppermute | solution.py:371
  70.6 7.7 %collective-permute-start.12 = (bf16[128,256]{1,0:T(8,128)(2,1)S(1)}, bf16[128,256]{1,0:T(8,128)(2,1)S(1)}, u32[]{:S(2)}, u32[]{:S(2)}) collective-permute-start(bf16[128,256]{1,0:T(8,128)(2,1)S(1)} %get-tuple-element.63), channel_id=1, source_target_pairs={{0,28},{2,30},{4,8},{6,10},{8,4},{10,6},{12,16},{14,18},{16,12},{1... | collective-permute-start | bytes 196616 | tf_op jit(solution)/shard_map/ppermute | solution.py:371
  71.2 7.1 %collective-permute-start.13 = (bf16[128,256]{1,0:T(8,128)(2,1)S(1)}, bf16[128,256]{1,0:T(8,128)(2,1)S(1)}, u32[]{:S(2)}, u32[]{:S(2)}) collective-permute-start(bf16[128,256]{1,0:T(8,128)(2,1)S(1)} %get-tuple-element.64), channel_id=1, source_target_pairs={{0,30},{2,4},{4,2},{6,8},{8,6},{10,12},{12,10},{14,16},{16,14},{18... | collective-permute-start | bytes 196616 | tf_op jit(solution)/shard_map/ppermute | solution.py:371
  72.1 6.2 %collective-permute-start.14 = (bf16[128,256]{1,0:T(8,128)(2,1)S(1)}, bf16[128,256]{1,0:T(8,128)(2,1)S(1)}, u32[]{:S(2)}, u32[]{:S(2)}) collective-permute-start(bf16[128,256]{1,0:T(8,128)(2,1)S(1)} %get-tuple-element.65), channel_id=1, source_target_pairs={{0,4},{2,6},{4,0},{6,2},{8,12},{10,14},{12,8},{14,10},{16,20},{18,... | collective-permute-start | bytes 196616 | tf_op jit(solution)/shard_map/ppermute | solution.py:371
  73.8 4.5 %collective-permute-start.15 = (bf16[128,256]{1,0:T(8,128)(2,1)S(1)}, bf16[128,256]{1,0:T(8,128)(2,1)S(1)}, u32[]{:S(2)}, u32[]{:S(2)}) collective-permute-start(bf16[128,256]{1,0:T(8,128)(2,1)S(1)} %get-tuple-element.66), channel_id=1, source_target_pairs={{0,2},{2,0},{4,6},{6,4},{8,10},{10,8},{12,14},{14,12},{16,18},{18,... | collective-permute-start | bytes 196616 | tf_op jit(solution)/shard_map/ppermute | solution.py:371
  80.0 12.1 %collective-permute-start.17 = (bf16[3,256,128]{2,1,0:T(8,128)(2,1)S(1)}, bf16[3,256,128]{2,1,0:T(8,128)(2,1)S(1)}, u32[]{:S(2)}, u32[]{:S(2)}) collective-permute-start(bf16[3,256,128]{2,1,0:T(8,128)(2,1)S(1)} %shard_map.79.mine), channel_id=1, source_target_pairs={{0,1},{1,0},{2,3},{3,2},{4,5},{5,4},{6,7},{7,6},{8,9},{9,8},{10,11... | collective-permute-start | bytes 589832 | tf_op jit(solution)/shard_map/ppermute | solution.py:306
  81.0 7.1 %collective-permute-start.18 = (bf16[128,256]{1,0:T(8,128)(2,1)S(1)}, bf16[128,256]{1,0:T(8,128)(2,1)S(1)}, u32[]{:S(2)}, u32[]{:S(2)}) collective-permute-start(bf16[128,256]{1,0:T(8,128)(2,1)S(1)} %get-tuple-element.71), channel_id=1, source_target_pairs={{0,28},{2,30},{4,8},{6,10},{8,4},{10,6},{12,16},{14,18},{16,12},{1... | collective-permute-start | bytes 196616 | tf_op jit(solution)/shard_map/ppermute | solution.py:371
  83.9 6.4 %collective-permute-start.19 = (bf16[128,256]{1,0:T(8,128)(2,1)S(1)}, bf16[128,256]{1,0:T(8,128)(2,1)S(1)}, u32[]{:S(2)}, u32[]{:S(2)}) collective-permute-start(bf16[128,256]{1,0:T(8,128)(2,1)S(1)} %get-tuple-element.72), channel_id=1, source_target_pairs={{0,30},{2,4},{4,2},{6,8},{8,6},{10,12},{12,10},{14,16},{16,14},{18... | collective-permute-start | bytes 196616 | tf_op jit(solution)/shard_map/ppermute | solution.py:371
  83.9 6.4 %collective-permute-start.20 = (bf16[128,256]{1,0:T(8,128)(2,1)S(1)}, bf16[128,256]{1,0:T(8,128)(2,1)S(1)}, u32[]{:S(2)}, u32[]{:S(2)}) collective-permute-start(bf16[128,256]{1,0:T(8,128)(2,1)S(1)} %get-tuple-element.73), channel_id=1, source_target_pairs={{0,4},{2,6},{4,0},{6,2},{8,12},{10,14},{12,8},{14,10},{16,20},{18,... | collective-permute-start | bytes 196616 | tf_op jit(solution)/shard_map/ppermute | solution.py:371
  85.5 4.8 %collective-permute-start.21 = (bf16[128,256]{1,0:T(8,128)(2,1)S(1)}, bf16[128,256]{1,0:T(8,128)(2,1)S(1)}, u32[]{:S(2)}, u32[]{:S(2)}) collective-permute-start(bf16[128,256]{1,0:T(8,128)(2,1)S(1)} %get-tuple-element.74), channel_id=1, source_target_pairs={{0,2},{2,0},{4,6},{6,4},{8,10},{10,8},{12,14},{14,12},{16,18},{18,... | collective-permute-start | bytes 196616 | tf_op jit(solution)/shard_map/ppermute | solution.py:371
  91.1 4.3 %collective-permute-start.22 = (bf16[256,128]{1,0:T(8,128)(2,1)S(1)}, bf16[256,128]{1,0:T(8,128)(2,1)S(1)}, u32[]{:S(2)}, u32[]{:S(2)}) collective-permute-start(bf16[256,128]{1,0:T(8,128)(2,1)S(1)} %shard_map.81.mine), channel_id=1, source_target_pairs={{0,1},{1,0},{2,3},{3,2},{4,5},{5,4},{6,7},{7,6},{8,9},{9,8},{10,11... | collective-permute-start | bytes 196616 | tf_op jit(solution)/shard_map/ppermute | solution.py:306

commit v3 on v2

--- a/solution.py
+++ b/solution.py
@@ -92,7 +92,7 @@
     outs, (rows, blocks, sems, out_sems) = refs[:-4], refs[-4:]
     messages, outs = outs[: NEAR - 1], outs[NEAR - 1 :]
     own, stage, recent, inverse = outs[:4]
-    rest = outs[4:]
+    (rest,) = outs[4:]
     band, tile_len, shots = history.shape
     lag = lax.axis_index("lag")
     offsets = slot_offsets(lax.axis_index("patch"))
@@ -178,8 +178,7 @@
         )
         for j in range(NEAR - 1):
             pl.when(slot == j)(lambda j=j: send(j, 0, messages[j]).start())
-        for step in range(1, steps):
-            send(slot, step, rest[step - 1].at[pl.ds(slot * shots, shots)]).start()
+        send(slot, 1, rest.at[pl.ds(slot * shots, shots)]).start()
         return carry
 
     lax.fori_loop(0, NEAR, one_slot, None)
@@ -188,35 +187,42 @@
     for slot in range(NEAR):
         if slot < NEAR - 1:
             send(slot, 0, messages[slot]).wait()
-        for step in range(1, steps):
-            send(slot, step, rest[step - 1].at[pl.ds(slot * shots, shots)]).wait()
+        send(slot, 1, rest.at[pl.ds(slot * shots, shots)]).wait()
 
 
 def step_kernel(step, last_step, ranges, source, inverse, own, *refs):
-    shots = own.shape[0]
-    tile_len = own.shape[1]
+    shots, tile_len = own.shape
     refs = list(refs)
-    received = [refs.pop(0) for _ in range(1 if step == 0 else NEAR - 1)]
-    right = source[...] - own[...]
+    received = [refs.pop(0) for _ in range(NEAR - 1 if step > 0 else 0)]
+    total = own[...]
     for block in received:
-        right = right - block[...].astype(jnp.float32)
+        total = total + block[...].astype(jnp.float32)
+    right = source[...] - total
+    if step != 1:
+        right = right - refs.pop(0)[...].astype(jnp.float32)
     density = dot(right.astype(jnp.bfloat16), inverse[...])
+    rounded = density.astype(jnp.bfloat16)
     if last_step:
-        (natural,) = refs
-        natural[...] = density.T.astype(jnp.bfloat16)
+        refs[0][...] = rounded
         return
-    weights, stage, rest_far = refs[:3]
-    olders, outs = refs[3 : 3 + step], refs[3 + step :]
-    density_ref, next_own = outs[:2]
-    messages = outs[2:]
-    rounded = density.astype(jnp.bfloat16)
+    weights, stage = refs[:2]
+    rest_far = refs[2] if step == 0 else None
+    refs = refs[3 if step == 0 else 2 :]
+    olders, outs = refs[:step], refs[step:]
+    density_ref, cross, next_own = outs[:3]
+    messages = outs[3:]
+    band_zero = lax.axis_index("lag") == 0
     density_ref[...] = rounded
-    band_zero = lax.axis_index("lag") == 0
+    cross[...] = jnp.where(band_zero, density, total).astype(jnp.bfloat16)
     recent = [rounded] + [ref[...] for ref in olders]
-    nxt = step + 1
+    steps = stage.shape[1] // shots
+    ahead = jnp.where(band_zero, step + 1, min(step + 2, steps - 1))
+    rows = pl.ds(pl.multiple_of(ahead * shots, shots), shots)
     for slot, offset in enumerate(slot_offsets(lax.axis_index("patch"))):
-        terms = stage[slot, nxt * shots : (nxt + 1) * shots, :].astype(jnp.float32)
-        terms = terms + rest_far[slot * shots : (slot + 1) * shots, :].astype(jnp.float32)
+        terms = stage[slot, rows, :].astype(jnp.float32)
+        if step == 0:
+            there = rest_far[slot * shots : (slot + 1) * shots, :].astype(jnp.float32)
+            terms = terms + jnp.where(band_zero, there, 0.0)
         columns = pl.ds(pl.multiple_of(offset * tile_len, tile_len), tile_len)
         for k, block in enumerate(recent):
             lag = k + 1
@@ -229,34 +235,25 @@
             next_own[...] = terms
 
 
-def natural_kernel(*refs):
-    blocks, out = refs[:-1], refs[-1]
-    for k, block in enumerate(blocks):
-        out[k] = block[...].astype(jnp.float32).T.astype(jnp.bfloat16)
-
-
-def early_kernel(near_lags, mine, far, out, sem):
-    def move(block):
-        copy = pltpu.make_async_copy(block, out.at[pl.ds(0, block.shape[0])], sem)
-        copy.start()
-        copy.wait()
-
+def begin_kernel(near_lags, *refs):
+    count = (len(refs) - 3) // 2
+    mine, far, (out, rows, sem) = refs[:count], refs[count : 2 * count], refs[2 * count :]
     keeps = lax.axis_index("lag") < near_lags
-    pl.when(keeps)(lambda: move(mine))
-    pl.when(jnp.logical_not(keeps))(lambda: move(far))
-
-
-def late_kernel(near_lags, begun, mine, far, out, sem):
+    for k in range(count):
+        block = jnp.where(keeps, mine[k][...], far[k][...])
+        rows[k] = block.astype(jnp.float32).T.astype(jnp.bfloat16)
+    copy = pltpu.make_async_copy(rows, out.at[pl.ds(0, count)], sem)
+    copy.start()
+    copy.wait()
+
+
+def finish_kernel(near_lags, begun, mine, far, out, rows, sem):
     del begun
-
-    def move(block):
-        copy = pltpu.make_async_copy(block, out.at[out.shape[0] - 1], sem)
-        copy.start()
-        copy.wait()
-
-    keeps = lax.axis_index("lag") < near_lags
-    pl.when(keeps)(lambda: move(mine))
-    pl.when(jnp.logical_not(keeps))(lambda: move(far))
+    block = jnp.where(lax.axis_index("lag") < near_lags, mine[...], far[...])
+    rows[...] = block.astype(jnp.float32).T.astype(jnp.bfloat16)
+    copy = pltpu.make_async_copy(rows, out.at[out.shape[0] - 1], sem)
+    copy.start()
+    copy.wait()
 
 
 def call(kernel, outs, specs, scratch=(), out_specs=None, aliases=None, limit=8 << 20):
@@ -351,7 +348,7 @@
             ((steps - 1, tile_len, NEAR * tile_len), bf16, VMEM),
             ((tile_len, tile_len), bf16, VMEM),
         ]
-        + [((NEAR * shots, tile_len), bf16)] * (steps - 1),
+        + [((NEAR * shots, tile_len), bf16)],
         [pltpu.SMEM, VMEM, VMEM, pltpu.HBM, pltpu.HBM],
         [
             VMEM(((band + steps - 1) * shots, tile_len), bf16),
@@ -359,10 +356,10 @@
             pltpu.SemaphoreType.DMA((NEAR, band)),
             pltpu.SemaphoreType.DMA((NEAR + 1, steps)),
         ],
-        out_specs=[pl.ANY] * (NEAR - 1) + [VMEM] * 4 + [pl.ANY] * (steps - 1),
+        out_specs=[pl.ANY] * (NEAR - 1) + [VMEM] * 4 + [pl.ANY],
         limit=54 << 20,
     )(lag_ranges, rim, history, far_memory(near_inverse), far_memory(interaction))
-    messages, (own, stage, recent, inverse), rest = older[: NEAR - 1], older[NEAR - 1 : NEAR + 3], older[NEAR + 3 :]
+    messages, (own, stage, recent, inverse, rest) = older[: NEAR - 1], older[NEAR - 1 :]
     stage, recent, inverse = near_memory(stage), near_memory(recent), near_memory(inverse)
 
     def exchange(blocks):
@@ -374,53 +371,64 @@
     for incoming in exchange(messages):
         own = own + incoming.astype(f32)
     own, far = lag_sum(own, lags)
-    received = [far]
-    pairs = []
-    for r in rest:
-        pairs.append(lag_sum(r, lags))
-
-    densities = []
+    here, there = lag_sum(rest, lags)
+    if lags > 2:
+        there = there + (here - rest)
+
+    def cross_bands(block):
+        if lags == 2:
+            swapped = lax.ppermute(block, "lag", lag_partners(lags, 1))
+            return (block, swapped), swapped
+        outward = from_band_zero(block, lags)
+        inward, last = lag_sum(jnp.where(lax.axis_index("lag") > 0, block, 0), lags)
+        return outward, inward + last
+
+    densities, outward, inward = [], [], [far]
+    received = []
     for step in range(steps):
         last_step = step == steps - 1
         inputs = [lag_ranges, source[step], inverse, own, *received]
-        if last_step:
-            outs = [((tile_len, shots), bf16)]
-        else:
-            here, there = pairs[step]
-            if lags > 2:
-                there = there + (here - rest[step])
-            inputs += [recent, stage, there, *densities[::-1]]
-            outs = [(block, bf16, VMEM), (block, f32, VMEM)] + [(block, bf16)] * (NEAR - 1)
+        if step != 1:
+            inputs.append(inward[max(step - 1, 0)])
+        outs = [(block, bf16)]
+        if not last_step:
+            inputs += [recent, stage] + [there] * (step == 0) + densities[::-1]
+            outs = [(block, bf16, VMEM), (block, bf16), (block, f32, VMEM)]
+            outs += [(block, bf16)] * (NEAR - 1)
         results = call(
             functools.partial(step_kernel, step, last_step),
             outs,
             [pltpu.SMEM] + [VMEM] * (len(inputs) - 1),
         )(*inputs)
-        if not last_step:
+        if last_step:
+            ends, _ = cross_bands(results[0])
+        else:
             densities.append(near_memory(results[0]))
-            own = near_memory(results[1])
-            received = exchange(results[2:])
-    (early,) = call(
-        natural_kernel, [((steps - 1, tile_len, shots), bf16)], [VMEM] * (steps - 1)
-    )(*densities)
-    early = from_band_zero(early, lags)
-    late = from_band_zero(results[0], lags)
+            sent, back = cross_bands(results[1])
+            outward.append(sent)
+            if step == 0:
+                inward = [far]
+            else:
+                inward.append(back)
+            own = near_memory(results[2])
+            received = exchange(results[3:])
     whole = ((steps, tile_len, shots), bf16)
+    pairs = [mine for mine, _ in outward] + [theirs for _, theirs in outward]
     (begun,) = call(
-        functools.partial(early_kernel, lags // 2),
+        functools.partial(begin_kernel, lags // 2),
         [whole],
-        [pl.ANY] * 2,
-        [pltpu.SemaphoreType.DMA],
+        [VMEM] * len(pairs),
+        [VMEM((steps - 1, tile_len, shots), bf16), pltpu.SemaphoreType.DMA],
         out_specs=[pl.ANY],
-    )(*early)
+    )(*pairs)
     (out,) = call(
-        functools.partial(late_kernel, lags // 2),
+        functools.partial(finish_kernel, lags // 2),
         [whole],
-        [pl.ANY] * 3,
-        [pltpu.SemaphoreType.DMA],
+        [pl.ANY, VMEM, VMEM],
+        [VMEM((tile_len, shots), bf16), pltpu.SemaphoreType.DMA],
         out_specs=[pl.ANY],
         aliases={0: 0},
-    )(begun, *late)
+    )(begun, *ends)
     return out
 
 

time: 96.5 us -> 81.2 us (0.84)
  waiting for transfers between devices: 43.9 us -> 29.1 us
    ppermute x4 -> x2, waiting for transfers between devices: 15.6 us -> 3.6 us  [lag_sum(): lax.ppermute(block.astype(jnp.bfloat16), 'lag', lag_partners(lags, distan...]
    ppermute x16, waiting for transfers between devices: 20 us -> 17.3 us  [exchange(): gone.append(lax.ppermute(b, 'patch', r))]
    ppermute x4 -> x2, starting transfers between devices: 3.48 us -> 1.46 us  [lag_sum(): lax.ppermute(block.astype(jnp.bfloat16), 'lag', lag_partners(lags, distan...]
    ppermute x2 -> x4, starting transfers between devices: 1.96 us -> 3.8 us  [cross_bands(): swapped = lax.ppermute(block, 'lag', lag_partners(lags, 1))]
    ppermute x2 -> x4, waiting for transfers between devices: 2.63 us -> 2.48 us  [cross_bands(): swapped = lax.ppermute(block, 'lag', lag_partners(lags, 1))]
where the time goes in v3:
time: 81.2 us; the launch traced here: 80.8 us
  starting transfers between devices  30.9 us (38%)
  waiting for transfers between devices  29.1 us (36%)
  Pallas kernels  18.4 us (23%)
  local copies, waits for them, and re-layouts  1.67 us (2%)
    ppermute x16, waiting for transfers between devices, exchange(): gone.append(lax.ppermute(b, 'patch', r))  17.3 us
    ppermute x16, starting transfers between devices, exchange(): gone.append(lax.ppermute(b, 'patch', r))  16.6 us
    pallas_call x1, Pallas kernels, local(): call(functools.partial(older_kernel, steps, sizes), [(block, bf16)] * (NE...  8.98 us
    all_to_all x1, starting transfers between devices, local(): lax.all_to_all(outgoing.reshape(patches, CAP, width + LANES), 'patch', sp...  7.47 us
    ppermute x1, waiting for transfers between devices, local(): rim = lax.ppermute(edge, 'lag', [(i, (i + 1) % lags) for i in range(lags)])  5.68 us
    pallas_call x4, Pallas kernels, local(): call(functools.partial(step_kernel, step, last_step), outs, [pltpu.SMEM]...  4.82 us
    ppermute x4, starting transfers between devices, cross_bands(): swapped = lax.ppermute(block, 'lag', lag_partners(lags, 1))  3.8 us
    ppermute x2, waiting for transfers between devices, lag_sum(): lax.ppermute(block.astype(jnp.bfloat16), 'lag', lag_partners(lags, distan...  3.6 us
  transfers between devices with their start and end apart: 24, of which 10 were waited for; matrix products, arithmetic and copies ran while one was open for 1% of the time, Pallas kernels for 15%

profile of v3, /device:TPU:0, one launch (start us, length us, event | category | flops | bytes accessed | tf_op | source)
XLA Modules:
  0.0 80.8 jit_solution(3880521114418227106)
XLA Ops:
  0.0 1.0 %copy.11 = bf16[32,8,4,128]{3,1,2,0:T(8,128)(2,1)S(1)} copy(bf16[32,8,4,128]{3,2,1,0:T(4,128)(2,1)} %bitcast.9) | data formatting | bytes 524288
  1.0 1.8 %shard_map.73 = (bf16[256,640]{1,0:T(8,128)(2,1)}, bf16[3,256,128]{2,1,0:T(8,128)(2,1)S(1)}) custom-call(s32[1,256]{1,0:T(1,128)} %bitcast.10, s32[1,256]{1,0:T(1,128)} %bitcast.11, bf16[15,256,128]{2,1,0:T(8,128)(2,1)} %history.3, bf16[256,512]{1,0:T(8,128)(2,1)S(1)} %bitcast.8), custom_call_target="tpu_custom_call" | custom-call | tf_op jit(solution)/shard_map/pallas_call | solution.py:318
  2.8 7.5 %all-to-all-start = ((bf16[16,16,640]{2,1,0:T(8,128)(2,1)}), bf16[16,16,640]{2,1,0:T(8,128)(2,1)}, u32[]{:S(2)}, u32[]{:S(2)}) async-start(bf16[16,16,640]{2,1,0:T(8,128)(2,1)} %bitcast.2), calls=%async_computation | async-start | bytes 655360 | tf_op jit(solution)/shard_map/all_to_all | solution.py:331
  10.3 1.6 %collective-permute-start = (bf16[3,256,128]{2,1,0:T(8,128)(2,1)S(1)}, bf16[3,256,128]{2,1,0:T(8,128)(2,1)S(1)}, u32[]{:S(2)}, u32[]{:S(2)}) collective-permute-start(bf16[3,256,128]{2,1,0:T(8,128)(2,1)S(1)} %get-tuple-element.42), channel_id=1, source_target_pairs={{0,1},{1,0},{2,3},{3,2},{4,5},{5,4},{6,7},{7,6},{8,9},{9,8},{10,11... | collective-permute-start | bytes 589832 | tf_op jit(solution)/shard_map/ppermute | solution.py:330
  11.9 5.7 %collective-permute-done.rim = bf16[3,256,128]{2,1,0:T(8,128)(2,1)S(1)} collective-permute-done((bf16[3,256,128]{2,1,0:T(8,128)(2,1)S(1)}, bf16[3,256,128]{2,1,0:T(8,128)(2,1)S(1)}, u32[]{:S(2)}, u32[]{:S(2)}) %collective-permute-start) | collective-permute-done | bytes 196640 | tf_op jit(solution)/shard_map/ppermute | solution.py:330
  18.2 9.0 %shard_map.75 = (bf16[128,256]{1,0:T(8,128)(2,1)}, bf16[128,256]{1,0:T(8,128)(2,1)}, bf16[128,256]{1,0:T(8,128)(2,1)}, bf16[128,256]{1,0:T(8,128)(2,1)}, f32[128...) custom-call(s32[1,10]{1,0:T(1,128)} %ranges.9, ...), custom_call_target="tpu_custom_call" | custom-call | tf_op jit(solution)/shard_map/pallas_call | solution.py:342
  27.2 3.7 %collective-permute-start.1 = (bf16[128,256]{1,0:T(8,128)(2,1)}, bf16[128,256]{1,0:T(8,128)(2,1)S(1)}, u32[]{:S(2)}, u32[]{:S(2)}) collective-permute-start(bf16[128,256]{1,0:T(8,128)(2,1)} %get-tuple-element.45), channel_id=1, source_target_pairs={{0,28},{2,30},{4,8},{6,10},{8,4},{10,6},{12,16},{14,18},{16,12},{1... | collective-permute-start | bytes 196616 | tf_op jit(solution)/shard_map/ppermute | solution.py:368
  31.3 1.5 %collective-permute-start.6 = (bf16[640,256]{1,0:T(8,128)(2,1)}, bf16[640,256]{1,0:T(8,128)(2,1)}, u32[]{:S(2)}, u32[]{:S(2)}) collective-permute-start(bf16[640,256]{1,0:T(8,128)(2,1)} %get-tuple-element.51), channel_id=1, source_target_pairs={{0,1},{1,0},{2,3},{3,2},{4,5},{5,4},{6,7},{7,6},{8,9},{9,8},{10,11... | collective-permute-start | bytes 983048 | tf_op jit(solution)/shard_map/ppermute | solution.py:291
  32.8 1.7 %collective-permute-done.1 = bf16[128,256]{1,0:T(8,128)(2,1)S(1)} collective-permute-done((bf16[128,256]{1,0:T(8,128)(2,1)}, bf16[128,256]{1,0:T(8,128)(2,1)S(1)}, u32[]{:S(2)}, u32[]{:S(2)}) %collective-permute-start.1) | collective-permute-done | bytes 65568 | tf_op jit(solution)/shard_map/ppermute | solution.py:368
  34.5 3.0 %collective-permute-done.2 = bf16[128,256]{1,0:T(8,128)(2,1)S(1)} collective-permute-done((bf16[128,256]{1,0:T(8,128)(2,1)}, bf16[128,256]{1,0:T(8,128)(2,1)S(1)}, u32[]{:S(2)}, u32[]{:S(2)}) %collective-permute-start.2) | collective-permute-done | bytes 65568 | tf_op jit(solution)/shard_map/ppermute | solution.py:368
  38.2 1.2 %shard_map.74 = (f32[128,256]{1,0:T(8,128)S(1)}, f32[128,256]{1,0:T(8,128)S(1)}, f32[128,256]{1,0:T(8,128)S(1)}, f32[128,256]{1,0:T(8,128)S(1)}) custom-call(bf16[256,640]{1,0:T(8,128)(2,1)} %bitcast.3.arrived_ref), custom_call_target="tpu_custom_call" | custom-call | tf_op jit(solution)/shard_map/pallas_call | solution.py:338
  39.5 3.6 %collective-permute-done.5.refs_0_ = bf16[128,256]{1,0:T(8,128)(2,1)} collective-permute-done((bf16[128,256]{1,0:T(8,128)(2,1)}, bf16[128,256]{1,0:T(8,128)(2,1)}, u32[]{:S(2)}, u32[]{:S(2)}) %collective-permute-start.5) | collective-permute-done | bytes 65568 | tf_op jit(solution)/shard_map/ppermute | solution.py:291
  43.1 1.4 %shard_map.76 = (bf16[128,256]{1,0:T(8,128)(2,1)S(1)}, bf16[128,256]{1,0:T(8,128)(2,1)S(1)}, f32[128,256]{1,0:T(8,128)S(1)}, bf16[128,256]{1,0:T(8,128)(2,1)S(1)...) custom-call(s32[1,10]{1,0:T(1,128)S(1)} %copy-done, ...), custom_call_target="tpu_custom_call" | custom-call | tf_op jit(solution)/shard_map/pallas_call | solution.py:398
  44.5 4.1 %collective-permute-start.7 = (bf16[128,256]{1,0:T(8,128)(2,1)S(1)}, bf16[128,256]{1,0:T(8,128)(2,1)S(1)}, u32[]{:S(2)}, u32[]{:S(2)}) collective-permute-start(bf16[128,256]{1,0:T(8,128)(2,1)S(1)} %get-tuple-element.55), channel_id=1, source_target_pairs={{0,28},{2,30},{4,8},{6,10},{8,4},{10,6},{12,16},{14,18},{16,12},{1... | collective-permute-start | bytes 196616 | tf_op jit(solution)/shard_map/ppermute | solution.py:368
  49.1 2.5 %collective-permute-done.7.refs_0_ = bf16[128,256]{1,0:T(8,128)(2,1)S(1)} collective-permute-done((bf16[128,256]{1,0:T(8,128)(2,1)S(1)}, bf16[128,256]{1,0:T(8,128)(2,1)S(1)}, u32[]{:S(2)}, u32[]{:S(2)}) %collective-permute-start.7) | collective-permute-done | bytes 65568 | tf_op jit(solution)/shard_map/ppermute | solution.py:368
  51.6 3.4 %collective-permute-done.8.refs_1_ = bf16[128,256]{1,0:T(8,128)(2,1)S(1)} collective-permute-done((bf16[128,256]{1,0:T(8,128)(2,1)S(1)}, bf16[128,256]{1,0:T(8,128)(2,1)S(1)}, u32[]{:S(2)}, u32[]{:S(2)}) %collective-permute-start.8) | collective-permute-done | bytes 65568 | tf_op jit(solution)/shard_map/ppermute | solution.py:368
  55.0 1.0 %shard_map.77 = (bf16[128,256]{1,0:T(8,128)(2,1)S(1)}, bf16[128,256]{1,0:T(8,128)(2,1)S(1)}, f32[128,256]{1,0:T(8,128)S(1)}, bf16[128,256]{1,0:T(8,128)(2,1)S(1)...) custom-call(s32[1,10]{1,0:T(1,128)S(1)} %copy-done, ...), custom_call_target="tpu_custom_call" | custom-call | tf_op jit(solution)/shard_map/pallas_call | solution.py:398
  56.7 0.9 %collective-permute-start.12 = (bf16[128,256]{1,0:T(8,128)(2,1)S(1)}, bf16[128,256]{1,0:T(8,128)(2,1)S(1)}, u32[]{:S(2)}, u32[]{:S(2)}) collective-permute-start(bf16[128,256]{1,0:T(8,128)(2,1)S(1)} %get-tuple-element.64), channel_id=1, source_target_pairs={{0,30},{2,4},{4,2},{6,8},{8,6},{10,12},{12,10},{14,16},{16,14},{18... | collective-permute-start | bytes 196616 | tf_op jit(solution)/shard_map/ppermute | solution.py:368
  57.6 1.7 %collective-permute-start.13 = (bf16[128,256]{1,0:T(8,128)(2,1)S(1)}, bf16[128,256]{1,0:T(8,128)(2,1)S(1)}, u32[]{:S(2)}, u32[]{:S(2)}) collective-permute-start(bf16[128,256]{1,0:T(8,128)(2,1)S(1)} %get-tuple-element.65), channel_id=1, source_target_pairs={{0,4},{2,6},{4,0},{6,2},{8,12},{10,14},{12,8},{14,10},{16,20},{18,... | collective-permute-start | bytes 196616 | tf_op jit(solution)/shard_map/ppermute | solution.py:368
  59.2 0.8 %collective-permute-start.15 = (bf16[128,256]{1,0:T(8,128)(2,1)S(1)}, bf16[128,256]{1,0:T(8,128)(2,1)S(1)}, u32[]{:S(2)}, u32[]{:S(2)}) collective-permute-start(bf16[128,256]{1,0:T(8,128)(2,1)S(1)} %get-tuple-element.60.refs_1_), channel_id=1, source_target_pairs={{0,1},{1,0},{2,3},{3,2},{4,5},{5,4},{6,7},{7,6},{8,9},{9,8},{10,11... | collective-permute-start | bytes 196616 | tf_op jit(solution)/shard_map/ppermute | solution.py:380
  60.1 3.7 %collective-permute-done.11.refs_0_ = bf16[128,256]{1,0:T(8,128)(2,1)S(1)} collective-permute-done((bf16[128,256]{1,0:T(8,128)(2,1)S(1)}, bf16[128,256]{1,0:T(8,128)(2,1)S(1)}, u32[]{:S(2)}, u32[]{:S(2)}) %collective-permute-start.11) | collective-permute-done | bytes 65568 | tf_op jit(solution)/shard_map/ppermute | solution.py:368
  63.8 1.7 %shard_map.78 = (bf16[128,256]{1,0:T(8,128)(2,1)}, bf16[128,256]{1,0:T(8,128)(2,1)S(1)}, f32[128,256]{1,0:T(8,128)S(1)}, bf16[128,256]{1,0:T(8,128)(2,1)S(1)}, b...) custom-call(s32[1,10]{1,0:T(1,128)S(1)} %copy-done, ...), custom_call_target="tpu_custom_call" | custom-call | tf_op jit(solution)/shard_map/pallas_call | solution.py:398
  65.4 3.2 %collective-permute-start.18 = (bf16[128,256]{1,0:T(8,128)(2,1)S(1)}, bf16[128,256]{1,0:T(8,128)(2,1)S(1)}, u32[]{:S(2)}, u32[]{:S(2)}) collective-permute-start(bf16[128,256]{1,0:T(8,128)(2,1)S(1)} %get-tuple-element.71), channel_id=1, source_target_pairs={{0,28},{2,30},{4,8},{6,10},{8,4},{10,6},{12,16},{14,18},{16,12},{1... | collective-permute-start | bytes 196616 | tf_op jit(solution)/shard_map/ppermute | solution.py:368
  69.1 1.0 %collective-permute-start.20 = (bf16[128,256]{1,0:T(8,128)(2,1)S(1)}, bf16[128,256]{1,0:T(8,128)(2,1)S(1)}, u32[]{:S(2)}, u32[]{:S(2)}) collective-permute-start(bf16[128,256]{1,0:T(8,128)(2,1)S(1)} %get-tuple-element.73), channel_id=1, source_target_pairs={{0,4},{2,6},{4,0},{6,2},{8,12},{10,14},{12,8},{14,10},{16,20},{18,... | collective-permute-start | bytes 196616 | tf_op jit(solution)/shard_map/ppermute | solution.py:368
  70.1 1.0 %collective-permute-start.17 = (bf16[128,256]{1,0:T(8,128)(2,1)S(1)}, bf16[128,256]{1,0:T(8,128)(2,1)S(1)}, u32[]{:S(2)}, u32[]{:S(2)}) collective-permute-start(bf16[128,256]{1,0:T(8,128)(2,1)S(1)} %get-tuple-element.68.refs_2_), channel_id=1, source_target_pairs={{0,1},{1,0},{2,3},{3,2},{4,5},{5,4},{6,7},{7,6},{8,9},{9,8},{10,11... | collective-permute-start | bytes 196616 | tf_op jit(solution)/shard_map/ppermute | solution.py:380
  71.1 1.4 %collective-permute-done.18.refs_0_ = bf16[128,256]{1,0:T(8,128)(2,1)S(1)} collective-permute-done((bf16[128,256]{1,0:T(8,128)(2,1)S(1)}, bf16[128,256]{1,0:T(8,128)(2,1)S(1)}, u32[]{:S(2)}, u32[]{:S(2)}) %collective-permute-start.18) | collective-permute-done | bytes 65568 | tf_op jit(solution)/shard_map/ppermute | solution.py:368
  72.5 0.9 %collective-permute-start.16 = (bf16[128,256]{1,0:T(8,128)(2,1)S(1)}, bf16[128,256]{1,0:T(8,128)(2,1)S(1)}, u32[]{:S(2)}, u32[]{:S(2)}) collective-permute-start(bf16[128,256]{1,0:T(8,128)(2,1)S(1)} %get-tuple-element.52.refs_0_), channel_id=1, source_target_pairs={{0,1},{1,0},{2,3},{3,2},{4,5},{5,4},{6,7},{7,6},{8,9},{9,8},{10,11... | collective-permute-start | bytes 196616 | tf_op jit(solution)/shard_map/ppermute | solution.py:380
  73.4 1.6 %collective-permute-done.19.refs_1_ = bf16[128,256]{1,0:T(8,128)(2,1)S(1)} collective-permute-done((bf16[128,256]{1,0:T(8,128)(2,1)S(1)}, bf16[128,256]{1,0:T(8,128)(2,1)S(1)}, u32[]{:S(2)}, u32[]{:S(2)}) %collective-permute-start.19) | collective-permute-done | bytes 65568 | tf_op jit(solution)/shard_map/ppermute | solution.py:368
  75.8 1.1 %collective-permute-start.22 = (bf16[128,256]{1,0:T(8,128)(2,1)S(1)}, bf16[128,256]{1,0:T(8,128)(2,1)S(1)}, u32[]{:S(2)}, u32[]{:S(2)}) collective-permute-start(bf16[128,256]{1,0:T(8,128)(2,1)S(1)} %shard_map.80.mine), channel_id=1, source_target_pairs={{0,1},{1,0},{2,3},{3,2},{4,5},{5,4},{6,7},{7,6},{8,9},{9,8},{10,11... | collective-permute-start | bytes 196616 | tf_op jit(solution)/shard_map/ppermute | solution.py:380
  76.8 0.8 %shard_map.79.begun = bf16[4,256,128]{2,1,0:T(8,128)(2,1)} custom-call(bf16[128,256]{1,0:T(8,128)(2,1)S(1)} %get-tuple-element.52.refs_0_, bf16[128,256]{1,0:T(8,128)(2,1)S(1)} %get-tuple-element.60.refs_1_, bf16[128,256]{1,0:T(8,128)(2,1)S(1)} %get-tuple-element.68.refs_2_, bf16[128,256]{1,0:T(8,128)(2,1)S(1)} %collective-permute-done.16.refs_3_, ...), custom_call_target="tpu_custom_call" | custom-call | tf_op jit(solution)/shard_map/pallas_call | solution.py:417
  77.7 2.4 %collective-permute-done.22.far = bf16[128,256]{1,0:T(8,128)(2,1)S(1)} collective-permute-done((bf16[128,256]{1,0:T(8,128)(2,1)S(1)}, bf16[128,256]{1,0:T(8,128)(2,1)S(1)}, u32[]{:S(2)}, u32[]{:S(2)}) %collective-permute-start.22) | collective-permute-done | bytes 65568 | tf_op jit(solution)/shard_map/ppermute | solution.py:380
  80.1 0.7 shard_map.81
  (31 shorter events, 4.2 us)
Async XLA Ops:
  2.8 35.4 %all-to-all-start = ((bf16[16,16,640]{2,1,0:T(8,128)(2,1)}), bf16[16,16,640]{2,1,0:T(8,128)(2,1)}, u32[]{:S(2)}, u32[]{:S(2)}) async-start(bf16[16,16,640]{2,1,0:T(8,128)(2,1)} %bitcast.2), calls=%async_computation | async-start | bytes 655360 | tf_op jit(solution)/shard_map/all_to_all | solution.py:331
  10.3 32.7 %copy-start = (s32[1,10]{1,0:T(1,128)S(1)}, s32[1,10]{1,0:T(1,128)}, u32[]{:S(2)}) copy-start(s32[1,10]{1,0:T(1,128)} %ranges.9) | copy-start | bytes 124
  10.3 7.2 %collective-permute-start = (bf16[3,256,128]{2,1,0:T(8,128)(2,1)S(1)}, bf16[3,256,128]{2,1,0:T(8,128)(2,1)S(1)}, u32[]{:S(2)}, u32[]{:S(2)}) collective-permute-start(bf16[3,256,128]{2,1,0:T(8,128)(2,1)S(1)} %get-tuple-element.42), channel_id=1, source_target_pairs={{0,1},{1,0},{2,3},{3,2},{4,5},{5,4},{6,7},{7,6},{8,9},{9,8},{10,11... | collective-permute-start | bytes 589832 | tf_op jit(solution)/shard_map/ppermute | solution.py:330
  17.6 0.7 copy-start.1
  27.2 7.3 %collective-permute-start.1 = (bf16[128,256]{1,0:T(8,128)(2,1)}, bf16[128,256]{1,0:T(8,128)(2,1)S(1)}, u32[]{:S(2)}, u32[]{:S(2)}) collective-permute-start(bf16[128,256]{1,0:T(8,128)(2,1)} %get-tuple-element.45), channel_id=1, source_target_pairs={{0,28},{2,30},{4,8},{6,10},{8,4},{10,6},{12,16},{14,18},{16,12},{1... | collective-permute-start | bytes 196616 | tf_op jit(solution)/shard_map/ppermute | solution.py:368
  30.9 6.6 %collective-permute-start.2 = (bf16[128,256]{1,0:T(8,128)(2,1)}, bf16[128,256]{1,0:T(8,128)(2,1)S(1)}, u32[]{:S(2)}, u32[]{:S(2)}) collective-permute-start(bf16[128,256]{1,0:T(8,128)(2,1)} %get-tuple-element.46), channel_id=1, source_target_pairs={{0,30},{2,4},{4,2},{6,8},{8,6},{10,12},{12,10},{14,16},{16,14},{18... | collective-permute-start | bytes 196616 | tf_op jit(solution)/shard_map/ppermute | solution.py:368
  30.9 6.6 %collective-permute-start.3 = (bf16[128,256]{1,0:T(8,128)(2,1)}, bf16[128,256]{1,0:T(8,128)(2,1)S(1)}, u32[]{:S(2)}, u32[]{:S(2)}) collective-permute-start(bf16[128,256]{1,0:T(8,128)(2,1)} %get-tuple-element.47), channel_id=1, source_target_pairs={{0,4},{2,6},{4,0},{6,2},{8,12},{10,14},{12,8},{14,10},{16,20},{18,... | collective-permute-start | bytes 196616 | tf_op jit(solution)/shard_map/ppermute | solution.py:368
  31.2 6.3 %collective-permute-start.4 = (bf16[128,256]{1,0:T(8,128)(2,1)}, bf16[128,256]{1,0:T(8,128)(2,1)S(1)}, u32[]{:S(2)}, u32[]{:S(2)}) collective-permute-start(bf16[128,256]{1,0:T(8,128)(2,1)} %get-tuple-element.48), channel_id=1, source_target_pairs={{0,2},{2,0},{4,6},{6,4},{8,10},{10,8},{12,14},{14,12},{16,18},{18,... | collective-permute-start | bytes 196616 | tf_op jit(solution)/shard_map/ppermute | solution.py:368
  31.3 11.7 %collective-permute-start.6 = (bf16[640,256]{1,0:T(8,128)(2,1)}, bf16[640,256]{1,0:T(8,128)(2,1)}, u32[]{:S(2)}, u32[]{:S(2)}) collective-permute-start(bf16[640,256]{1,0:T(8,128)(2,1)} %get-tuple-element.51), channel_id=1, source_target_pairs={{0,1},{1,0},{2,3},{3,2},{4,5},{5,4},{6,7},{7,6},{8,9},{9,8},{10,11... | collective-permute-start | bytes 983048 | tf_op jit(solution)/shard_map/ppermute | solution.py:291
  38.2 4.8 %collective-permute-start.5 = (bf16[128,256]{1,0:T(8,128)(2,1)}, bf16[128,256]{1,0:T(8,128)(2,1)}, u32[]{:S(2)}, u32[]{:S(2)}) collective-permute-start(bf16[128,256]{1,0:T(8,128)(2,1)} %get-tuple-element.75), channel_id=1, source_target_pairs={{0,1},{1,0},{2,3},{3,2},{4,5},{5,4},{6,7},{7,6},{8,9},{9,8},{10,11... | collective-permute-start | bytes 196616 | tf_op jit(solution)/shard_map/ppermute | solution.py:291
  44.5 7.1 %collective-permute-start.7 = (bf16[128,256]{1,0:T(8,128)(2,1)S(1)}, bf16[128,256]{1,0:T(8,128)(2,1)S(1)}, u32[]{:S(2)}, u32[]{:S(2)}) collective-permute-start(bf16[128,256]{1,0:T(8,128)(2,1)S(1)} %get-tuple-element.55), channel_id=1, source_target_pairs={{0,28},{2,30},{4,8},{6,10},{8,4},{10,6},{12,16},{14,18},{16,12},{1... | collective-permute-start | bytes 196616 | tf_op jit(solution)/shard_map/ppermute | solution.py:368
  48.6 6.4 %collective-permute-start.8 = (bf16[128,256]{1,0:T(8,128)(2,1)S(1)}, bf16[128,256]{1,0:T(8,128)(2,1)S(1)}, u32[]{:S(2)}, u32[]{:S(2)}) collective-permute-start(bf16[128,256]{1,0:T(8,128)(2,1)S(1)} %get-tuple-element.56), channel_id=1, source_target_pairs={{0,30},{2,4},{4,2},{6,8},{8,6},{10,12},{12,10},{14,16},{16,14},{18... | collective-permute-start | bytes 196616 | tf_op jit(solution)/shard_map/ppermute | solution.py:368
  48.6 6.4 %collective-permute-start.9 = (bf16[128,256]{1,0:T(8,128)(2,1)S(1)}, bf16[128,256]{1,0:T(8,128)(2,1)S(1)}, u32[]{:S(2)}, u32[]{:S(2)}) collective-permute-start(bf16[128,256]{1,0:T(8,128)(2,1)S(1)} %get-tuple-element.57), channel_id=1, source_target_pairs={{0,4},{2,6},{4,0},{6,2},{8,12},{10,14},{12,8},{14,10},{16,20},{18,... | collective-permute-start | bytes 196616 | tf_op jit(solution)/shard_map/ppermute | solution.py:368
  49.1 5.9 %collective-permute-start.10 = (bf16[128,256]{1,0:T(8,128)(2,1)S(1)}, bf16[128,256]{1,0:T(8,128)(2,1)S(1)}, u32[]{:S(2)}, u32[]{:S(2)}) collective-permute-start(bf16[128,256]{1,0:T(8,128)(2,1)S(1)} %get-tuple-element.58), channel_id=1, source_target_pairs={{0,2},{2,0},{4,6},{6,4},{8,10},{10,8},{12,14},{14,12},{16,18},{18,... | collective-permute-start | bytes 196616 | tf_op jit(solution)/shard_map/ppermute | solution.py:368
  56.0 7.7 %collective-permute-start.11 = (bf16[128,256]{1,0:T(8,128)(2,1)S(1)}, bf16[128,256]{1,0:T(8,128)(2,1)S(1)}, u32[]{:S(2)}, u32[]{:S(2)}) collective-permute-start(bf16[128,256]{1,0:T(8,128)(2,1)S(1)} %get-tuple-element.63), channel_id=1, source_target_pairs={{0,28},{2,30},{4,8},{6,10},{8,4},{10,6},{12,16},{14,18},{16,12},{1... | collective-permute-start | bytes 196616 | tf_op jit(solution)/shard_map/ppermute | solution.py:368
  56.7 7.1 %collective-permute-start.12 = (bf16[128,256]{1,0:T(8,128)(2,1)S(1)}, bf16[128,256]{1,0:T(8,128)(2,1)S(1)}, u32[]{:S(2)}, u32[]{:S(2)}) collective-permute-start(bf16[128,256]{1,0:T(8,128)(2,1)S(1)} %get-tuple-element.64), channel_id=1, source_target_pairs={{0,30},{2,4},{4,2},{6,8},{8,6},{10,12},{12,10},{14,16},{16,14},{18... | collective-permute-start | bytes 196616 | tf_op jit(solution)/shard_map/ppermute | solution.py:368
  57.6 6.2 %collective-permute-start.13 = (bf16[128,256]{1,0:T(8,128)(2,1)S(1)}, bf16[128,256]{1,0:T(8,128)(2,1)S(1)}, u32[]{:S(2)}, u32[]{:S(2)}) collective-permute-start(bf16[128,256]{1,0:T(8,128)(2,1)S(1)} %get-tuple-element.65), channel_id=1, source_target_pairs={{0,4},{2,6},{4,0},{6,2},{8,12},{10,14},{12,8},{14,10},{16,20},{18,... | collective-permute-start | bytes 196616 | tf_op jit(solution)/shard_map/ppermute | solution.py:368
  59.2 4.5 %collective-permute-start.14 = (bf16[128,256]{1,0:T(8,128)(2,1)S(1)}, bf16[128,256]{1,0:T(8,128)(2,1)S(1)}, u32[]{:S(2)}, u32[]{:S(2)}) collective-permute-start(bf16[128,256]{1,0:T(8,128)(2,1)S(1)} %get-tuple-element.66), channel_id=1, source_target_pairs={{0,2},{2,0},{4,6},{6,4},{8,10},{10,8},{12,14},{14,12},{16,18},{18,... | collective-permute-start | bytes 196616 | tf_op jit(solution)/shard_map/ppermute | solution.py:368
  59.2 4.5 %collective-permute-start.15 = (bf16[128,256]{1,0:T(8,128)(2,1)S(1)}, bf16[128,256]{1,0:T(8,128)(2,1)S(1)}, u32[]{:S(2)}, u32[]{:S(2)}) collective-permute-start(bf16[128,256]{1,0:T(8,128)(2,1)S(1)} %get-tuple-element.60.refs_1_), channel_id=1, source_target_pairs={{0,1},{1,0},{2,3},{3,2},{4,5},{5,4},{6,7},{7,6},{8,9},{9,8},{10,11... | collective-permute-start | bytes 196616 | tf_op jit(solution)/shard_map/ppermute | solution.py:380
  65.4 7.1 %collective-permute-start.18 = (bf16[128,256]{1,0:T(8,128)(2,1)S(1)}, bf16[128,256]{1,0:T(8,128)(2,1)S(1)}, u32[]{:S(2)}, u32[]{:S(2)}) collective-permute-start(bf16[128,256]{1,0:T(8,128)(2,1)S(1)} %get-tuple-element.71), channel_id=1, source_target_pairs={{0,28},{2,30},{4,8},{6,10},{8,4},{10,6},{12,16},{14,18},{16,12},{1... | collective-permute-start | bytes 196616 | tf_op jit(solution)/shard_map/ppermute | solution.py:368
  68.6 6.4 %collective-permute-start.19 = (bf16[128,256]{1,0:T(8,128)(2,1)S(1)}, bf16[128,256]{1,0:T(8,128)(2,1)S(1)}, u32[]{:S(2)}, u32[]{:S(2)}) collective-permute-start(bf16[128,256]{1,0:T(8,128)(2,1)S(1)} %get-tuple-element.72), channel_id=1, source_target_pairs={{0,30},{2,4},{4,2},{6,8},{8,6},{10,12},{12,10},{14,16},{16,14},{18... | collective-permute-start | bytes 196616 | tf_op jit(solution)/shard_map/ppermute | solution.py:368
  69.1 5.9 %collective-permute-start.20 = (bf16[128,256]{1,0:T(8,128)(2,1)S(1)}, bf16[128,256]{1,0:T(8,128)(2,1)S(1)}, u32[]{:S(2)}, u32[]{:S(2)}) collective-permute-start(bf16[128,256]{1,0:T(8,128)(2,1)S(1)} %get-tuple-element.73), channel_id=1, source_target_pairs={{0,4},{2,6},{4,0},{6,2},{8,12},{10,14},{12,8},{14,10},{16,20},{18,... | collective-permute-start | bytes 196616 | tf_op jit(solution)/shard_map/ppermute | solution.py:368
  70.1 4.9 %collective-permute-start.21 = (bf16[128,256]{1,0:T(8,128)(2,1)S(1)}, bf16[128,256]{1,0:T(8,128)(2,1)S(1)}, u32[]{:S(2)}, u32[]{:S(2)}) collective-permute-start(bf16[128,256]{1,0:T(8,128)(2,1)S(1)} %get-tuple-element.74), channel_id=1, source_target_pairs={{0,2},{2,0},{4,6},{6,4},{8,10},{10,8},{12,14},{14,12},{16,18},{18,... | collective-permute-start | bytes 196616 | tf_op jit(solution)/shard_map/ppermute | solution.py:368
  70.1 5.0 %collective-permute-start.17 = (bf16[128,256]{1,0:T(8,128)(2,1)S(1)}, bf16[128,256]{1,0:T(8,128)(2,1)S(1)}, u32[]{:S(2)}, u32[]{:S(2)}) collective-permute-start(bf16[128,256]{1,0:T(8,128)(2,1)S(1)} %get-tuple-element.68.refs_2_), channel_id=1, source_target_pairs={{0,1},{1,0},{2,3},{3,2},{4,5},{5,4},{6,7},{7,6},{8,9},{9,8},{10,11... | collective-permute-start | bytes 196616 | tf_op jit(solution)/shard_map/ppermute | solution.py:380
  72.5 4.3 %collective-permute-start.16 = (bf16[128,256]{1,0:T(8,128)(2,1)S(1)}, bf16[128,256]{1,0:T(8,128)(2,1)S(1)}, u32[]{:S(2)}, u32[]{:S(2)}) collective-permute-start(bf16[128,256]{1,0:T(8,128)(2,1)S(1)} %get-tuple-element.52.refs_0_), channel_id=1, source_target_pairs={{0,1},{1,0},{2,3},{3,2},{4,5},{5,4},{6,7},{7,6},{8,9},{9,8},{10,11... | collective-permute-start | bytes 196616 | tf_op jit(solution)/shard_map/ppermute | solution.py:380
  75.8 4.3 %collective-permute-start.22 = (bf16[128,256]{1,0:T(8,128)(2,1)S(1)}, bf16[128,256]{1,0:T(8,128)(2,1)S(1)}, u32[]{:S(2)}, u32[]{:S(2)}) collective-permute-start(bf16[128,256]{1,0:T(8,128)(2,1)S(1)} %shard_map.80.mine), channel_id=1, source_target_pairs={{0,1},{1,0},{2,3},{3,2},{4,5},{5,4},{6,7},{7,6},{8,9},{9,8},{10,11... | collective-permute-start | bytes 196616 | tf_op jit(solution)/shard_map/ppermute | solution.py:380

commit v4 on v3

--- a/solution.py
+++ b/solution.py
@@ -10,8 +10,11 @@
 NEAR = 5
 CAP = 16
 HALF = NEAR // 2
+FIRST = 2
 LANES = 128
 VMEM = pltpu.VMEM
+FAR_LIMIT = 40 << 20
+NEAR_LIMIT = 40 << 20
 
 
 def dot(left, right):
@@ -88,70 +91,32 @@
         )
 
 
-def older_kernel(steps, sizes, ranges, rim, history, inverse_hbm, weights, *refs):
-    outs, (rows, blocks, sems, out_sems) = refs[:-4], refs[-4:]
-    messages, outs = outs[: NEAR - 1], outs[NEAR - 1 :]
-    own, stage, recent, inverse = outs[:4]
-    (rest,) = outs[4:]
-    band, tile_len, shots = history.shape
+def active(ranges, offset, lag, band):
+    base = lag * band + 1
+    first = jnp.clip(ranges[0, offset] - base, 0, band)
+    last = jnp.clip(ranges[0, NEAR + offset] - base, 0, band)
+    return first, last
+
+
+def history_terms(ranges, slots, sizes, shots, rows, blocks, stage, arrive, emitted):
+    _, width, tile_len = stage.shape
+    band = blocks.shape[1]
     lag = lax.axis_index("lag")
     offsets = slot_offsets(lax.axis_index("patch"))
 
-    def bounds(offset):
-        base = lag * band + 1
-        first = jnp.clip(ranges[0, offset] - base, 0, band)
-        last = jnp.clip(ranges[0, NEAR + offset] - base, 0, band)
-        return first, last
-
-    def fetch(slot, offset, k):
-        columns = pl.ds(pl.multiple_of(offset * tile_len, tile_len), tile_len)
-        return pltpu.make_async_copy(
-            weights.at[k, :, columns], blocks.at[slot, k], sems.at[slot, k]
-        )
-
-    def send(slot, step, target):
-        return pltpu.make_async_copy(
-            stage.at[slot, pl.ds(step * shots, shots)], target, out_sems.at[slot, step]
-        )
-
-    for slot, offset in enumerate(offsets):
-        first, last = bounds(offset)
-        lax.fori_loop(first, last, lambda k, c, s=slot, o=offset: fetch(s, o, k).start(), None)
-    keep = [
-        pltpu.make_async_copy(weights.at[pl.ds(0, steps - 1)], recent, out_sems.at[NEAR, 0]),
-        pltpu.make_async_copy(inverse_hbm, inverse, out_sems.at[NEAR, 1]),
-    ]
-    for copy in keep:
-        copy.start()
-    for k in range(band):
-        rows[(band - 1 - k) * shots : (band - k) * shots, :] = history[k].T
-
-    @pl.when(lag > 0)
-    def _():
-        for k in range(steps - 1):
-            at = (band + steps - 2 - k) * shots
-            rows[at : at + shots, :] = rim[k].T
-
-    @pl.when(lag == 0)
-    def _():
-        rows[band * shots :, :] = jnp.zeros(((steps - 1) * shots, tile_len), jnp.bfloat16)
-
     def window(k):
-        return rows[pl.ds(pl.multiple_of((band - 1 - k) * shots, shots), steps * shots), :]
-
-    def one_slot(slot, carry):
-        offset = offsets[-1]
-        for j in range(NEAR - 1):
-            offset = jnp.where(slot == j, offsets[j], offset)
-        first, last = bounds(offset)
-        lax.fori_loop(first, last, lambda k, c: fetch(slot, offset, k).wait(), None)
+        return rows[pl.ds(pl.multiple_of((band - 1 - k) * shots, shots), width), :]
+
+    def one_slot(index, carry):
+        offset = offsets[slots[-1]]
+        for i, slot in enumerate(slots[:-1]):
+            offset = jnp.where(index == i, offsets[slot], offset)
+        first, last = active(ranges, offset, lag, band)
+        arrive(index, first, last, offset)
 
         def emit(total):
-            stage[slot] = total.astype(jnp.bfloat16)
-
-            @pl.when(slot == NEAR - 1)
-            def _():
-                own[...] = total[:shots]
+            stage[index] = total.astype(jnp.bfloat16)
+            emitted(index, total)
 
         def branch(size):
             def run():
@@ -160,7 +125,7 @@
                 for i in range(size):
                     k = start + i
                     live = (k >= first) & (k < last)
-                    tile = blocks[slot, k]
+                    tile = blocks[index, k]
                     left.append(window(k))
                     right.append(jnp.where(live, tile, jnp.zeros_like(tile)))
                 emit(dot(jnp.concatenate(left, axis=1), jnp.concatenate(right, axis=0)))
@@ -173,21 +138,119 @@
             which = jnp.where(count > size, i + 2, which)
         lax.switch(
             which,
-            [lambda: emit(jnp.zeros((steps * shots, tile_len), jnp.float32))]
+            [lambda: emit(jnp.zeros((width, tile_len), jnp.float32))]
             + [branch(size) for size in sizes],
         )
-        for j in range(NEAR - 1):
-            pl.when(slot == j)(lambda j=j: send(j, 0, messages[j]).start())
-        send(slot, 1, rest.at[pl.ds(slot * shots, shots)]).start()
         return carry
 
-    lax.fori_loop(0, NEAR, one_slot, None)
-    for copy in keep:
-        copy.wait()
+    lax.fori_loop(0, len(slots), one_slot, None)
+
+
+def far_kernel(steps, sizes, ranges, rim, history_hbm, inverse_hbm, weights, *refs):
+    far_message, odd_message, stage, rows, later, recent, inverse = refs[:7]
+    blocks, history, sems, keep_sems, out_sems = refs[7:]
+    band, tile_len, shots = history.shape
+    lag = lax.axis_index("lag")
+    offsets = slot_offsets(lax.axis_index("patch"))
+
+    def fetch(slot, offset, k):
+        columns = pl.ds(pl.multiple_of(offset * tile_len, tile_len), tile_len)
+        place = blocks.at[slot, k] if slot < FIRST else later.at[slot - FIRST, k]
+        return pltpu.make_async_copy(weights.at[k, :, columns], place, sems.at[slot, k])
+
+    keep = [
+        pltpu.make_async_copy(history_hbm, history, keep_sems.at[0]),
+        pltpu.make_async_copy(weights.at[pl.ds(0, steps - 1)], recent, keep_sems.at[1]),
+        pltpu.make_async_copy(inverse_hbm, inverse, keep_sems.at[2]),
+    ]
+    keep[0].start()
+    for slot, offset in enumerate(offsets):
+        first, last = active(ranges, offset, lag, band)
+        lax.fori_loop(first, last, lambda k, c, s=slot, o=offset: fetch(s, o, k).start(), None)
+    keep[1].start()
+    keep[2].start()
+    keep[0].wait()
+    for k in range(band):
+        rows[(band - 1 - k) * shots : (band - k) * shots, :] = history[k].T
+
+    @pl.when(lag > 0)
+    def _():
+        for k in range(steps - 1):
+            at = (band + steps - 2 - k) * shots
+            rows[at : at + shots, :] = rim[k].T
+
+    @pl.when(lag == 0)
+    def _():
+        rows[band * shots :, :] = jnp.zeros(((steps - 1) * shots, tile_len), jnp.bfloat16)
+
+    def arrive(index, first, last, offset):
+        def wait(k, carry):
+            columns = pl.ds(pl.multiple_of(offset * tile_len, tile_len), tile_len)
+            pltpu.make_async_copy(
+                weights.at[k, :, columns], blocks.at[index, k], sems.at[index, k]
+            ).wait()
+            return carry
+
+        lax.fori_loop(first, last, wait, None)
+
+    targets = (far_message, odd_message)
+
+    def send(index):
+        return pltpu.make_async_copy(
+            stage.at[index, pl.ds(0, shots)], targets[index], out_sems.at[index]
+        )
+
+    def emitted(index, total):
+        for i in range(FIRST):
+            pl.when(index == i)(lambda i=i: send(i).start())
+
+    history_terms(ranges, range(FIRST), sizes, shots, rows, blocks, stage, arrive, emitted)
+    for slot in range(FIRST, NEAR):
+        first, last = active(ranges, offsets[slot], lag, band)
+        lax.fori_loop(first, last, lambda k, c, s=slot: fetch(s, offsets[s], k).wait(), None)
+    keep[1].wait()
+    keep[2].wait()
+    for index in range(FIRST):
+        send(index).wait()
+
+
+def near_kernel(sizes, ranges, rows, blocks, far_stage, *refs):
+    near_message, core_message, own, stage, rest, out_sems = refs
+    shots = own.shape[0]
+    targets = (near_message, core_message)
+
+    def pass_on(slot):
+        held = far_stage.at[slot] if slot < FIRST else stage.at[slot - FIRST]
+        return pltpu.make_async_copy(
+            held.at[pl.ds(shots, shots)], rest.at[pl.ds(slot * shots, shots)], out_sems.at[0, slot]
+        )
+
+    def send(index):
+        return pltpu.make_async_copy(
+            stage.at[index, pl.ds(0, shots)], targets[index], out_sems.at[1, index]
+        )
+
+    for slot in range(FIRST):
+        pass_on(slot).start()
+
+    def emitted(index, total):
+        for i in range(NEAR - FIRST):
+
+            @pl.when(index == i)
+            def _(i=i):
+                pass_on(FIRST + i).start()
+                if i < len(targets):
+                    send(i).start()
+                else:
+                    own[...] = total[:shots]
+
+    history_terms(
+        ranges, range(FIRST, NEAR), sizes, shots, rows, blocks, stage, lambda *_: None, emitted
+    )
     for slot in range(NEAR):
-        if slot < NEAR - 1:
-            send(slot, 0, messages[slot]).wait()
-        send(slot, 1, rest.at[pl.ds(slot * shots, shots)]).wait()
+        pass_on(slot).wait()
+    for index in range(len(targets)):
+        send(index).wait()
 
 
 def step_kernel(step, last_step, ranges, source, inverse, own, *refs):
@@ -205,21 +268,23 @@
     if last_step:
         refs[0][...] = rounded
         return
-    weights, stage = refs[:2]
-    rest_far = refs[2] if step == 0 else None
-    refs = refs[3 if step == 0 else 2 :]
+    weights, far_stage, near_stage = refs[:3]
+    rest_far = refs[3] if step == 0 else None
+    refs = refs[4 if step == 0 else 3 :]
     olders, outs = refs[:step], refs[step:]
-    density_ref, cross, next_own = outs[:3]
-    messages = outs[3:]
+    cross, next_own = outs[:2]
+    messages = outs[2 : NEAR + 1]
     band_zero = lax.axis_index("lag") == 0
-    density_ref[...] = rounded
+    for density_ref in outs[NEAR + 1 :]:
+        density_ref[...] = rounded
     cross[...] = jnp.where(band_zero, density, total).astype(jnp.bfloat16)
     recent = [rounded] + [ref[...] for ref in olders]
-    steps = stage.shape[1] // shots
+    steps = far_stage.shape[1] // shots
     ahead = jnp.where(band_zero, step + 1, min(step + 2, steps - 1))
     rows = pl.ds(pl.multiple_of(ahead * shots, shots), shots)
     for slot, offset in enumerate(slot_offsets(lax.axis_index("patch"))):
-        terms = stage[slot, rows, :].astype(jnp.float32)
+        held = far_stage.at[slot] if slot < FIRST else near_stage.at[slot - FIRST]
+        terms = held[rows, :].astype(jnp.float32)
         if step == 0:
             there = rest_far[slot * shots : (slot + 1) * shots, :].astype(jnp.float32)
             terms = terms + jnp.where(band_zero, there, 0.0)
@@ -339,28 +404,45 @@
     source = [near_memory(s) for s in source]
 
     sizes = [*range(2, band, 2), band]
-    older = call(
-        functools.partial(older_kernel, steps, sizes),
-        [(block, bf16)] * (NEAR - 1)
+    older_rows = ((band + steps - 1) * shots, tile_len)
+    *first, far_stage, rows, later, recent, inverse = call(
+        functools.partial(far_kernel, steps, sizes),
+        [(block, bf16, pltpu.HBM)] * FIRST
         + [
-            (block, f32, VMEM),
-            ((NEAR, width, tile_len), bf16, VMEM),
+            ((FIRST, width, tile_len), bf16, VMEM),
+            (older_rows, bf16, VMEM),
+            ((NEAR - FIRST, band, tile_len, tile_len), bf16, VMEM),
             ((steps - 1, tile_len, NEAR * tile_len), bf16, VMEM),
             ((tile_len, tile_len), bf16, VMEM),
-        ]
-        + [((NEAR * shots, tile_len), bf16)],
-        [pltpu.SMEM, VMEM, VMEM, pltpu.HBM, pltpu.HBM],
+        ],
+        [pltpu.SMEM, VMEM] + [pltpu.HBM] * 3,
         [
-            VMEM(((band + steps - 1) * shots, tile_len), bf16),
-            VMEM((NEAR, band, tile_len, tile_len), bf16),
+            VMEM((FIRST, band, tile_len, tile_len), bf16),
+            VMEM((band, tile_len, shots), bf16),
             pltpu.SemaphoreType.DMA((NEAR, band)),
-            pltpu.SemaphoreType.DMA((NEAR + 1, steps)),
+            pltpu.SemaphoreType.DMA((3,)),
+            pltpu.SemaphoreType.DMA((FIRST,)),
         ],
-        out_specs=[pl.ANY] * (NEAR - 1) + [VMEM] * 4 + [pl.ANY],
-        limit=54 << 20,
-    )(lag_ranges, rim, history, far_memory(near_inverse), far_memory(interaction))
-    messages, (own, stage, recent, inverse, rest) = older[: NEAR - 1], older[NEAR - 1 :]
-    stage, recent, inverse = near_memory(stage), near_memory(recent), near_memory(inverse)
+        out_specs=[pltpu.HBM] * FIRST + [VMEM] * 5,
+        limit=FAR_LIMIT,
+    )(far_memory(lag_ranges), rim, far_memory(history), far_memory(near_inverse), far_memory(interaction))
+    far_stage, rows, later = near_memory(far_stage), near_memory(rows), near_memory(later)
+    recent, inverse = near_memory(recent), near_memory(inverse)
+    *second, own, near_stage, rest = call(
+        functools.partial(near_kernel, sizes),
+        [(block, bf16, pltpu.HBM)] * (NEAR - 1 - FIRST)
+        + [
+            (block, f32),
+            ((NEAR - FIRST, width, tile_len), bf16, VMEM),
+            ((NEAR * shots, tile_len), bf16, pltpu.HBM),
+        ],
+        [pltpu.SMEM] + [VMEM] * 3,
+        [pltpu.SemaphoreType.DMA((2, NEAR))],
+        out_specs=[pltpu.HBM] * (NEAR - 1 - FIRST) + [VMEM] * 2 + [pltpu.HBM],
+        limit=NEAR_LIMIT,
+    )(lag_ranges, rows, later, far_stage)
+    near_stage = near_memory(near_stage)
+    messages = [*first, *second]
 
     def exchange(blocks):
         gone = []
@@ -392,9 +474,9 @@
             inputs.append(inward[max(step - 1, 0)])
         outs = [(block, bf16)]
         if not last_step:
-            inputs += [recent, stage] + [there] * (step == 0) + densities[::-1]
-            outs = [(block, bf16, VMEM), (block, bf16), (block, f32, VMEM)]
-            outs += [(block, bf16)] * (NEAR - 1)
+            inputs += [recent, far_stage, near_stage] + [there] * (step == 0) + densities[::-1]
+            outs = [(block, bf16), (block, f32, VMEM)] + [(block, bf16)] * (NEAR - 1)
+            outs += [(block, bf16, VMEM)] * (step < steps - 2)
         results = call(
             functools.partial(step_kernel, step, last_step),
             outs,
@@ -403,15 +485,15 @@
         if last_step:
             ends, _ = cross_bands(results[0])
         else:
-            densities.append(near_memory(results[0]))
-            sent, back = cross_bands(results[1])
+            densities += [near_memory(r) for r in results[NEAR + 1 :]]
+            sent, back = cross_bands(results[0])
             outward.append(sent)
             if step == 0:
                 inward = [far]
             else:
                 inward.append(back)
-            own = near_memory(results[2])
-            received = exchange(results[3:])
+            own = near_memory(results[1])
+            received = exchange(results[2 : NEAR + 1])
     whole = ((steps, tile_len, shots), bf16)
     pairs = [mine for mine, _ in outward] + [theirs for _, theirs in outward]
     (begun,) = call(

time: 81.2 us -> 80.9 us (level)
  starting transfers between devices: 30.9 us -> 34.9 us
  waiting for transfers between devices: 29.1 us -> 25.2 us
    ppermute x2, starting transfers between devices: 1.46 us -> 3.81 us  [lag_sum(): lax.ppermute(block.astype(jnp.bfloat16), 'lag', lag_partners(lags, distan...]
    ppermute x16, waiting for transfers between devices: 17.3 us -> 15.5 us  [exchange(): gone.append(lax.ppermute(b, 'patch', r))]
    ppermute x2, waiting for transfers between devices: 3.6 us -> 2.09 us  [lag_sum(): lax.ppermute(block.astype(jnp.bfloat16), 'lag', lag_partners(lags, distan...]
    ppermute x16, starting transfers between devices: 16.6 us -> 17.9 us  [exchange(): gone.append(lax.ppermute(b, 'patch', r))]
    unnamed x5 -> x7, local copies, waits for them, and re-layouts: 1.67 us -> 1 us
    pallas_call x1 -> x2, Pallas kernels: 8.98 us -> 9.54 us  [the longest x1 5.34 us: local(): call(functools.partial(far_kernel, steps, sizes), [(block, bf16, pltpu.HB...]
  transfers between devices with their start and end apart: 24 -> 24, of which waited for: 10 -> 11; matrix products, arithmetic and copies ran while one was open for 1% -> 1% of each run, Pallas kernels for 15% -> 15%
where the time goes in v4:
time: 80.9 us; the launch traced here: 80.6 us
  starting transfers between devices  34.9 us (43%)
  waiting for transfers between devices  25.2 us (31%)
  Pallas kernels  18.5 us (23%)
  local copies, waits for them, and re-layouts  1 us (1%)
    ppermute x16, starting transfers between devices, exchange(): gone.append(lax.ppermute(b, 'patch', r))  17.9 us
    ppermute x16, waiting for transfers between devices, exchange(): gone.append(lax.ppermute(b, 'patch', r))  15.5 us
    all_to_all x1, starting transfers between devices, local(): lax.all_to_all(outgoing.reshape(patches, CAP, width + LANES), 'patch', sp...  7.47 us
    ppermute x1, waiting for transfers between devices, local(): rim = lax.ppermute(edge, 'lag', [(i, (i + 1) % lags) for i in range(lags)])  5.62 us
    pallas_call x1, Pallas kernels, local(): call(functools.partial(far_kernel, steps, sizes), [(block, bf16, pltpu.HB...  5.34 us
    pallas_call x4, Pallas kernels, local(): call(functools.partial(step_kernel, step, last_step), outs, [pltpu.SMEM]...  4.29 us
    pallas_call x1, Pallas kernels, local(): call(functools.partial(near_kernel, sizes), [(block, bf16, pltpu.HBM)] *...  4.2 us
    ppermute x4, starting transfers between devices, cross_bands(): swapped = lax.ppermute(block, 'lag', lag_partners(lags, 1))  4.11 us
  transfers between devices with their start and end apart: 24, of which 11 were waited for; matrix products, arithmetic and copies ran while one was open for 1% of the time, Pallas kernels for 15%

profile of v4, /device:TPU:0, one launch (start us, length us, event | category | flops | bytes accessed | tf_op | source)
XLA Modules:
  0.0 80.6 jit_solution(1307471123773664724)
XLA Ops:
  0.0 1.0 %copy.11 = bf16[32,8,4,128]{3,1,2,0:T(8,128)(2,1)S(1)} copy(bf16[32,8,4,128]{3,2,1,0:T(4,128)(2,1)} %bitcast.9) | data formatting | bytes 524288
  1.0 1.8 %shard_map.73 = (bf16[256,640]{1,0:T(8,128)(2,1)}, bf16[3,256,128]{2,1,0:T(8,128)(2,1)S(1)}) custom-call(s32[1,256]{1,0:T(1,128)} %bitcast.10, s32[1,256]{1,0:T(1,128)} %bitcast.11, bf16[15,256,128]{2,1,0:T(8,128)(2,1)} %history_hbm.1, bf16[256,512]{1,0:T(8,128)(2,1)S(1)} %bitcast.8), custom_call_target="tpu_custom_call" | custom-call | tf_op jit(solution)/shard_map/pallas_call | solution.py:383
  2.8 7.5 %all-to-all-start = ((bf16[16,16,640]{2,1,0:T(8,128)(2,1)}), bf16[16,16,640]{2,1,0:T(8,128)(2,1)}, u32[]{:S(2)}, u32[]{:S(2)}) async-start(bf16[16,16,640]{2,1,0:T(8,128)(2,1)} %bitcast.2), calls=%async_computation | async-start | bytes 655360 | tf_op jit(solution)/shard_map/all_to_all | solution.py:396
  10.3 1.6 %collective-permute-start = (bf16[3,256,128]{2,1,0:T(8,128)(2,1)S(1)}, bf16[3,256,128]{2,1,0:T(8,128)(2,1)S(1)}, u32[]{:S(2)}, u32[]{:S(2)}) collective-permute-start(bf16[3,256,128]{2,1,0:T(8,128)(2,1)S(1)} %get-tuple-element.45), channel_id=1, source_target_pairs={{0,1},{1,0},{2,3},{3,2},{4,5},{5,4},{6,7},{7,6},{8,9},{9,8},{10,11... | collective-permute-start | bytes 589832 | tf_op jit(solution)/shard_map/ppermute | solution.py:395
  11.9 5.6 %collective-permute-done.rim = bf16[3,256,128]{2,1,0:T(8,128)(2,1)S(1)} collective-permute-done((bf16[3,256,128]{2,1,0:T(8,128)(2,1)S(1)}, bf16[3,256,128]{2,1,0:T(8,128)(2,1)S(1)}, u32[]{:S(2)}, u32[]{:S(2)}) %collective-permute-start) | collective-permute-done | bytes 196640 | tf_op jit(solution)/shard_map/ppermute | solution.py:395
  17.5 5.3 %shard_map.75 = (bf16[128,256]{1,0:T(8,128)(2,1)}, bf16[128,256]{1,0:T(8,128)(2,1)}, bf16[2,512,256]{2,1,0:T(8,128)(2,1)S(1)}, bf16[2304,256]{1,0:T(8,128)(2,1)S...) custom-call(s32[1,10]{1,0:T(1,128)} %ranges.11, ...), custom_call_target="tpu_custom_call" | custom-call | tf_op jit(solution)/shard_map/pallas_call | solution.py:408
  22.9 4.2 %shard_map.76 = (bf16[128,256]{1,0:T(8,128)(2,1)}, bf16[128,256]{1,0:T(8,128)(2,1)}, f32[128,256]{1,0:T(8,128)S(1)}, bf16[3,512,256]{2,1,0:T(8,128)(2,1)S(1)}, bf16[640,256]{1,0:T(8,128)(2,1)}) custom-call(s32[1,10]{1,0:T(1,128)S(1)} %copy-done, bf16[2304,256]{1,0:T(8,128)(2,1)S(1)} %get-tuple-element.47.rows, ...), custom_call_target="tpu_custom_call" | custom-call | tf_op jit(solution)/shard_map/pallas_call | solution.py:431
  27.7 3.1 %collective-permute-start.1 = (bf16[128,256]{1,0:T(8,128)(2,1)S(1)}, bf16[128,256]{1,0:T(8,128)(2,1)S(1)}, u32[]{:S(2)}, u32[]{:S(2)}) collective-permute-start(bf16[128,256]{1,0:T(8,128)(2,1)S(1)} %copy-done.2), channel_id=1, source_target_pairs={{0,28},{2,30},{4,8},{6,10},{8,4},{10,6},{12,16},{14,18},{16,12},{1... | collective-permute-start | bytes 196616 | tf_op jit(solution)/shard_map/ppermute | solution.py:450
  30.8 1.0 %collective-permute-start.2 = (bf16[128,256]{1,0:T(8,128)(2,1)S(1)}, bf16[128,256]{1,0:T(8,128)(2,1)S(1)}, u32[]{:S(2)}, u32[]{:S(2)}) collective-permute-start(bf16[128,256]{1,0:T(8,128)(2,1)S(1)} %copy-done.1), channel_id=1, source_target_pairs={{0,30},{2,4},{4,2},{6,8},{8,6},{10,12},{12,10},{14,16},{16,14},{18... | collective-permute-start | bytes 196616 | tf_op jit(solution)/shard_map/ppermute | solution.py:450
  31.8 2.6 %collective-permute-start.6 = (bf16[640,256]{1,0:T(8,128)(2,1)}, bf16[640,256]{1,0:T(8,128)(2,1)}, u32[]{:S(2)}, u32[]{:S(2)}) collective-permute-start(bf16[640,256]{1,0:T(8,128)(2,1)} %get-tuple-element.57), channel_id=1, source_target_pairs={{0,1},{1,0},{2,3},{3,2},{4,5},{5,4},{6,7},{7,6},{8,9},{9,8},{10,11... | collective-permute-start | bytes 983048 | tf_op jit(solution)/shard_map/ppermute | solution.py:356
  34.8 2.5 %collective-permute-done.2 = bf16[128,256]{1,0:T(8,128)(2,1)S(1)} collective-permute-done((bf16[128,256]{1,0:T(8,128)(2,1)S(1)}, bf16[128,256]{1,0:T(8,128)(2,1)S(1)}, u32[]{:S(2)}, u32[]{:S(2)}) %collective-permute-start.2) | collective-permute-done | bytes 65568 | tf_op jit(solution)/shard_map/ppermute | solution.py:450
  37.9 1.3 %collective-permute-start.5 = (bf16[128,256]{1,0:T(8,128)(2,1)}, bf16[128,256]{1,0:T(8,128)(2,1)}, u32[]{:S(2)}, u32[]{:S(2)}) collective-permute-start(bf16[128,256]{1,0:T(8,128)(2,1)} %get-tuple-element.81), channel_id=1, source_target_pairs={{0,1},{1,0},{2,3},{3,2},{4,5},{5,4},{6,7},{7,6},{8,9},{9,8},{10,11... | collective-permute-start | bytes 196616 | tf_op jit(solution)/shard_map/ppermute | solution.py:356
  39.2 1.2 %shard_map.74 = (f32[128,256]{1,0:T(8,128)S(1)}, f32[128,256]{1,0:T(8,128)S(1)}, f32[128,256]{1,0:T(8,128)S(1)}, f32[128,256]{1,0:T(8,128)S(1)}) custom-call(bf16[256,640]{1,0:T(8,128)(2,1)} %bitcast.3.arrived_ref), custom_call_target="tpu_custom_call" | custom-call | tf_op jit(solution)/shard_map/pallas_call | solution.py:403
  40.4 2.1 %collective-permute-done.5.refs_0_ = bf16[128,256]{1,0:T(8,128)(2,1)} collective-permute-done((bf16[128,256]{1,0:T(8,128)(2,1)}, bf16[128,256]{1,0:T(8,128)(2,1)}, u32[]{:S(2)}, u32[]{:S(2)}) %collective-permute-start.5) | collective-permute-done | bytes 65568 | tf_op jit(solution)/shard_map/ppermute | solution.py:356
  42.5 1.4 %shard_map.77 = (bf16[128,256]{1,0:T(8,128)(2,1)S(1)}, f32[128,256]{1,0:T(8,128)S(1)}, bf16[128,256]{1,0:T(8,128)(2,1)S(1)}, bf16[128,256]{1,0:T(8,128)(2,1)S(1)...) custom-call(s32[1,10]{1,0:T(1,128)S(1)} %copy-done, ...), custom_call_target="tpu_custom_call" | custom-call | tf_op jit(solution)/shard_map/pallas_call | solution.py:480
  44.0 3.7 %collective-permute-start.7 = (bf16[128,256]{1,0:T(8,128)(2,1)S(1)}, bf16[128,256]{1,0:T(8,128)(2,1)S(1)}, u32[]{:S(2)}, u32[]{:S(2)}) collective-permute-start(bf16[128,256]{1,0:T(8,128)(2,1)S(1)} %get-tuple-element.61), channel_id=1, source_target_pairs={{0,28},{2,30},{4,8},{6,10},{8,4},{10,6},{12,16},{14,18},{16,12},{1... | collective-permute-start | bytes 196616 | tf_op jit(solution)/shard_map/ppermute | solution.py:450
  47.7 0.8 %collective-permute-start.8 = (bf16[128,256]{1,0:T(8,128)(2,1)S(1)}, bf16[128,256]{1,0:T(8,128)(2,1)S(1)}, u32[]{:S(2)}, u32[]{:S(2)}) collective-permute-start(bf16[128,256]{1,0:T(8,128)(2,1)S(1)} %get-tuple-element.62), channel_id=1, source_target_pairs={{0,30},{2,4},{4,2},{6,8},{8,6},{10,12},{12,10},{14,16},{16,14},{18... | collective-permute-start | bytes 196616 | tf_op jit(solution)/shard_map/ppermute | solution.py:450
  49.1 2.2 %collective-permute-done.7.refs_0_ = bf16[128,256]{1,0:T(8,128)(2,1)S(1)} collective-permute-done((bf16[128,256]{1,0:T(8,128)(2,1)S(1)}, bf16[128,256]{1,0:T(8,128)(2,1)S(1)}, u32[]{:S(2)}, u32[]{:S(2)}) %collective-permute-start.7) | collective-permute-done | bytes 65568 | tf_op jit(solution)/shard_map/ppermute | solution.py:450
  51.3 2.8 %collective-permute-done.8.refs_1_ = bf16[128,256]{1,0:T(8,128)(2,1)S(1)} collective-permute-done((bf16[128,256]{1,0:T(8,128)(2,1)S(1)}, bf16[128,256]{1,0:T(8,128)(2,1)S(1)}, u32[]{:S(2)}, u32[]{:S(2)}) %collective-permute-start.8) | collective-permute-done | bytes 65568 | tf_op jit(solution)/shard_map/ppermute | solution.py:450
  54.1 1.0 %shard_map.78 = (bf16[128,256]{1,0:T(8,128)(2,1)S(1)}, f32[128,256]{1,0:T(8,128)S(1)}, bf16[128,256]{1,0:T(8,128)(2,1)S(1)}, bf16[128,256]{1,0:T(8,128)(2,1)S(1)...) custom-call(s32[1,10]{1,0:T(1,128)S(1)} %copy-done, ...), custom_call_target="tpu_custom_call" | custom-call | tf_op jit(solution)/shard_map/pallas_call | solution.py:480
  55.1 2.2 %collective-permute-start.11 = (bf16[128,256]{1,0:T(8,128)(2,1)S(1)}, bf16[128,256]{1,0:T(8,128)(2,1)S(1)}, u32[]{:S(2)}, u32[]{:S(2)}) collective-permute-start(bf16[128,256]{1,0:T(8,128)(2,1)S(1)} %get-tuple-element.69), channel_id=1, source_target_pairs={{0,28},{2,30},{4,8},{6,10},{8,4},{10,6},{12,16},{14,18},{16,12},{1... | collective-permute-start | bytes 196616 | tf_op jit(solution)/shard_map/ppermute | solution.py:450
  57.5 1.3 %collective-permute-start.13 = (bf16[128,256]{1,0:T(8,128)(2,1)S(1)}, bf16[128,256]{1,0:T(8,128)(2,1)S(1)}, u32[]{:S(2)}, u32[]{:S(2)}) collective-permute-start(bf16[128,256]{1,0:T(8,128)(2,1)S(1)} %get-tuple-element.71), channel_id=1, source_target_pairs={{0,4},{2,6},{4,0},{6,2},{8,12},{10,14},{12,8},{14,10},{16,20},{18,... | collective-permute-start | bytes 196616 | tf_op jit(solution)/shard_map/ppermute | solution.py:450
  59.5 2.7 %collective-permute-done.11.refs_0_ = bf16[128,256]{1,0:T(8,128)(2,1)S(1)} collective-permute-done((bf16[128,256]{1,0:T(8,128)(2,1)S(1)}, bf16[128,256]{1,0:T(8,128)(2,1)S(1)}, u32[]{:S(2)}, u32[]{:S(2)}) %collective-permute-start.11) | collective-permute-done | bytes 65568 | tf_op jit(solution)/shard_map/ppermute | solution.py:450
  62.2 1.5 %collective-permute-done.12.refs_1_ = bf16[128,256]{1,0:T(8,128)(2,1)S(1)} collective-permute-done((bf16[128,256]{1,0:T(8,128)(2,1)S(1)}, bf16[128,256]{1,0:T(8,128)(2,1)S(1)}, u32[]{:S(2)}, u32[]{:S(2)}) %collective-permute-start.12) | collective-permute-done | bytes 65568 | tf_op jit(solution)/shard_map/ppermute | solution.py:450
  63.7 1.1 %shard_map.79 = (bf16[128,256]{1,0:T(8,128)(2,1)S(1)}, f32[128,256]{1,0:T(8,128)S(1)}, bf16[128,256]{1,0:T(8,128)(2,1)S(1)}, bf16[128,256]{1,0:T(8,128)(2,1)S(1)...) custom-call(s32[1,10]{1,0:T(1,128)S(1)} %copy-done, f32[128,256]{1,0:T(8,128)S(1)} %get-tuple-element.67.source, ...), custom_call_target="tpu_custom_call" | custom-call | tf_op jit(solution)/shard_map/pallas_call | solution.py:480
  65.4 2.8 %collective-permute-start.18 = (bf16[128,256]{1,0:T(8,128)(2,1)S(1)}, bf16[128,256]{1,0:T(8,128)(2,1)S(1)}, u32[]{:S(2)}, u32[]{:S(2)}) collective-permute-start(bf16[128,256]{1,0:T(8,128)(2,1)S(1)} %get-tuple-element.77), channel_id=1, source_target_pairs={{0,28},{2,30},{4,8},{6,10},{8,4},{10,6},{12,16},{14,18},{16,12},{1... | collective-permute-start | bytes 196616 | tf_op jit(solution)/shard_map/ppermute | solution.py:450
  68.6 1.1 %collective-permute-start.20 = (bf16[128,256]{1,0:T(8,128)(2,1)S(1)}, bf16[128,256]{1,0:T(8,128)(2,1)S(1)}, u32[]{:S(2)}, u32[]{:S(2)}) collective-permute-start(bf16[128,256]{1,0:T(8,128)(2,1)S(1)} %get-tuple-element.79), channel_id=1, source_target_pairs={{0,4},{2,6},{4,0},{6,2},{8,12},{10,14},{12,8},{14,10},{16,20},{18,... | collective-permute-start | bytes 196616 | tf_op jit(solution)/shard_map/ppermute | solution.py:450
  69.7 1.4 %collective-permute-start.16 = (bf16[128,256]{1,0:T(8,128)(2,1)S(1)}, bf16[128,256]{1,0:T(8,128)(2,1)S(1)}, u32[]{:S(2)}, u32[]{:S(2)}) collective-permute-start(bf16[128,256]{1,0:T(8,128)(2,1)S(1)} %get-tuple-element.58.refs_0_), channel_id=1, source_target_pairs={{0,1},{1,0},{2,3},{3,2},{4,5},{5,4},{6,7},{7,6},{8,9},{9,8},{10,11... | collective-permute-start | bytes 196616 | tf_op jit(solution)/shard_map/ppermute | solution.py:462
  71.1 1.4 %collective-permute-done.18.refs_0_ = bf16[128,256]{1,0:T(8,128)(2,1)S(1)} collective-permute-done((bf16[128,256]{1,0:T(8,128)(2,1)S(1)}, bf16[128,256]{1,0:T(8,128)(2,1)S(1)}, u32[]{:S(2)}, u32[]{:S(2)}) %collective-permute-start.18) | collective-permute-done | bytes 65568 | tf_op jit(solution)/shard_map/ppermute | solution.py:450
  72.5 2.1 %collective-permute-done.19.refs_1_ = bf16[128,256]{1,0:T(8,128)(2,1)S(1)} collective-permute-done((bf16[128,256]{1,0:T(8,128)(2,1)S(1)}, bf16[128,256]{1,0:T(8,128)(2,1)S(1)}, u32[]{:S(2)}, u32[]{:S(2)}) %collective-permute-start.19) | collective-permute-done | bytes 65568 | tf_op jit(solution)/shard_map/ppermute | solution.py:450
  75.3 1.5 %collective-permute-start.22 = (bf16[128,256]{1,0:T(8,128)(2,1)S(1)}, bf16[128,256]{1,0:T(8,128)(2,1)S(1)}, u32[]{:S(2)}, u32[]{:S(2)}) collective-permute-start(bf16[128,256]{1,0:T(8,128)(2,1)S(1)} %shard_map.81.mine), channel_id=1, source_target_pairs={{0,1},{1,0},{2,3},{3,2},{4,5},{5,4},{6,7},{7,6},{8,9},{9,8},{10,11... | collective-permute-start | bytes 196616 | tf_op jit(solution)/shard_map/ppermute | solution.py:462
  77.7 2.0 %collective-permute-done.22.far = bf16[128,256]{1,0:T(8,128)(2,1)S(1)} collective-permute-done((bf16[128,256]{1,0:T(8,128)(2,1)S(1)}, bf16[128,256]{1,0:T(8,128)(2,1)S(1)}, u32[]{:S(2)}, u32[]{:S(2)}) %collective-permute-start.22) | collective-permute-done | bytes 65568 | tf_op jit(solution)/shard_map/ppermute | solution.py:462
  (34 shorter events, 6.6 us)
Async XLA Ops:
  2.8 20.0 %copy-start = (s32[1,10]{1,0:T(1,128)S(1)}, s32[1,10]{1,0:T(1,128)}, u32[]{:S(2)}) copy-start(s32[1,10]{1,0:T(1,128)} %ranges.11) | copy-start | bytes 124
  2.8 36.3 %all-to-all-start = ((bf16[16,16,640]{2,1,0:T(8,128)(2,1)}), bf16[16,16,640]{2,1,0:T(8,128)(2,1)}, u32[]{:S(2)}, u32[]{:S(2)}) async-start(bf16[16,16,640]{2,1,0:T(8,128)(2,1)} %bitcast.2), calls=%async_computation | async-start | bytes 655360 | tf_op jit(solution)/shard_map/all_to_all | solution.py:396
  10.3 7.2 %collective-permute-start = (bf16[3,256,128]{2,1,0:T(8,128)(2,1)S(1)}, bf16[3,256,128]{2,1,0:T(8,128)(2,1)S(1)}, u32[]{:S(2)}, u32[]{:S(2)}) collective-permute-start(bf16[3,256,128]{2,1,0:T(8,128)(2,1)S(1)} %get-tuple-element.45), channel_id=1, source_target_pairs={{0,1},{1,0},{2,3},{3,2},{4,5},{5,4},{6,7},{7,6},{8,9},{9,8},{10,11... | collective-permute-start | bytes 589832 | tf_op jit(solution)/shard_map/ppermute | solution.py:395
  22.9 4.9 %copy-start.2 = (bf16[128,256]{1,0:T(8,128)(2,1)S(1)}, bf16[128,256]{1,0:T(8,128)(2,1)}, u32[]{:S(2)}) copy-start(bf16[128,256]{1,0:T(8,128)(2,1)} %get-tuple-element.51) | copy-start | bytes 196612
  22.9 8.0 %copy-start.1 = (bf16[128,256]{1,0:T(8,128)(2,1)S(1)}, bf16[128,256]{1,0:T(8,128)(2,1)}, u32[]{:S(2)}) copy-start(bf16[128,256]{1,0:T(8,128)(2,1)} %get-tuple-element.52) | copy-start | bytes 196612
  27.1 7.3 %collective-permute-start.3 = (bf16[128,256]{1,0:T(8,128)(2,1)}, bf16[128,256]{1,0:T(8,128)(2,1)S(1)}, u32[]{:S(2)}, u32[]{:S(2)}) collective-permute-start(bf16[128,256]{1,0:T(8,128)(2,1)} %get-tuple-element.53), channel_id=1, source_target_pairs={{0,4},{2,6},{4,0},{6,2},{8,12},{10,14},{12,8},{14,10},{16,20},{18,... | collective-permute-start | bytes 196616 | tf_op jit(solution)/shard_map/ppermute | solution.py:450
  27.2 7.2 %collective-permute-start.4 = (bf16[128,256]{1,0:T(8,128)(2,1)}, bf16[128,256]{1,0:T(8,128)(2,1)S(1)}, u32[]{:S(2)}, u32[]{:S(2)}) collective-permute-start(bf16[128,256]{1,0:T(8,128)(2,1)} %get-tuple-element.54), channel_id=1, source_target_pairs={{0,2},{2,0},{4,6},{6,4},{8,10},{10,8},{12,14},{14,12},{16,18},{18,... | collective-permute-start | bytes 196616 | tf_op jit(solution)/shard_map/ppermute | solution.py:450
  27.7 7.0 %collective-permute-start.1 = (bf16[128,256]{1,0:T(8,128)(2,1)S(1)}, bf16[128,256]{1,0:T(8,128)(2,1)S(1)}, u32[]{:S(2)}, u32[]{:S(2)}) collective-permute-start(bf16[128,256]{1,0:T(8,128)(2,1)S(1)} %copy-done.2), channel_id=1, source_target_pairs={{0,28},{2,30},{4,8},{6,10},{8,4},{10,6},{12,16},{14,18},{16,12},{1... | collective-permute-start | bytes 196616 | tf_op jit(solution)/shard_map/ppermute | solution.py:450
  30.8 6.4 %collective-permute-start.2 = (bf16[128,256]{1,0:T(8,128)(2,1)S(1)}, bf16[128,256]{1,0:T(8,128)(2,1)S(1)}, u32[]{:S(2)}, u32[]{:S(2)}) collective-permute-start(bf16[128,256]{1,0:T(8,128)(2,1)S(1)} %copy-done.1), channel_id=1, source_target_pairs={{0,30},{2,4},{4,2},{6,8},{8,6},{10,12},{12,10},{14,16},{16,14},{18... | collective-permute-start | bytes 196616 | tf_op jit(solution)/shard_map/ppermute | solution.py:450
  31.8 10.7 %collective-permute-start.6 = (bf16[640,256]{1,0:T(8,128)(2,1)}, bf16[640,256]{1,0:T(8,128)(2,1)}, u32[]{:S(2)}, u32[]{:S(2)}) collective-permute-start(bf16[640,256]{1,0:T(8,128)(2,1)} %get-tuple-element.57), channel_id=1, source_target_pairs={{0,1},{1,0},{2,3},{3,2},{4,5},{5,4},{6,7},{7,6},{8,9},{9,8},{10,11... | collective-permute-start | bytes 983048 | tf_op jit(solution)/shard_map/ppermute | solution.py:356
  37.9 4.6 %collective-permute-start.5 = (bf16[128,256]{1,0:T(8,128)(2,1)}, bf16[128,256]{1,0:T(8,128)(2,1)}, u32[]{:S(2)}, u32[]{:S(2)}) collective-permute-start(bf16[128,256]{1,0:T(8,128)(2,1)} %get-tuple-element.81), channel_id=1, source_target_pairs={{0,1},{1,0},{2,3},{3,2},{4,5},{5,4},{6,7},{7,6},{8,9},{9,8},{10,11... | collective-permute-start | bytes 196616 | tf_op jit(solution)/shard_map/ppermute | solution.py:356
  43.9 5.2 %collective-permute-start.10 = (bf16[128,256]{1,0:T(8,128)(2,1)S(1)}, bf16[128,256]{1,0:T(8,128)(2,1)S(1)}, u32[]{:S(2)}, u32[]{:S(2)}) collective-permute-start(bf16[128,256]{1,0:T(8,128)(2,1)S(1)} %get-tuple-element.64), channel_id=1, source_target_pairs={{0,2},{2,0},{4,6},{6,4},{8,10},{10,8},{12,14},{14,12},{16,18},{18,... | collective-permute-start | bytes 196616 | tf_op jit(solution)/shard_map/ppermute | solution.py:450
  44.0 7.3 %collective-permute-start.7 = (bf16[128,256]{1,0:T(8,128)(2,1)S(1)}, bf16[128,256]{1,0:T(8,128)(2,1)S(1)}, u32[]{:S(2)}, u32[]{:S(2)}) collective-permute-start(bf16[128,256]{1,0:T(8,128)(2,1)S(1)} %get-tuple-element.61), channel_id=1, source_target_pairs={{0,28},{2,30},{4,8},{6,10},{8,4},{10,6},{12,16},{14,18},{16,12},{1... | collective-permute-start | bytes 196616 | tf_op jit(solution)/shard_map/ppermute | solution.py:450
  47.7 6.4 %collective-permute-start.8 = (bf16[128,256]{1,0:T(8,128)(2,1)S(1)}, bf16[128,256]{1,0:T(8,128)(2,1)S(1)}, u32[]{:S(2)}, u32[]{:S(2)}) collective-permute-start(bf16[128,256]{1,0:T(8,128)(2,1)S(1)} %get-tuple-element.62), channel_id=1, source_target_pairs={{0,30},{2,4},{4,2},{6,8},{8,6},{10,12},{12,10},{14,16},{16,14},{18... | collective-permute-start | bytes 196616 | tf_op jit(solution)/shard_map/ppermute | solution.py:450
  48.5 5.5 %collective-permute-start.9 = (bf16[128,256]{1,0:T(8,128)(2,1)S(1)}, bf16[128,256]{1,0:T(8,128)(2,1)S(1)}, u32[]{:S(2)}, u32[]{:S(2)}) collective-permute-start(bf16[128,256]{1,0:T(8,128)(2,1)S(1)} %get-tuple-element.63), channel_id=1, source_target_pairs={{0,4},{2,6},{4,0},{6,2},{8,12},{10,14},{12,8},{14,10},{16,20},{18,... | collective-permute-start | bytes 196616 | tf_op jit(solution)/shard_map/ppermute | solution.py:450
  55.1 7.1 %collective-permute-start.11 = (bf16[128,256]{1,0:T(8,128)(2,1)S(1)}, bf16[128,256]{1,0:T(8,128)(2,1)S(1)}, u32[]{:S(2)}, u32[]{:S(2)}) collective-permute-start(bf16[128,256]{1,0:T(8,128)(2,1)S(1)} %get-tuple-element.69), channel_id=1, source_target_pairs={{0,28},{2,30},{4,8},{6,10},{8,4},{10,6},{12,16},{14,18},{16,12},{1... | collective-permute-start | bytes 196616 | tf_op jit(solution)/shard_map/ppermute | solution.py:450
  57.3 6.4 %collective-permute-start.12 = (bf16[128,256]{1,0:T(8,128)(2,1)S(1)}, bf16[128,256]{1,0:T(8,128)(2,1)S(1)}, u32[]{:S(2)}, u32[]{:S(2)}) collective-permute-start(bf16[128,256]{1,0:T(8,128)(2,1)S(1)} %get-tuple-element.70), channel_id=1, source_target_pairs={{0,30},{2,4},{4,2},{6,8},{8,6},{10,12},{12,10},{14,16},{16,14},{18... | collective-permute-start | bytes 196616 | tf_op jit(solution)/shard_map/ppermute | solution.py:450
  57.5 6.2 %collective-permute-start.13 = (bf16[128,256]{1,0:T(8,128)(2,1)S(1)}, bf16[128,256]{1,0:T(8,128)(2,1)S(1)}, u32[]{:S(2)}, u32[]{:S(2)}) collective-permute-start(bf16[128,256]{1,0:T(8,128)(2,1)S(1)} %get-tuple-element.71), channel_id=1, source_target_pairs={{0,4},{2,6},{4,0},{6,2},{8,12},{10,14},{12,8},{14,10},{16,20},{18,... | collective-permute-start | bytes 196616 | tf_op jit(solution)/shard_map/ppermute | solution.py:450
  58.8 4.9 %collective-permute-start.14 = (bf16[128,256]{1,0:T(8,128)(2,1)S(1)}, bf16[128,256]{1,0:T(8,128)(2,1)S(1)}, u32[]{:S(2)}, u32[]{:S(2)}) collective-permute-start(bf16[128,256]{1,0:T(8,128)(2,1)S(1)} %get-tuple-element.72), channel_id=1, source_target_pairs={{0,2},{2,0},{4,6},{6,4},{8,10},{10,8},{12,14},{14,12},{16,18},{18,... | collective-permute-start | bytes 196616 | tf_op jit(solution)/shard_map/ppermute | solution.py:450
  58.8 4.9 %collective-permute-start.15 = (bf16[128,256]{1,0:T(8,128)(2,1)S(1)}, bf16[128,256]{1,0:T(8,128)(2,1)S(1)}, u32[]{:S(2)}, u32[]{:S(2)}) collective-permute-start(bf16[128,256]{1,0:T(8,128)(2,1)S(1)} %get-tuple-element.66.refs_1_), channel_id=1, source_target_pairs={{0,1},{1,0},{2,3},{3,2},{4,5},{5,4},{6,7},{7,6},{8,9},{9,8},{10,11... | collective-permute-start | bytes 196616 | tf_op jit(solution)/shard_map/ppermute | solution.py:462
  64.8 4.9 %collective-permute-start.17 = (bf16[128,256]{1,0:T(8,128)(2,1)S(1)}, bf16[128,256]{1,0:T(8,128)(2,1)S(1)}, u32[]{:S(2)}, u32[]{:S(2)}) collective-permute-start(bf16[128,256]{1,0:T(8,128)(2,1)S(1)} %get-tuple-element.74.refs_2_), channel_id=1, source_target_pairs={{0,1},{1,0},{2,3},{3,2},{4,5},{5,4},{6,7},{7,6},{8,9},{9,8},{10,11... | collective-permute-start | bytes 196616 | tf_op jit(solution)/shard_map/ppermute | solution.py:462
  65.4 7.1 %collective-permute-start.18 = (bf16[128,256]{1,0:T(8,128)(2,1)S(1)}, bf16[128,256]{1,0:T(8,128)(2,1)S(1)}, u32[]{:S(2)}, u32[]{:S(2)}) collective-permute-start(bf16[128,256]{1,0:T(8,128)(2,1)S(1)} %get-tuple-element.77), channel_id=1, source_target_pairs={{0,28},{2,30},{4,8},{6,10},{8,4},{10,6},{12,16},{14,18},{16,12},{1... | collective-permute-start | bytes 196616 | tf_op jit(solution)/shard_map/ppermute | solution.py:450
  68.2 6.4 %collective-permute-start.19 = (bf16[128,256]{1,0:T(8,128)(2,1)S(1)}, bf16[128,256]{1,0:T(8,128)(2,1)S(1)}, u32[]{:S(2)}, u32[]{:S(2)}) collective-permute-start(bf16[128,256]{1,0:T(8,128)(2,1)S(1)} %get-tuple-element.78), channel_id=1, source_target_pairs={{0,30},{2,4},{4,2},{6,8},{8,6},{10,12},{12,10},{14,16},{16,14},{18... | collective-permute-start | bytes 196616 | tf_op jit(solution)/shard_map/ppermute | solution.py:450
  68.6 6.0 %collective-permute-start.20 = (bf16[128,256]{1,0:T(8,128)(2,1)S(1)}, bf16[128,256]{1,0:T(8,128)(2,1)S(1)}, u32[]{:S(2)}, u32[]{:S(2)}) collective-permute-start(bf16[128,256]{1,0:T(8,128)(2,1)S(1)} %get-tuple-element.79), channel_id=1, source_target_pairs={{0,4},{2,6},{4,0},{6,2},{8,12},{10,14},{12,8},{14,10},{16,20},{18,... | collective-permute-start | bytes 196616 | tf_op jit(solution)/shard_map/ppermute | solution.py:450
  69.7 4.8 %collective-permute-start.21 = (bf16[128,256]{1,0:T(8,128)(2,1)S(1)}, bf16[128,256]{1,0:T(8,128)(2,1)S(1)}, u32[]{:S(2)}, u32[]{:S(2)}) collective-permute-start(bf16[128,256]{1,0:T(8,128)(2,1)S(1)} %get-tuple-element.80), channel_id=1, source_target_pairs={{0,2},{2,0},{4,6},{6,4},{8,10},{10,8},{12,14},{14,12},{16,18},{18,... | collective-permute-start | bytes 196616 | tf_op jit(solution)/shard_map/ppermute | solution.py:450
  69.7 7.1 %collective-permute-start.16 = (bf16[128,256]{1,0:T(8,128)(2,1)S(1)}, bf16[128,256]{1,0:T(8,128)(2,1)S(1)}, u32[]{:S(2)}, u32[]{:S(2)}) collective-permute-start(bf16[128,256]{1,0:T(8,128)(2,1)S(1)} %get-tuple-element.58.refs_0_), channel_id=1, source_target_pairs={{0,1},{1,0},{2,3},{3,2},{4,5},{5,4},{6,7},{7,6},{8,9},{9,8},{10,11... | collective-permute-start | bytes 196616 | tf_op jit(solution)/shard_map/ppermute | solution.py:462
  75.3 4.3 %collective-permute-start.22 = (bf16[128,256]{1,0:T(8,128)(2,1)S(1)}, bf16[128,256]{1,0:T(8,128)(2,1)S(1)}, u32[]{:S(2)}, u32[]{:S(2)}) collective-permute-start(bf16[128,256]{1,0:T(8,128)(2,1)S(1)} %shard_map.81.mine), channel_id=1, source_target_pairs={{0,1},{1,0},{2,3},{3,2},{4,5},{5,4},{6,7},{7,6},{8,9},{9,8},{10,11... | collective-permute-start | bytes 196616 | tf_op jit(solution)/shard_map/ppermute | solution.py:462

commit v5 on v3

--- a/solution.py
+++ b/solution.py
@@ -10,6 +10,8 @@
 NEAR = 5
 CAP = 16
 HALF = NEAR // 2
+PIECES = 2
+LIMIT = 46 << 20
 LANES = 128
 VMEM = pltpu.VMEM
 
@@ -32,21 +34,18 @@
     return [list(enumerate(p)) for p in (far, odd_even, near, core)]
 
 
-def pack_kernel(tile_hbm, panel_hbm, history, rows_ref, out_ref, edge, tile_ref, panel_ref, sems):
+def pack_kernel(tile_hbm, panel_hbm, rows_ref, out_hbm, tile_ref, panel_ref, sems, out_ref, out_sem):
     copies = [
         pltpu.make_async_copy(tile_hbm, tile_ref, sems.at[0]),
         pltpu.make_async_copy(panel_hbm, panel_ref, sems.at[1]),
-        pltpu.make_async_copy(
-            history.at[pl.ds(history.shape[0] - edge.shape[0], edge.shape[0])], edge, sems.at[2]
-        ),
     ]
     for copy in copies:
         copy.start()
-    for copy in copies[:2]:
+    for copy in copies:
         copy.wait()
     recv = rows_ref.shape[0]
-    width = rows_ref.shape[1]
-    slots = out_ref.shape[0]
+    slots, width = out_ref.shape
+    width = width - LANES
     patches = slots // CAP
     tile = tile_ref[...]
     hot = lax.broadcasted_iota(jnp.int32, (patches, recv), 0) == tile
@@ -59,17 +58,20 @@
     slot = tile * CAP + earlier
     placed = lax.broadcasted_iota(jnp.int32, (slots, recv), 0) == slot
     placer = jnp.where(placed, 1.0, 0.0).astype(jnp.bfloat16)
-    out_ref[:, :width] = dot(placer, rows_ref[...]).astype(jnp.bfloat16)
+    piece = lax.rem(lax.axis_index("lag"), rows_ref.shape[1] // width)
+    rows = rows_ref[:, pl.ds(pl.multiple_of(piece * width, width), width)]
+    out_ref[:, :width] = dot(placer, rows).astype(jnp.bfloat16)
     marks = jnp.where(placed, (panel_ref[...] + 1).astype(jnp.float32), 0.0)
     label = jnp.sum(marks, axis=1, keepdims=True)
     out_ref[:, width:] = jnp.broadcast_to(label, (slots, LANES)).astype(jnp.bfloat16)
-    copies[2].wait()
-
-
-def source_kernel(arrived_ref, *outs):
+    copy = pltpu.make_async_copy(out_ref, out_hbm, out_sem)
+    copy.start()
+    copy.wait()
+
+
+def source_kernel(shots, arrived_ref, out):
     slots = arrived_ref.shape[0]
-    shots, tile_len = outs[0].shape
-    width = len(outs) * shots
+    width, tile_len = out.shape
     label = arrived_ref[:, width:].astype(jnp.float32)
     lane = lax.broadcasted_iota(jnp.int32, (slots, LANES), 1)
     picker = jnp.concatenate(
@@ -79,9 +81,9 @@
         ],
         axis=1,
     ).astype(jnp.bfloat16)
-    for step, out in enumerate(outs):
-        out[...] = lax.dot_general(
-            arrived_ref[:, step * shots : (step + 1) * shots],
+    for first in range(0, width, shots):
+        out[first : first + shots, :] = lax.dot_general(
+            arrived_ref[:, first : first + shots],
             picker,
             (((0,), (0,)), ((), ())),
             preferred_element_type=jnp.float32,
@@ -190,14 +192,23 @@
         send(slot, 1, rest.at[pl.ds(slot * shots, shots)]).wait()
 
 
+def sum_kernel(own, *refs):
+    *blocks, half = refs
+    total = own[...]
+    for block in blocks:
+        total = total + block[...].astype(jnp.float32)
+    half[...] = total.astype(jnp.bfloat16)
+
+
 def step_kernel(step, last_step, ranges, source, inverse, own, *refs):
     shots, tile_len = own.shape
     refs = list(refs)
-    received = [refs.pop(0) for _ in range(NEAR - 1 if step > 0 else 0)]
+    received = [refs.pop(0) for _ in range(NEAR - 1)]
     total = own[...]
     for block in received:
         total = total + block[...].astype(jnp.float32)
-    right = source[...] - total
+    held = source.shape[0] // shots
+    right = source[step * shots : (step + 1) * shots, :] - total if step < held else -total
     if step != 1:
         right = right - refs.pop(0)[...].astype(jnp.float32)
     density = dot(right.astype(jnp.bfloat16), inverse[...])
@@ -213,6 +224,10 @@
     messages = outs[3:]
     band_zero = lax.axis_index("lag") == 0
     density_ref[...] = rounded
+    if step + 1 >= held:
+        at = (step + 1 - held) * shots
+        carried = jnp.where(lax.axis_index("lag") == 1, source[at : at + shots, :], 0.0)
+        total = total - carried
     cross[...] = jnp.where(band_zero, density, total).astype(jnp.bfloat16)
     recent = [rounded] + [ref[...] for ref in olders]
     steps = stage.shape[1] // shots
@@ -314,41 +329,47 @@
     f32, bf16 = jnp.float32, jnp.bfloat16
     block = (shots, tile_len)
     routes = pairings(patches)
-
-    outgoing, edge = call(
+    piece = width // PIECES
+
+    piece = width // PIECES
+    rim = lax.ppermute(
+        history[band - steps + 1 :], "lag", [(i, (i + 1) % lags) for i in range(lags)]
+    )
+    (outgoing,) = call(
         pack_kernel,
-        [((patches * CAP, width + LANES), bf16), ((steps - 1, tile_len, shots), bf16)],
-        [pltpu.HBM] * 3 + [VMEM],
-        [VMEM((1, recv), jnp.int32)] * 2 + [pltpu.SemaphoreType.DMA((3,))],
-        out_specs=[VMEM, pl.ANY],
+        [((patches * CAP, piece + LANES), bf16, pltpu.HBM)],
+        [pltpu.HBM] * 2 + [VMEM],
+        [VMEM((1, recv), jnp.int32)] * 2 + [pltpu.SemaphoreType.DMA((2,))]
+        + [VMEM((patches * CAP, piece + LANES), bf16), pltpu.SemaphoreType.DMA],
+        out_specs=[pltpu.HBM],
     )(
         far_memory(receiver_tile.reshape(1, recv)),
         far_memory(receiver_panel.reshape(1, recv)),
-        far_memory(history),
         residuals.reshape(recv, width),
     )
-    rim = lax.ppermute(edge, "lag", [(i, (i + 1) % lags) for i in range(lags)])
     arrived = lax.all_to_all(
-        outgoing.reshape(patches, CAP, width + LANES),
+        outgoing.reshape(patches, CAP, piece + LANES),
         "patch",
         split_axis=0,
         concat_axis=0,
         tiled=True,
-    ).reshape(patches * CAP, width + LANES)
-    source = call(source_kernel, [(block, f32, VMEM)] * steps, [VMEM])(arrived)
-    source = [near_memory(s) for s in source]
+    ).reshape(patches * CAP, piece + LANES)
+    (source,) = call(
+        functools.partial(source_kernel, shots), [((piece, tile_len), f32, VMEM)], [VMEM]
+    )(arrived)
+    source = near_memory(source)
 
     sizes = [*range(2, band, 2), band]
     older = call(
         functools.partial(older_kernel, steps, sizes),
-        [(block, bf16)] * (NEAR - 1)
+        [(block, bf16, pltpu.HBM)] * (NEAR - 1)
         + [
             (block, f32, VMEM),
             ((NEAR, width, tile_len), bf16, VMEM),
             ((steps - 1, tile_len, NEAR * tile_len), bf16, VMEM),
             ((tile_len, tile_len), bf16, VMEM),
         ]
-        + [((NEAR * shots, tile_len), bf16)],
+        + [((NEAR * shots, tile_len), bf16, pltpu.HBM)],
         [pltpu.SMEM, VMEM, VMEM, pltpu.HBM, pltpu.HBM],
         [
             VMEM(((band + steps - 1) * shots, tile_len), bf16),
@@ -356,9 +377,9 @@
             pltpu.SemaphoreType.DMA((NEAR, band)),
             pltpu.SemaphoreType.DMA((NEAR + 1, steps)),
         ],
-        out_specs=[pl.ANY] * (NEAR - 1) + [VMEM] * 4 + [pl.ANY],
-        limit=54 << 20,
-    )(lag_ranges, rim, history, far_memory(near_inverse), far_memory(interaction))
+        out_specs=[pltpu.HBM] * (NEAR - 1) + [VMEM] * 4 + [pltpu.HBM],
+        limit=LIMIT,
+    )(far_memory(lag_ranges), rim, history, far_memory(near_inverse), far_memory(interaction))
     messages, (own, stage, recent, inverse, rest) = older[: NEAR - 1], older[NEAR - 1 :]
     stage, recent, inverse = near_memory(stage), near_memory(recent), near_memory(inverse)
 
@@ -368,9 +389,14 @@
             gone.append(lax.ppermute(b, "patch", r))
         return gone
 
-    for incoming in exchange(messages):
-        own = own + incoming.astype(f32)
-    own, far = lag_sum(own, lags)
+    own = near_memory(own)
+    received = exchange(messages)
+    (half,) = call(sum_kernel, [(block, bf16)], [VMEM] * NEAR)(own, *received)
+    if lags > 2:
+        half = lag_sum(jnp.where(lax.axis_index("lag") > 0, half, 0), lags)
+        far = half[0] + half[1]
+    else:
+        far = lax.ppermute(half, "lag", lag_partners(lags, 1))
     here, there = lag_sum(rest, lags)
     if lags > 2:
         there = there + (here - rest)
@@ -384,10 +410,9 @@
         return outward, inward + last
 
     densities, outward, inward = [], [], [far]
-    received = []
     for step in range(steps):
         last_step = step == steps - 1
-        inputs = [lag_ranges, source[step], inverse, own, *received]
+        inputs = [lag_ranges, source, inverse, own, *received]
         if step != 1:
             inputs.append(inward[max(step - 1, 0)])
         outs = [(block, bf16)]

time: 81.2 us -> 81.2 us (level)
  waiting for transfers between devices: 29.1 us -> 20.7 us
  local copies, waits for them, and re-layouts: 1.67 us -> 8.71 us
  starting transfers between devices: 30.9 us -> 32.6 us
    unnamed x5 -> x25, local copies, waits for them, and re-layouts: 1.67 us -> 7.77 us
    ppermute x1 -> x2, waiting for transfers between devices: 5.68 us -> 1.48 us  [the longest x1 1.48 us: local(): far = lax.ppermute(half, 'lag', lag_partners(lags, 1))]
    ppermute x2 -> x1, waiting for transfers between devices: 3.6 us -> 0.01 us  [lag_sum(): lax.ppermute(block.astype(jnp.bfloat16), 'lag', lag_partners(lags, distan...]
    ppermute x1 -> x2, starting transfers between devices: 1.55 us -> 4.98 us  [the longest x1 3.03 us: local(): lax.ppermute(history[band - steps + 1:], 'lag', [(i, (i + 1) % lags) for...]
    all_to_all x1, starting transfers between devices: 7.47 us -> 5.99 us  [local(): lax.all_to_all(outgoing.reshape(patches, CAP, piece + LANES), 'patch', sp...]
    ppermute x2 -> x1, starting transfers between devices: 1.46 us -> 0.07 us  [lag_sum(): lax.ppermute(block.astype(jnp.bfloat16), 'lag', lag_partners(lags, distan...]
    ppermute x4, starting transfers between devices: 3.8 us -> 4.91 us  [cross_bands(): swapped = lax.ppermute(block, 'lag', lag_partners(lags, 1))]
    slice x0 -> x1, local copies, waits for them, and re-layouts: none -> 0.94 us  [local(): history[band - steps + 1:]]
  transfers between devices with their start and end apart: 24 -> 24, of which waited for: 10 -> 11; matrix products, arithmetic and copies ran while one was open for 1% -> 1% of each run, Pallas kernels for 15% -> 17%
where the time goes in v5:
time: 81.2 us; the launch traced here: 80.6 us
  starting transfers between devices  32.6 us (40%)
  waiting for transfers between devices  20.7 us (25%)
  Pallas kernels  18.4 us (23%)
  local copies, waits for them, and re-layouts  8.71 us (11%)
    ppermute x16, waiting for transfers between devices, exchange(): gone.append(lax.ppermute(b, 'patch', r))  16.9 us
    ppermute x16, starting transfers between devices, exchange(): gone.append(lax.ppermute(b, 'patch', r))  16.7 us
    pallas_call x1, Pallas kernels, local(): call(functools.partial(older_kernel, steps, sizes), [(block, bf16, pltpu....  8.46 us
    unnamed x25, local copies, waits for them, and re-layouts  7.77 us
    all_to_all x1, starting transfers between devices, local(): lax.all_to_all(outgoing.reshape(patches, CAP, piece + LANES), 'patch', sp...  5.99 us
    ppermute x4, starting transfers between devices, cross_bands(): swapped = lax.ppermute(block, 'lag', lag_partners(lags, 1))  4.91 us
    pallas_call x4, Pallas kernels, local(): call(functools.partial(step_kernel, step, last_step), outs, [pltpu.SMEM]...  4.81 us
    ppermute x1, starting transfers between devices, local(): lax.ppermute(history[band - steps + 1:], 'lag', [(i, (i + 1) % lags) for...  3.03 us
  transfers between devices with their start and end apart: 24, of which 11 were waited for; matrix products, arithmetic and copies ran while one was open for 1% of the time, Pallas kernels for 17%

profile of v5, /device:TPU:0, one launch (start us, length us, event | category | flops | bytes accessed | tf_op | source)
XLA Modules:
  0.0 80.6 jit_solution(916232510693655231)
XLA Ops:
  0.9 3.0 %collective-permute-start = (bf16[3,256,128]{2,1,0:T(8,128)(2,1)S(1)}, bf16[3,256,128]{2,1,0:T(8,128)(2,1)S(1)}, u32[]{:S(2)}, u32[]{:S(2)}) collective-permute-start(bf16[3,256,128]{2,1,0:T(8,128)(2,1)S(1)} %slice.3), channel_id=1, source_target_pairs={{0,1},{1,0},{2,3},{3,2},{4,5},{5,4},{6,7},{7,6},{8,9},{9,8},{10,11... | collective-permute-start | bytes 589832 | tf_op jit(solution)/shard_map/ppermute | solution.py:335
  4.0 1.0 %copy.11 = bf16[32,8,4,128]{3,1,2,0:T(8,128)(2,1)S(1)} copy(bf16[32,8,4,128]{3,2,1,0:T(4,128)(2,1)} %bitcast.10) | data formatting | bytes 524288
  5.0 1.7 %shard_map.73 = bf16[256,384]{1,0:T(8,128)(2,1)} custom-call(s32[1,256]{1,0:T(1,128)} %bitcast.11, s32[1,256]{1,0:T(1,128)} %bitcast.12, bf16[256,512]{1,0:T(8,128)(2,1)S(1)} %bitcast.8), custom_call_target="tpu_custom_call" | custom-call | tf_op jit(solution)/shard_map/pallas_call | solution.py:338
  6.7 6.0 %all-to-all-start = ((bf16[16,16,384]{2,1,0:T(8,128)(2,1)}), bf16[16,16,384]{2,1,0:T(8,128)(2,1)}, u32[]{:S(2)}, u32[]{:S(2)}) async-start(bf16[16,16,384]{2,1,0:T(8,128)(2,1)} %bitcast.9), calls=%async_computation | async-start | bytes 393216 | tf_op jit(solution)/shard_map/all_to_all | solution.py:350
  13.4 1.2 %copy-done = bf16[15,256,128]{2,1,0:T(8,128)(2,1)S(1)} copy-done((bf16[15,256,128]{2,1,0:T(8,128)(2,1)S(1)}, bf16[15,256,128]{2,1,0:T(8,128)(2,1)}, u32[]{:S(2)}) %copy-start) | copy-done | bytes 983064
  15.5 8.5 %shard_map.75 = (bf16[128,256]{1,0:T(8,128)(2,1)}, bf16[128,256]{1,0:T(8,128)(2,1)}, bf16[128,256]{1,0:T(8,128)(2,1)}, bf16[128,256]{1,0:T(8,128)(2,1)}, f32[128...) custom-call(s32[1,10]{1,0:T(1,128)} %ranges.9, ...), custom_call_target="tpu_custom_call" | custom-call | tf_op jit(solution)/shard_map/pallas_call | solution.py:363
  24.1 4.0 %collective-permute-start.1 = (bf16[128,256]{1,0:T(8,128)(2,1)}, bf16[128,256]{1,0:T(8,128)(2,1)S(1)}, u32[]{:S(2)}, u32[]{:S(2)}) collective-permute-start(bf16[128,256]{1,0:T(8,128)(2,1)} %get-tuple-element.36), channel_id=1, source_target_pairs={{0,28},{2,30},{4,8},{6,10},{8,4},{10,6},{12,16},{14,18},{16,12},{1... | collective-permute-start | bytes 196616 | tf_op jit(solution)/shard_map/ppermute | solution.py:389
  28.0 1.2 %collective-permute-start.3 = (bf16[128,256]{1,0:T(8,128)(2,1)}, bf16[128,256]{1,0:T(8,128)(2,1)S(1)}, u32[]{:S(2)}, u32[]{:S(2)}) collective-permute-start(bf16[128,256]{1,0:T(8,128)(2,1)} %get-tuple-element.38), channel_id=1, source_target_pairs={{0,4},{2,6},{4,0},{6,2},{8,12},{10,14},{12,8},{14,10},{16,20},{18,... | collective-permute-start | bytes 196616 | tf_op jit(solution)/shard_map/ppermute | solution.py:389
  29.2 2.1 %collective-permute-done.1.refs_0_ = bf16[128,256]{1,0:T(8,128)(2,1)S(1)} collective-permute-done((bf16[128,256]{1,0:T(8,128)(2,1)}, bf16[128,256]{1,0:T(8,128)(2,1)S(1)}, u32[]{:S(2)}, u32[]{:S(2)}) %collective-permute-start.1) | collective-permute-done | bytes 65568 | tf_op jit(solution)/shard_map/ppermute | solution.py:389
  31.4 3.3 %collective-permute-done.2.refs_1_ = bf16[128,256]{1,0:T(8,128)(2,1)S(1)} collective-permute-done((bf16[128,256]{1,0:T(8,128)(2,1)}, bf16[128,256]{1,0:T(8,128)(2,1)S(1)}, u32[]{:S(2)}, u32[]{:S(2)}) %collective-permute-start.2) | collective-permute-done | bytes 65568 | tf_op jit(solution)/shard_map/ppermute | solution.py:389
  36.0 1.9 %collective-permute-start.5 = (bf16[128,256]{1,0:T(8,128)(2,1)}, bf16[128,256]{1,0:T(8,128)(2,1)}, u32[]{:S(2)}, u32[]{:S(2)}) collective-permute-start(bf16[128,256]{1,0:T(8,128)(2,1)} %shard_map.76), channel_id=1, source_target_pairs={{0,1},{1,0},{2,3},{3,2},{4,5},{5,4},{6,7},{7,6},{8,9},{9,8},{10,11... | collective-permute-start | bytes 196616 | tf_op jit(solution)/shard_map/ppermute | solution.py:399
  37.9 1.1 %shard_map.74.source = f32[256,256]{1,0:T(8,128)S(1)} custom-call(bf16[256,384]{1,0:T(8,128)(2,1)} %bitcast.3.arrived_ref), custom_call_target="tpu_custom_call" | custom-call | tf_op jit(solution)/shard_map/pallas_call | solution.py:357
  39.1 1.5 %collective-permute-done.5.refs_4_ = bf16[128,256]{1,0:T(8,128)(2,1)} collective-permute-done((bf16[128,256]{1,0:T(8,128)(2,1)}, bf16[128,256]{1,0:T(8,128)(2,1)}, u32[]{:S(2)}, u32[]{:S(2)}) %collective-permute-start.5) | collective-permute-done | bytes 65568 | tf_op jit(solution)/shard_map/ppermute | solution.py:399
  43.9 1.4 %shard_map.77 = (bf16[128,256]{1,0:T(8,128)(2,1)S(1)}, bf16[128,256]{1,0:T(8,128)(2,1)S(1)}, f32[128,256]{1,0:T(8,128)S(1)}, bf16[128,256]{1,0:T(8,128)(2,1)S(1)...) custom-call(s32[1,10]{1,0:T(1,128)S(1)} %copy-done.11, ...), custom_call_target="tpu_custom_call" | custom-call | tf_op jit(solution)/shard_map/pallas_call | solution.py:423
  45.3 2.1 %collective-permute-start.7 = (bf16[128,256]{1,0:T(8,128)(2,1)S(1)}, bf16[128,256]{1,0:T(8,128)(2,1)S(1)}, u32[]{:S(2)}, u32[]{:S(2)}) collective-permute-start(bf16[128,256]{1,0:T(8,128)(2,1)S(1)} %get-tuple-element.45), channel_id=1, source_target_pairs={{0,28},{2,30},{4,8},{6,10},{8,4},{10,6},{12,16},{14,18},{16,12},{1... | collective-permute-start | bytes 196616 | tf_op jit(solution)/shard_map/ppermute | solution.py:389
  47.5 1.1 %collective-permute-start.9 = (bf16[128,256]{1,0:T(8,128)(2,1)S(1)}, bf16[128,256]{1,0:T(8,128)(2,1)S(1)}, u32[]{:S(2)}, u32[]{:S(2)}) collective-permute-start(bf16[128,256]{1,0:T(8,128)(2,1)S(1)} %get-tuple-element.47), channel_id=1, source_target_pairs={{0,4},{2,6},{4,0},{6,2},{8,12},{10,14},{12,8},{14,10},{16,20},{18,... | collective-permute-start | bytes 196616 | tf_op jit(solution)/shard_map/ppermute | solution.py:389
  48.5 3.9 %collective-permute-done.7.refs_0_ = bf16[128,256]{1,0:T(8,128)(2,1)S(1)} collective-permute-done((bf16[128,256]{1,0:T(8,128)(2,1)S(1)}, bf16[128,256]{1,0:T(8,128)(2,1)S(1)}, u32[]{:S(2)}, u32[]{:S(2)}) %collective-permute-start.7) | collective-permute-done | bytes 65568 | tf_op jit(solution)/shard_map/ppermute | solution.py:389
  52.4 1.4 %collective-permute-done.8.refs_1_ = bf16[128,256]{1,0:T(8,128)(2,1)S(1)} collective-permute-done((bf16[128,256]{1,0:T(8,128)(2,1)S(1)}, bf16[128,256]{1,0:T(8,128)(2,1)S(1)}, u32[]{:S(2)}, u32[]{:S(2)}) %collective-permute-start.8) | collective-permute-done | bytes 65568 | tf_op jit(solution)/shard_map/ppermute | solution.py:389
  53.9 1.0 %shard_map.78 = (bf16[128,256]{1,0:T(8,128)(2,1)S(1)}, bf16[128,256]{1,0:T(8,128)(2,1)S(1)}, f32[128,256]{1,0:T(8,128)S(1)}, bf16[128,256]{1,0:T(8,128)(2,1)S(1)...) custom-call(s32[1,10]{1,0:T(1,128)S(1)} %copy-done.11, ...), custom_call_target="tpu_custom_call" | custom-call | tf_op jit(solution)/shard_map/pallas_call | solution.py:423
  54.9 2.7 %collective-permute-start.11 = (bf16[128,256]{1,0:T(8,128)(2,1)S(1)}, bf16[128,256]{1,0:T(8,128)(2,1)S(1)}, u32[]{:S(2)}, u32[]{:S(2)}) collective-permute-start(bf16[128,256]{1,0:T(8,128)(2,1)S(1)} %get-tuple-element.52), channel_id=1, source_target_pairs={{0,28},{2,30},{4,8},{6,10},{8,4},{10,6},{12,16},{14,18},{16,12},{1... | collective-permute-start | bytes 196616 | tf_op jit(solution)/shard_map/ppermute | solution.py:389
  57.6 1.5 %collective-permute-start.13 = (bf16[128,256]{1,0:T(8,128)(2,1)S(1)}, bf16[128,256]{1,0:T(8,128)(2,1)S(1)}, u32[]{:S(2)}, u32[]{:S(2)}) collective-permute-start(bf16[128,256]{1,0:T(8,128)(2,1)S(1)} %get-tuple-element.54), channel_id=1, source_target_pairs={{0,4},{2,6},{4,0},{6,2},{8,12},{10,14},{12,8},{14,10},{16,20},{18,... | collective-permute-start | bytes 196616 | tf_op jit(solution)/shard_map/ppermute | solution.py:389
  59.0 1.4 %collective-permute-start.15 = (bf16[128,256]{1,0:T(8,128)(2,1)S(1)}, bf16[128,256]{1,0:T(8,128)(2,1)S(1)}, u32[]{:S(2)}, u32[]{:S(2)}) collective-permute-start(bf16[128,256]{1,0:T(8,128)(2,1)S(1)} %get-tuple-element.50.refs_1_), channel_id=1, source_target_pairs={{0,1},{1,0},{2,3},{3,2},{4,5},{5,4},{6,7},{7,6},{8,9},{9,8},{10,11... | collective-permute-start | bytes 196616 | tf_op jit(solution)/shard_map/ppermute | solution.py:406
  60.4 1.6 %collective-permute-done.11.refs_0_ = bf16[128,256]{1,0:T(8,128)(2,1)S(1)} collective-permute-done((bf16[128,256]{1,0:T(8,128)(2,1)S(1)}, bf16[128,256]{1,0:T(8,128)(2,1)S(1)}, u32[]{:S(2)}, u32[]{:S(2)}) %collective-permute-start.11) | collective-permute-done | bytes 65568 | tf_op jit(solution)/shard_map/ppermute | solution.py:389
  62.0 2.0 %collective-permute-done.12.refs_1_ = bf16[128,256]{1,0:T(8,128)(2,1)S(1)} collective-permute-done((bf16[128,256]{1,0:T(8,128)(2,1)S(1)}, bf16[128,256]{1,0:T(8,128)(2,1)S(1)}, u32[]{:S(2)}, u32[]{:S(2)}) %collective-permute-start.12) | collective-permute-done | bytes 65568 | tf_op jit(solution)/shard_map/ppermute | solution.py:389
  64.0 1.7 %shard_map.79 = (bf16[128,256]{1,0:T(8,128)(2,1)}, bf16[128,256]{1,0:T(8,128)(2,1)S(1)}, f32[128,256]{1,0:T(8,128)S(1)}, bf16[128,256]{1,0:T(8,128)(2,1)S(1)}, b...) custom-call(s32[1,10]{1,0:T(1,128)S(1)} %copy-done.11, ...), custom_call_target="tpu_custom_call" | custom-call | tf_op jit(solution)/shard_map/pallas_call | solution.py:423
  65.6 2.7 %collective-permute-start.18 = (bf16[128,256]{1,0:T(8,128)(2,1)S(1)}, bf16[128,256]{1,0:T(8,128)(2,1)S(1)}, u32[]{:S(2)}, u32[]{:S(2)}) collective-permute-start(bf16[128,256]{1,0:T(8,128)(2,1)S(1)} %get-tuple-element.59), channel_id=1, source_target_pairs={{0,28},{2,30},{4,8},{6,10},{8,4},{10,6},{12,16},{14,18},{16,12},{1... | collective-permute-start | bytes 196616 | tf_op jit(solution)/shard_map/ppermute | solution.py:389
  69.8 1.2 %collective-permute-start.17 = (bf16[128,256]{1,0:T(8,128)(2,1)S(1)}, bf16[128,256]{1,0:T(8,128)(2,1)S(1)}, u32[]{:S(2)}, u32[]{:S(2)}) collective-permute-start(bf16[128,256]{1,0:T(8,128)(2,1)S(1)} %get-tuple-element.57.refs_2_), channel_id=1, source_target_pairs={{0,1},{1,0},{2,3},{3,2},{4,5},{5,4},{6,7},{7,6},{8,9},{9,8},{10,11... | collective-permute-start | bytes 196616 | tf_op jit(solution)/shard_map/ppermute | solution.py:406
  71.0 1.7 %collective-permute-done.18.refs_0_ = bf16[128,256]{1,0:T(8,128)(2,1)S(1)} collective-permute-done((bf16[128,256]{1,0:T(8,128)(2,1)S(1)}, bf16[128,256]{1,0:T(8,128)(2,1)S(1)}, u32[]{:S(2)}, u32[]{:S(2)}) %collective-permute-start.18) | collective-permute-done | bytes 65568 | tf_op jit(solution)/shard_map/ppermute | solution.py:389
  72.7 1.0 %collective-permute-start.16 = (bf16[128,256]{1,0:T(8,128)(2,1)S(1)}, bf16[128,256]{1,0:T(8,128)(2,1)S(1)}, u32[]{:S(2)}, u32[]{:S(2)}) collective-permute-start(bf16[128,256]{1,0:T(8,128)(2,1)S(1)} %get-tuple-element.43.refs_0_), channel_id=1, source_target_pairs={{0,1},{1,0},{2,3},{3,2},{4,5},{5,4},{6,7},{7,6},{8,9},{9,8},{10,11... | collective-permute-start | bytes 196616 | tf_op jit(solution)/shard_map/ppermute | solution.py:406
  73.7 1.0 %collective-permute-done.19.refs_1_ = bf16[128,256]{1,0:T(8,128)(2,1)S(1)} collective-permute-done((bf16[128,256]{1,0:T(8,128)(2,1)S(1)}, bf16[128,256]{1,0:T(8,128)(2,1)S(1)}, u32[]{:S(2)}, u32[]{:S(2)}) %collective-permute-start.19) | collective-permute-done | bytes 65568 | tf_op jit(solution)/shard_map/ppermute | solution.py:389
  75.5 1.3 %collective-permute-start.22 = (bf16[128,256]{1,0:T(8,128)(2,1)S(1)}, bf16[128,256]{1,0:T(8,128)(2,1)S(1)}, u32[]{:S(2)}, u32[]{:S(2)}) collective-permute-start(bf16[128,256]{1,0:T(8,128)(2,1)S(1)} %shard_map.81.mine), channel_id=1, source_target_pairs={{0,1},{1,0},{2,3},{3,2},{4,5},{5,4},{6,7},{7,6},{8,9},{9,8},{10,11... | collective-permute-start | bytes 196616 | tf_op jit(solution)/shard_map/ppermute | solution.py:406
  77.8 2.0 %collective-permute-done.22.far = bf16[128,256]{1,0:T(8,128)(2,1)S(1)} collective-permute-done((bf16[128,256]{1,0:T(8,128)(2,1)S(1)}, bf16[128,256]{1,0:T(8,128)(2,1)S(1)}, u32[]{:S(2)}, u32[]{:S(2)}) %collective-permute-start.22) | collective-permute-done | bytes 65568 | tf_op jit(solution)/shard_map/ppermute | solution.py:406
  (52 shorter events, 11.3 us)
Async XLA Ops:
  0.9 11.8 %collective-permute-start = (bf16[3,256,128]{2,1,0:T(8,128)(2,1)S(1)}, bf16[3,256,128]{2,1,0:T(8,128)(2,1)S(1)}, u32[]{:S(2)}, u32[]{:S(2)}) collective-permute-start(bf16[3,256,128]{2,1,0:T(8,128)(2,1)S(1)} %slice.3), channel_id=1, source_target_pairs={{0,1},{1,0},{2,3},{3,2},{4,5},{5,4},{6,7},{7,6},{8,9},{9,8},{10,11... | collective-permute-start | bytes 589832 | tf_op jit(solution)/shard_map/ppermute | solution.py:335
  6.7 31.2 %all-to-all-start = ((bf16[16,16,384]{2,1,0:T(8,128)(2,1)}), bf16[16,16,384]{2,1,0:T(8,128)(2,1)}, u32[]{:S(2)}, u32[]{:S(2)}) async-start(bf16[16,16,384]{2,1,0:T(8,128)(2,1)} %bitcast.9), calls=%async_computation | async-start | bytes 393216 | tf_op jit(solution)/shard_map/all_to_all | solution.py:350
  13.4 1.2 %copy-start = (bf16[15,256,128]{2,1,0:T(8,128)(2,1)S(1)}, bf16[15,256,128]{2,1,0:T(8,128)(2,1)}, u32[]{:S(2)}) copy-start(bf16[15,256,128]{2,1,0:T(8,128)(2,1)} %history.1) | copy-start | bytes 2949124
  14.6 0.9 %copy-start.10 = (bf16[3,256,128]{2,1,0:T(8,128)(2,1)S(1)}, bf16[3,256,128]{2,1,0:T(8,128)(2,1)}, u32[]{:S(2)}) copy-start(bf16[3,256,128]{2,1,0:T(8,128)(2,1)} %copy-done.9) | copy-start | bytes 589828
  15.5 25.0 %copy-start.11 = (s32[1,10]{1,0:T(1,128)S(1)}, s32[1,10]{1,0:T(1,128)}, u32[]{:S(2)}) copy-start(s32[1,10]{1,0:T(1,128)} %ranges.9) | copy-start | bytes 124
  24.0 16.5 %collective-permute-start.6 = (bf16[640,256]{1,0:T(8,128)(2,1)}, bf16[640,256]{1,0:T(8,128)(2,1)}, u32[]{:S(2)}, u32[]{:S(2)}) collective-permute-start(bf16[640,256]{1,0:T(8,128)(2,1)} %get-tuple-element.42), channel_id=1, source_target_pairs={{0,1},{1,0},{2,3},{3,2},{4,5},{5,4},{6,7},{7,6},{8,9},{9,8},{10,11... | collective-permute-start | bytes 983048 | tf_op jit(solution)/shard_map/ppermute | solution.py:306
  24.1 7.3 %collective-permute-start.1 = (bf16[128,256]{1,0:T(8,128)(2,1)}, bf16[128,256]{1,0:T(8,128)(2,1)S(1)}, u32[]{:S(2)}, u32[]{:S(2)}) collective-permute-start(bf16[128,256]{1,0:T(8,128)(2,1)} %get-tuple-element.36), channel_id=1, source_target_pairs={{0,28},{2,30},{4,8},{6,10},{8,4},{10,6},{12,16},{14,18},{16,12},{1... | collective-permute-start | bytes 196616 | tf_op jit(solution)/shard_map/ppermute | solution.py:389
  28.0 6.6 %collective-permute-start.2 = (bf16[128,256]{1,0:T(8,128)(2,1)}, bf16[128,256]{1,0:T(8,128)(2,1)S(1)}, u32[]{:S(2)}, u32[]{:S(2)}) collective-permute-start(bf16[128,256]{1,0:T(8,128)(2,1)} %get-tuple-element.37), channel_id=1, source_target_pairs={{0,30},{2,4},{4,2},{6,8},{8,6},{10,12},{12,10},{14,16},{16,14},{18... | collective-permute-start | bytes 196616 | tf_op jit(solution)/shard_map/ppermute | solution.py:389
  28.0 6.6 %collective-permute-start.3 = (bf16[128,256]{1,0:T(8,128)(2,1)}, bf16[128,256]{1,0:T(8,128)(2,1)S(1)}, u32[]{:S(2)}, u32[]{:S(2)}) collective-permute-start(bf16[128,256]{1,0:T(8,128)(2,1)} %get-tuple-element.38), channel_id=1, source_target_pairs={{0,4},{2,6},{4,0},{6,2},{8,12},{10,14},{12,8},{14,10},{16,20},{18,... | collective-permute-start | bytes 196616 | tf_op jit(solution)/shard_map/ppermute | solution.py:389
  29.2 5.4 %collective-permute-start.4 = (bf16[128,256]{1,0:T(8,128)(2,1)}, bf16[128,256]{1,0:T(8,128)(2,1)S(1)}, u32[]{:S(2)}, u32[]{:S(2)}) collective-permute-start(bf16[128,256]{1,0:T(8,128)(2,1)} %get-tuple-element.39), channel_id=1, source_target_pairs={{0,2},{2,0},{4,6},{6,4},{8,10},{10,8},{12,14},{14,12},{16,18},{18,... | collective-permute-start | bytes 196616 | tf_op jit(solution)/shard_map/ppermute | solution.py:389
  34.6 0.7 copy-start.3
  36.0 4.6 %collective-permute-start.5 = (bf16[128,256]{1,0:T(8,128)(2,1)}, bf16[128,256]{1,0:T(8,128)(2,1)}, u32[]{:S(2)}, u32[]{:S(2)}) collective-permute-start(bf16[128,256]{1,0:T(8,128)(2,1)} %shard_map.76), channel_id=1, source_target_pairs={{0,1},{1,0},{2,3},{3,2},{4,5},{5,4},{6,7},{7,6},{8,9},{9,8},{10,11... | collective-permute-start | bytes 196616 | tf_op jit(solution)/shard_map/ppermute | solution.py:399
  40.5 0.8 %copy-start.2 = (bf16[128,256]{1,0:T(8,128)(2,1)S(1)}, bf16[128,256]{1,0:T(8,128)(2,1)}, u32[]{:S(2)}) copy-start(bf16[128,256]{1,0:T(8,128)(2,1)} %copy-done.1) | copy-start | bytes 196612
  41.4 0.8 %copy-start.4 = (bf16[128,256]{1,0:T(8,128)(2,1)S(1)}, bf16[128,256]{1,0:T(8,128)(2,1)}, u32[]{:S(2)}) copy-start(bf16[128,256]{1,0:T(8,128)(2,1)} %copy-done.3) | copy-start | bytes 196612
  42.2 0.8 %copy-start.6 = (bf16[128,256]{1,0:T(8,128)(2,1)S(1)}, bf16[128,256]{1,0:T(8,128)(2,1)}, u32[]{:S(2)}) copy-start(bf16[128,256]{1,0:T(8,128)(2,1)} %copy-done.5) | copy-start | bytes 196612
  43.1 0.8 %copy-start.8 = (bf16[128,256]{1,0:T(8,128)(2,1)S(1)}, bf16[128,256]{1,0:T(8,128)(2,1)}, u32[]{:S(2)}) copy-start(bf16[128,256]{1,0:T(8,128)(2,1)} %copy-done.7) | copy-start | bytes 196612
  45.3 7.1 %collective-permute-start.7 = (bf16[128,256]{1,0:T(8,128)(2,1)S(1)}, bf16[128,256]{1,0:T(8,128)(2,1)S(1)}, u32[]{:S(2)}, u32[]{:S(2)}) collective-permute-start(bf16[128,256]{1,0:T(8,128)(2,1)S(1)} %get-tuple-element.45), channel_id=1, source_target_pairs={{0,28},{2,30},{4,8},{6,10},{8,4},{10,6},{12,16},{14,18},{16,12},{1... | collective-permute-start | bytes 196616 | tf_op jit(solution)/shard_map/ppermute | solution.py:389
  47.5 6.4 %collective-permute-start.8 = (bf16[128,256]{1,0:T(8,128)(2,1)S(1)}, bf16[128,256]{1,0:T(8,128)(2,1)S(1)}, u32[]{:S(2)}, u32[]{:S(2)}) collective-permute-start(bf16[128,256]{1,0:T(8,128)(2,1)S(1)} %get-tuple-element.46), channel_id=1, source_target_pairs={{0,30},{2,4},{4,2},{6,8},{8,6},{10,12},{12,10},{14,16},{16,14},{18... | collective-permute-start | bytes 196616 | tf_op jit(solution)/shard_map/ppermute | solution.py:389
  47.5 6.4 %collective-permute-start.9 = (bf16[128,256]{1,0:T(8,128)(2,1)S(1)}, bf16[128,256]{1,0:T(8,128)(2,1)S(1)}, u32[]{:S(2)}, u32[]{:S(2)}) collective-permute-start(bf16[128,256]{1,0:T(8,128)(2,1)S(1)} %get-tuple-element.47), channel_id=1, source_target_pairs={{0,4},{2,6},{4,0},{6,2},{8,12},{10,14},{12,8},{14,10},{16,20},{18,... | collective-permute-start | bytes 196616 | tf_op jit(solution)/shard_map/ppermute | solution.py:389
  48.5 5.3 %collective-permute-start.10 = (bf16[128,256]{1,0:T(8,128)(2,1)S(1)}, bf16[128,256]{1,0:T(8,128)(2,1)S(1)}, u32[]{:S(2)}, u32[]{:S(2)}) collective-permute-start(bf16[128,256]{1,0:T(8,128)(2,1)S(1)} %get-tuple-element.48), channel_id=1, source_target_pairs={{0,2},{2,0},{4,6},{6,4},{8,10},{10,8},{12,14},{14,12},{16,18},{18,... | collective-permute-start | bytes 196616 | tf_op jit(solution)/shard_map/ppermute | solution.py:389
  54.9 7.1 %collective-permute-start.11 = (bf16[128,256]{1,0:T(8,128)(2,1)S(1)}, bf16[128,256]{1,0:T(8,128)(2,1)S(1)}, u32[]{:S(2)}, u32[]{:S(2)}) collective-permute-start(bf16[128,256]{1,0:T(8,128)(2,1)S(1)} %get-tuple-element.52), channel_id=1, source_target_pairs={{0,28},{2,30},{4,8},{6,10},{8,4},{10,6},{12,16},{14,18},{16,12},{1... | collective-permute-start | bytes 196616 | tf_op jit(solution)/shard_map/ppermute | solution.py:389
  57.6 6.4 %collective-permute-start.12 = (bf16[128,256]{1,0:T(8,128)(2,1)S(1)}, bf16[128,256]{1,0:T(8,128)(2,1)S(1)}, u32[]{:S(2)}, u32[]{:S(2)}) collective-permute-start(bf16[128,256]{1,0:T(8,128)(2,1)S(1)} %get-tuple-element.53), channel_id=1, source_target_pairs={{0,30},{2,4},{4,2},{6,8},{8,6},{10,12},{12,10},{14,16},{16,14},{18... | collective-permute-start | bytes 196616 | tf_op jit(solution)/shard_map/ppermute | solution.py:389
  57.6 6.4 %collective-permute-start.13 = (bf16[128,256]{1,0:T(8,128)(2,1)S(1)}, bf16[128,256]{1,0:T(8,128)(2,1)S(1)}, u32[]{:S(2)}, u32[]{:S(2)}) collective-permute-start(bf16[128,256]{1,0:T(8,128)(2,1)S(1)} %get-tuple-element.54), channel_id=1, source_target_pairs={{0,4},{2,6},{4,0},{6,2},{8,12},{10,14},{12,8},{14,10},{16,20},{18,... | collective-permute-start | bytes 196616 | tf_op jit(solution)/shard_map/ppermute | solution.py:389
  59.0 4.9 %collective-permute-start.14 = (bf16[128,256]{1,0:T(8,128)(2,1)S(1)}, bf16[128,256]{1,0:T(8,128)(2,1)S(1)}, u32[]{:S(2)}, u32[]{:S(2)}) collective-permute-start(bf16[128,256]{1,0:T(8,128)(2,1)S(1)} %get-tuple-element.55), channel_id=1, source_target_pairs={{0,2},{2,0},{4,6},{6,4},{8,10},{10,8},{12,14},{14,12},{16,18},{18,... | collective-permute-start | bytes 196616 | tf_op jit(solution)/shard_map/ppermute | solution.py:389
  59.0 4.9 %collective-permute-start.15 = (bf16[128,256]{1,0:T(8,128)(2,1)S(1)}, bf16[128,256]{1,0:T(8,128)(2,1)S(1)}, u32[]{:S(2)}, u32[]{:S(2)}) collective-permute-start(bf16[128,256]{1,0:T(8,128)(2,1)S(1)} %get-tuple-element.50.refs_1_), channel_id=1, source_target_pairs={{0,1},{1,0},{2,3},{3,2},{4,5},{5,4},{6,7},{7,6},{8,9},{9,8},{10,11... | collective-permute-start | bytes 196616 | tf_op jit(solution)/shard_map/ppermute | solution.py:406
  65.6 7.1 %collective-permute-start.18 = (bf16[128,256]{1,0:T(8,128)(2,1)S(1)}, bf16[128,256]{1,0:T(8,128)(2,1)S(1)}, u32[]{:S(2)}, u32[]{:S(2)}) collective-permute-start(bf16[128,256]{1,0:T(8,128)(2,1)S(1)} %get-tuple-element.59), channel_id=1, source_target_pairs={{0,28},{2,30},{4,8},{6,10},{8,4},{10,6},{12,16},{14,18},{16,12},{1... | collective-permute-start | bytes 196616 | tf_op jit(solution)/shard_map/ppermute | solution.py:389
  68.3 6.4 %collective-permute-start.19 = (bf16[128,256]{1,0:T(8,128)(2,1)S(1)}, bf16[128,256]{1,0:T(8,128)(2,1)S(1)}, u32[]{:S(2)}, u32[]{:S(2)}) collective-permute-start(bf16[128,256]{1,0:T(8,128)(2,1)S(1)} %get-tuple-element.60), channel_id=1, source_target_pairs={{0,30},{2,4},{4,2},{6,8},{8,6},{10,12},{12,10},{14,16},{16,14},{18... | collective-permute-start | bytes 196616 | tf_op jit(solution)/shard_map/ppermute | solution.py:389
  68.9 5.8 %collective-permute-start.20 = (bf16[128,256]{1,0:T(8,128)(2,1)S(1)}, bf16[128,256]{1,0:T(8,128)(2,1)S(1)}, u32[]{:S(2)}, u32[]{:S(2)}) collective-permute-start(bf16[128,256]{1,0:T(8,128)(2,1)S(1)} %get-tuple-element.61), channel_id=1, source_target_pairs={{0,4},{2,6},{4,0},{6,2},{8,12},{10,14},{12,8},{14,10},{16,20},{18,... | collective-permute-start | bytes 196616 | tf_op jit(solution)/shard_map/ppermute | solution.py:389
  69.8 4.9 %collective-permute-start.21 = (bf16[128,256]{1,0:T(8,128)(2,1)S(1)}, bf16[128,256]{1,0:T(8,128)(2,1)S(1)}, u32[]{:S(2)}, u32[]{:S(2)}) collective-permute-start(bf16[128,256]{1,0:T(8,128)(2,1)S(1)} %get-tuple-element.62), channel_id=1, source_target_pairs={{0,2},{2,0},{4,6},{6,4},{8,10},{10,8},{12,14},{14,12},{16,18},{18,... | collective-permute-start | bytes 196616 | tf_op jit(solution)/shard_map/ppermute | solution.py:389
  69.8 5.0 %collective-permute-start.17 = (bf16[128,256]{1,0:T(8,128)(2,1)S(1)}, bf16[128,256]{1,0:T(8,128)(2,1)S(1)}, u32[]{:S(2)}, u32[]{:S(2)}) collective-permute-start(bf16[128,256]{1,0:T(8,128)(2,1)S(1)} %get-tuple-element.57.refs_2_), channel_id=1, source_target_pairs={{0,1},{1,0},{2,3},{3,2},{4,5},{5,4},{6,7},{7,6},{8,9},{9,8},{10,11... | collective-permute-start | bytes 196616 | tf_op jit(solution)/shard_map/ppermute | solution.py:406
  72.7 4.3 %collective-permute-start.16 = (bf16[128,256]{1,0:T(8,128)(2,1)S(1)}, bf16[128,256]{1,0:T(8,128)(2,1)S(1)}, u32[]{:S(2)}, u32[]{:S(2)}) collective-permute-start(bf16[128,256]{1,0:T(8,128)(2,1)S(1)} %get-tuple-element.43.refs_0_), channel_id=1, source_target_pairs={{0,1},{1,0},{2,3},{3,2},{4,5},{5,4},{6,7},{7,6},{8,9},{9,8},{10,11... | collective-permute-start | bytes 196616 | tf_op jit(solution)/shard_map/ppermute | solution.py:406
  75.5 4.3 %collective-permute-start.22 = (bf16[128,256]{1,0:T(8,128)(2,1)S(1)}, bf16[128,256]{1,0:T(8,128)(2,1)S(1)}, u32[]{:S(2)}, u32[]{:S(2)}) collective-permute-start(bf16[128,256]{1,0:T(8,128)(2,1)S(1)} %shard_map.81.mine), channel_id=1, source_target_pairs={{0,1},{1,0},{2,3},{3,2},{4,5},{5,4},{6,7},{7,6},{8,9},{9,8},{10,11... | collective-permute-start | bytes 196616 | tf_op jit(solution)/shard_map/ppermute | solution.py:406
  (4 other events, 2.7 us)

commit v6 on v4

--- a/solution.py
+++ b/solution.py
@@ -11,6 +11,7 @@
 CAP = 16
 HALF = NEAR // 2
 FIRST = 2
+PIECES = 2
 LANES = 128
 VMEM = pltpu.VMEM
 FAR_LIMIT = 40 << 20
@@ -35,21 +36,18 @@
     return [list(enumerate(p)) for p in (far, odd_even, near, core)]
 
 
-def pack_kernel(tile_hbm, panel_hbm, history, rows_ref, out_ref, edge, tile_ref, panel_ref, sems):
+def pack_kernel(tile_hbm, panel_hbm, rows_ref, out_hbm, tile_ref, panel_ref, sems, out_ref, out_sem):
     copies = [
         pltpu.make_async_copy(tile_hbm, tile_ref, sems.at[0]),
         pltpu.make_async_copy(panel_hbm, panel_ref, sems.at[1]),
-        pltpu.make_async_copy(
-            history.at[pl.ds(history.shape[0] - edge.shape[0], edge.shape[0])], edge, sems.at[2]
-        ),
     ]
     for copy in copies:
         copy.start()
-    for copy in copies[:2]:
+    for copy in copies:
         copy.wait()
     recv = rows_ref.shape[0]
-    width = rows_ref.shape[1]
-    slots = out_ref.shape[0]
+    slots, width = out_ref.shape
+    width = width - LANES
     patches = slots // CAP
     tile = tile_ref[...]
     hot = lax.broadcasted_iota(jnp.int32, (patches, recv), 0) == tile
@@ -62,17 +60,20 @@
     slot = tile * CAP + earlier
     placed = lax.broadcasted_iota(jnp.int32, (slots, recv), 0) == slot
     placer = jnp.where(placed, 1.0, 0.0).astype(jnp.bfloat16)
-    out_ref[:, :width] = dot(placer, rows_ref[...]).astype(jnp.bfloat16)
+    piece = lax.rem(lax.axis_index("lag"), rows_ref.shape[1] // width)
+    rows = rows_ref[:, pl.ds(pl.multiple_of(piece * width, width), width)]
+    out_ref[:, :width] = dot(placer, rows).astype(jnp.bfloat16)
     marks = jnp.where(placed, (panel_ref[...] + 1).astype(jnp.float32), 0.0)
     label = jnp.sum(marks, axis=1, keepdims=True)
     out_ref[:, width:] = jnp.broadcast_to(label, (slots, LANES)).astype(jnp.bfloat16)
-    copies[2].wait()
-
-
-def source_kernel(arrived_ref, *outs):
+    copy = pltpu.make_async_copy(out_ref, out_hbm, out_sem)
+    copy.start()
+    copy.wait()
+
+
+def source_kernel(shots, arrived_ref, out):
     slots = arrived_ref.shape[0]
-    shots, tile_len = outs[0].shape
-    width = len(outs) * shots
+    width, tile_len = out.shape
     label = arrived_ref[:, width:].astype(jnp.float32)
     lane = lax.broadcasted_iota(jnp.int32, (slots, LANES), 1)
     picker = jnp.concatenate(
@@ -82,9 +83,9 @@
         ],
         axis=1,
     ).astype(jnp.bfloat16)
-    for step, out in enumerate(outs):
-        out[...] = lax.dot_general(
-            arrived_ref[:, step * shots : (step + 1) * shots],
+    for first in range(0, width, shots):
+        out[first : first + shots, :] = lax.dot_general(
+            arrived_ref[:, first : first + shots],
             picker,
             (((0,), (0,)), ((), ())),
             preferred_element_type=jnp.float32,
@@ -146,30 +147,10 @@
     lax.fori_loop(0, len(slots), one_slot, None)
 
 
-def far_kernel(steps, sizes, ranges, rim, history_hbm, inverse_hbm, weights, *refs):
-    far_message, odd_message, stage, rows, later, recent, inverse = refs[:7]
-    blocks, history, sems, keep_sems, out_sems = refs[7:]
-    band, tile_len, shots = history.shape
+def transposed(rows, history, rim, steps):
+    band, _, shots = history.shape
+    tile_len = rows.shape[1]
     lag = lax.axis_index("lag")
-    offsets = slot_offsets(lax.axis_index("patch"))
-
-    def fetch(slot, offset, k):
-        columns = pl.ds(pl.multiple_of(offset * tile_len, tile_len), tile_len)
-        place = blocks.at[slot, k] if slot < FIRST else later.at[slot - FIRST, k]
-        return pltpu.make_async_copy(weights.at[k, :, columns], place, sems.at[slot, k])
-
-    keep = [
-        pltpu.make_async_copy(history_hbm, history, keep_sems.at[0]),
-        pltpu.make_async_copy(weights.at[pl.ds(0, steps - 1)], recent, keep_sems.at[1]),
-        pltpu.make_async_copy(inverse_hbm, inverse, keep_sems.at[2]),
-    ]
-    keep[0].start()
-    for slot, offset in enumerate(offsets):
-        first, last = active(ranges, offset, lag, band)
-        lax.fori_loop(first, last, lambda k, c, s=slot, o=offset: fetch(s, o, k).start(), None)
-    keep[1].start()
-    keep[2].start()
-    keep[0].wait()
     for k in range(band):
         rows[(band - 1 - k) * shots : (band - k) * shots, :] = history[k].T
 
@@ -183,15 +164,42 @@
     def _():
         rows[band * shots :, :] = jnp.zeros(((steps - 1) * shots, tile_len), jnp.bfloat16)
 
+
+def fetcher(ranges, slots, weights, blocks, sems):
+    band, tile_len = blocks.shape[1:3]
+    lag = lax.axis_index("lag")
+    offsets = slot_offsets(lax.axis_index("patch"))
+
+    def fetch(index, offset, k):
+        columns = pl.ds(pl.multiple_of(offset * tile_len, tile_len), tile_len)
+        return pltpu.make_async_copy(
+            weights.at[k, :, columns], blocks.at[index, k], sems.at[index, k]
+        )
+
+    def fetch_all():
+        for index, slot in enumerate(slots):
+            first, last = active(ranges, offsets[slot], lag, band)
+            lax.fori_loop(
+                first, last, lambda k, c, i=index, o=offsets[slot]: fetch(i, o, k).start(), None
+            )
+
     def arrive(index, first, last, offset):
-        def wait(k, carry):
-            columns = pl.ds(pl.multiple_of(offset * tile_len, tile_len), tile_len)
-            pltpu.make_async_copy(
-                weights.at[k, :, columns], blocks.at[index, k], sems.at[index, k]
-            ).wait()
-            return carry
-
-        lax.fori_loop(first, last, wait, None)
+        lax.fori_loop(first, last, lambda k, c: fetch(index, offset, k).wait(), None)
+
+    return fetch_all, arrive
+
+
+def far_kernel(steps, sizes, ranges, rim, history_hbm, weights, *refs):
+    far_message, odd_message, stage = refs[:3]
+    rows, blocks, history, sems, keep_sem, out_sems = refs[3:]
+    shots = history.shape[2]
+
+    held = pltpu.make_async_copy(history_hbm, history, keep_sem)
+    held.start()
+    fetch_all, arrive = fetcher(ranges, range(FIRST), weights, blocks, sems)
+    fetch_all()
+    held.wait()
+    transposed(rows, history, rim, steps)
 
     targets = (far_message, odd_message)
 
@@ -205,17 +213,19 @@
             pl.when(index == i)(lambda i=i: send(i).start())
 
     history_terms(ranges, range(FIRST), sizes, shots, rows, blocks, stage, arrive, emitted)
-    for slot in range(FIRST, NEAR):
-        first, last = active(ranges, offsets[slot], lag, band)
-        lax.fori_loop(first, last, lambda k, c, s=slot: fetch(s, offsets[s], k).wait(), None)
-    keep[1].wait()
-    keep[2].wait()
     for index in range(FIRST):
         send(index).wait()
 
 
-def near_kernel(sizes, ranges, rows, blocks, far_stage, *refs):
-    near_message, core_message, own, stage, rest, out_sems = refs
+def near_kernel(steps, sizes, ranges, rim, far_stage, history_hbm, weights, *refs):
+    near_message, core_message, own, stage, rest, recent = refs[:6]
+    rows, blocks, history, sems, keep_sems, out_sems = refs[6:]
+    past = pltpu.make_async_copy(history_hbm, history, keep_sems.at[1])
+    past.start()
+    fetch_all, arrive = fetcher(ranges, range(FIRST, NEAR), weights, blocks, sems)
+    fetch_all()
+    held = pltpu.make_async_copy(weights.at[pl.ds(0, recent.shape[0])], recent, keep_sems.at[0])
+    held.start()
     shots = own.shape[0]
     targets = (near_message, core_message)
 
@@ -244,13 +254,25 @@
                 else:
                     own[...] = total[:shots]
 
+    past.wait()
+    transposed(rows, history, rim, steps)
     history_terms(
-        ranges, range(FIRST, NEAR), sizes, shots, rows, blocks, stage, lambda *_: None, emitted
+        ranges, range(FIRST, NEAR), sizes, shots, rows, blocks, stage, arrive, emitted
     )
+    held.wait()
     for slot in range(NEAR):
         pass_on(slot).wait()
     for index in range(len(targets)):
         send(index).wait()
+
+
+def sum_kernel(own, *refs):
+    blocks, (total_ref, half) = refs[:-2], refs[-2:]
+    total = own[...]
+    for block in blocks:
+        total = total + block[...].astype(jnp.float32)
+    total_ref[...] = total
+    half[...] = total.astype(jnp.bfloat16)
 
 
 def step_kernel(step, last_step, ranges, source, inverse, own, *refs):
@@ -260,7 +282,8 @@
     total = own[...]
     for block in received:
         total = total + block[...].astype(jnp.float32)
-    right = source[...] - total
+    known = source.shape[0] // shots
+    right = source[step * shots : (step + 1) * shots, :] - total if step < known else -total
     if step != 1:
         right = right - refs.pop(0)[...].astype(jnp.float32)
     density = dot(right.astype(jnp.bfloat16), inverse[...])
@@ -277,6 +300,10 @@
     band_zero = lax.axis_index("lag") == 0
     for density_ref in outs[NEAR + 1 :]:
         density_ref[...] = rounded
+    if step + 1 >= known:
+        at = (step + 1 - known) * shots
+        carried = jnp.where(lax.axis_index("lag") == 1, source[at : at + shots, :], 0.0)
+        total = total - carried
     cross[...] = jnp.where(band_zero, density, total).astype(jnp.bfloat16)
     recent = [rounded] + [ref[...] for ref in olders]
     steps = far_stage.shape[1] // shots
@@ -379,69 +406,76 @@
     f32, bf16 = jnp.float32, jnp.bfloat16
     block = (shots, tile_len)
     routes = pairings(patches)
-
-    outgoing, edge = call(
+    piece = width // PIECES
+
+    rim = lax.ppermute(
+        history[band - steps + 1 :], "lag", [(i, (i + 1) % lags) for i in range(lags)]
+    )
+    (outgoing,) = call(
         pack_kernel,
-        [((patches * CAP, width + LANES), bf16), ((steps - 1, tile_len, shots), bf16)],
-        [pltpu.HBM] * 3 + [VMEM],
-        [VMEM((1, recv), jnp.int32)] * 2 + [pltpu.SemaphoreType.DMA((3,))],
-        out_specs=[VMEM, pl.ANY],
+        [((patches * CAP, piece + LANES), bf16, pltpu.HBM)],
+        [pltpu.HBM] * 2 + [VMEM],
+        [VMEM((1, recv), jnp.int32)] * 2 + [pltpu.SemaphoreType.DMA((2,))]
+        + [VMEM((patches * CAP, piece + LANES), bf16), pltpu.SemaphoreType.DMA],
+        out_specs=[pltpu.HBM],
     )(
         far_memory(receiver_tile.reshape(1, recv)),
         far_memory(receiver_panel.reshape(1, recv)),
-        far_memory(history),
         residuals.reshape(recv, width),
     )
-    rim = lax.ppermute(edge, "lag", [(i, (i + 1) % lags) for i in range(lags)])
     arrived = lax.all_to_all(
-        outgoing.reshape(patches, CAP, width + LANES),
+        outgoing.reshape(patches, CAP, piece + LANES),
         "patch",
         split_axis=0,
         concat_axis=0,
         tiled=True,
-    ).reshape(patches * CAP, width + LANES)
-    source = call(source_kernel, [(block, f32, VMEM)] * steps, [VMEM])(arrived)
-    source = [near_memory(s) for s in source]
+    ).reshape(patches * CAP, piece + LANES)
+    (source,) = call(
+        functools.partial(source_kernel, shots), [((piece, tile_len), f32, VMEM)], [VMEM]
+    )(arrived)
+    source = near_memory(source)
 
     sizes = [*range(2, band, 2), band]
     older_rows = ((band + steps - 1) * shots, tile_len)
-    *first, far_stage, rows, later, recent, inverse = call(
+    *first, far_stage = call(
         functools.partial(far_kernel, steps, sizes),
         [(block, bf16, pltpu.HBM)] * FIRST
-        + [
-            ((FIRST, width, tile_len), bf16, VMEM),
-            (older_rows, bf16, VMEM),
-            ((NEAR - FIRST, band, tile_len, tile_len), bf16, VMEM),
-            ((steps - 1, tile_len, NEAR * tile_len), bf16, VMEM),
-            ((tile_len, tile_len), bf16, VMEM),
-        ],
-        [pltpu.SMEM, VMEM] + [pltpu.HBM] * 3,
+        + [((FIRST, width, tile_len), bf16, VMEM)],
+        [pltpu.SMEM, VMEM] + [pltpu.HBM] * 2,
         [
+            VMEM(older_rows, bf16),
             VMEM((FIRST, band, tile_len, tile_len), bf16),
             VMEM((band, tile_len, shots), bf16),
-            pltpu.SemaphoreType.DMA((NEAR, band)),
-            pltpu.SemaphoreType.DMA((3,)),
+            pltpu.SemaphoreType.DMA((FIRST, band)),
+            pltpu.SemaphoreType.DMA,
             pltpu.SemaphoreType.DMA((FIRST,)),
         ],
-        out_specs=[pltpu.HBM] * FIRST + [VMEM] * 5,
+        out_specs=[pltpu.HBM] * FIRST + [VMEM],
         limit=FAR_LIMIT,
-    )(far_memory(lag_ranges), rim, far_memory(history), far_memory(near_inverse), far_memory(interaction))
-    far_stage, rows, later = near_memory(far_stage), near_memory(rows), near_memory(later)
-    recent, inverse = near_memory(recent), near_memory(inverse)
-    *second, own, near_stage, rest = call(
-        functools.partial(near_kernel, sizes),
+    )(far_memory(lag_ranges), far_memory(rim), far_memory(history), far_memory(interaction))
+    far_stage = near_memory(far_stage)
+    *second, own, near_stage, rest, recent = call(
+        functools.partial(near_kernel, steps, sizes),
         [(block, bf16, pltpu.HBM)] * (NEAR - 1 - FIRST)
         + [
-            (block, f32),
+            (block, f32, VMEM),
             ((NEAR - FIRST, width, tile_len), bf16, VMEM),
             ((NEAR * shots, tile_len), bf16, pltpu.HBM),
+            ((steps - 1, tile_len, NEAR * tile_len), bf16, VMEM),
         ],
-        [pltpu.SMEM] + [VMEM] * 3,
-        [pltpu.SemaphoreType.DMA((2, NEAR))],
-        out_specs=[pltpu.HBM] * (NEAR - 1 - FIRST) + [VMEM] * 2 + [pltpu.HBM],
+        [pltpu.SMEM] + [VMEM] * 2 + [pltpu.HBM] * 2,
+        [
+            VMEM(older_rows, bf16),
+            VMEM((NEAR - FIRST, band, tile_len, tile_len), bf16),
+            VMEM((band, tile_len, shots), bf16),
+            pltpu.SemaphoreType.DMA((NEAR - FIRST, band)),
+            pltpu.SemaphoreType.DMA((2,)),
+            pltpu.SemaphoreType.DMA((2, NEAR)),
+        ],
+        out_specs=[pltpu.HBM] * (NEAR - 1 - FIRST) + [VMEM] * 2 + [pltpu.HBM, VMEM],
         limit=NEAR_LIMIT,
-    )(lag_ranges, rows, later, far_stage)
-    near_stage = near_memory(near_stage)
+    )(far_memory(lag_ranges), far_memory(rim), far_stage, far_memory(history), far_memory(interaction))
+    near_stage, recent = near_memory(near_stage), near_memory(recent)
     messages = [*first, *second]
 
     def exchange(blocks):
@@ -450,9 +484,13 @@
             gone.append(lax.ppermute(b, "patch", r))
         return gone
 
-    for incoming in exchange(messages):
-        own = own + incoming.astype(f32)
-    own, far = lag_sum(own, lags)
+    own, half = call(
+        sum_kernel, [(block, f32, pltpu.HBM), (block, bf16)], [VMEM] * NEAR
+    )(near_memory(own), *exchange(messages))
+    if lags == 2:
+        own, far = far_memory(own), lax.ppermute(half, "lag", lag_partners(lags, 1))
+    else:
+        own, far = lag_sum(own, lags)
     here, there = lag_sum(rest, lags)
     if lags > 2:
         there = there + (here - rest)
@@ -465,11 +503,10 @@
         inward, last = lag_sum(jnp.where(lax.axis_index("lag") > 0, block, 0), lags)
         return outward, inward + last
 
-    densities, outward, inward = [], [], [far]
-    received = []
+    densities, outward, inward, received = [], [], [far], []
     for step in range(steps):
         last_step = step == steps - 1
-        inputs = [lag_ranges, source[step], inverse, own, *received]
+        inputs = [lag_ranges, source, near_inverse if step else far_memory(near_inverse), own, *received]
         if step != 1:
             inputs.append(inward[max(step - 1, 0)])
         outs = [(block, bf16)]

time: 80.9 us -> 78.8 us (0.974)
  starting transfers between devices: 34.9 us -> 31.2 us
  Pallas kernels: 18.5 us -> 21.7 us
  waiting for transfers between devices: 25.2 us -> 22.6 us
  local copies, waits for them, and re-layouts: 1 us -> 2.62 us
    ppermute x1 -> x2, waiting for transfers between devices: 5.62 us -> 1.17 us  [the longest x1 1.17 us: local(): lax.ppermute(half, 'lag', lag_partners(lags, 1))]
    ppermute x2 -> x1, starting transfers between devices: 3.81 us -> 0.07 us  [lag_sum(): lax.ppermute(block.astype(jnp.bfloat16), 'lag', lag_partners(lags, distan...]
    ppermute x1 -> x2, starting transfers between devices: 1.55 us -> 4.97 us  [the longest x1 3.03 us: local(): lax.ppermute(history[band - steps + 1:], 'lag', [(i, (i + 1) % lags) for...]
    pallas_call x3 -> x4, Pallas kernels: 7.27 us -> 10.5 us  [the longest x1 6.93 us: local(): call(functools.partial(near_kernel, steps, sizes), [(block, bf16, pltpu.H...]
    ppermute x16, waiting for transfers between devices: 15.5 us -> 18.6 us  [exchange(): gone.append(lax.ppermute(b, 'patch', r))]
    ppermute x2 -> x1, waiting for transfers between devices: 2.09 us -> 0.01 us  [lag_sum(): lax.ppermute(block.astype(jnp.bfloat16), 'lag', lag_partners(lags, distan...]
    ppermute x16, starting transfers between devices: 17.9 us -> 15.9 us  [exchange(): gone.append(lax.ppermute(b, 'patch', r))]
    all_to_all x1, starting transfers between devices: 7.47 us -> 6 us  [local(): lax.all_to_all(outgoing.reshape(patches, CAP, piece + LANES), 'patch', sp...]
  transfers between devices with their start and end apart: 24 -> 24, of which waited for: 11 -> 10; matrix products, arithmetic and copies ran while one was open for 1% -> 1% of each run, Pallas kernels for 15% -> 22%
where the time goes in v6:
time: 78.8 us; the launch traced here: 78.4 us
  starting transfers between devices  31.2 us (40%)
  waiting for transfers between devices  22.6 us (29%)
  Pallas kernels  21.7 us (28%)
  local copies, waits for them, and re-layouts  2.62 us (3%)
    ppermute x16, waiting for transfers between devices, exchange(): gone.append(lax.ppermute(b, 'patch', r))  18.6 us
    ppermute x16, starting transfers between devices, exchange(): gone.append(lax.ppermute(b, 'patch', r))  15.9 us
    pallas_call x1, Pallas kernels, local(): call(functools.partial(near_kernel, steps, sizes), [(block, bf16, pltpu.H...  6.93 us
    all_to_all x1, starting transfers between devices, local(): lax.all_to_all(outgoing.reshape(patches, CAP, piece + LANES), 'patch', sp...  6 us
    pallas_call x1, Pallas kernels, local(): call(functools.partial(far_kernel, steps, sizes), [(block, bf16, pltpu.HB...  5.17 us
    pallas_call x4, Pallas kernels, local(): call(functools.partial(step_kernel, step, last_step), outs, [pltpu.SMEM]...  4.39 us
    ppermute x4, starting transfers between devices, cross_bands(): swapped = lax.ppermute(block, 'lag', lag_partners(lags, 1))  4.25 us
    ppermute x1, starting transfers between devices, local(): lax.ppermute(history[band - steps + 1:], 'lag', [(i, (i + 1) % lags) for...  3.03 us
  transfers between devices with their start and end apart: 24, of which 10 were waited for; matrix products, arithmetic and copies ran while one was open for 1% of the time, Pallas kernels for 22%

profile of v6, /device:TPU:0, one launch (start us, length us, event | category | flops | bytes accessed | tf_op | source)
XLA Modules:
  0.0 78.4 jit_solution(5125042904391099926)
XLA Ops:
  0.0 0.9 %slice.3 = bf16[3,256,128]{2,1,0:T(8,128)(2,1)S(1)} slice(bf16[15,256,128]{2,1,0:T(8,128)(2,1)} %history_hbm.3), slice={[12:15], [0:256], [0:128]} | slice | bytes 393216 | tf_op jit(solution)/shard_map/slice | solution.py:412
  0.9 3.0 %collective-permute-start = (bf16[3,256,128]{2,1,0:T(8,128)(2,1)S(1)}, bf16[3,256,128]{2,1,0:T(8,128)(2,1)S(1)}, u32[]{:S(2)}, u32[]{:S(2)}) collective-permute-start(bf16[3,256,128]{2,1,0:T(8,128)(2,1)S(1)} %slice.3), channel_id=1, source_target_pairs={{0,1},{1,0},{2,3},{3,2},{4,5},{5,4},{6,7},{7,6},{8,9},{9,8},{10,11... | collective-permute-start | bytes 589832 | tf_op jit(solution)/shard_map/ppermute | solution.py:411
  4.0 1.0 %copy.11 = bf16[32,8,4,128]{3,1,2,0:T(8,128)(2,1)S(1)} copy(bf16[32,8,4,128]{3,2,1,0:T(4,128)(2,1)} %bitcast.10) | data formatting | bytes 524288
  5.0 1.7 %shard_map.73 = bf16[256,384]{1,0:T(8,128)(2,1)} custom-call(s32[1,256]{1,0:T(1,128)} %bitcast.11, s32[1,256]{1,0:T(1,128)} %bitcast.12, bf16[256,512]{1,0:T(8,128)(2,1)S(1)} %bitcast.8), custom_call_target="tpu_custom_call" | custom-call | tf_op jit(solution)/shard_map/pallas_call | solution.py:414
  6.7 6.0 %all-to-all-start = ((bf16[16,16,384]{2,1,0:T(8,128)(2,1)}), bf16[16,16,384]{2,1,0:T(8,128)(2,1)}, u32[]{:S(2)}, u32[]{:S(2)}) async-start(bf16[16,16,384]{2,1,0:T(8,128)(2,1)} %bitcast.9), calls=%async_computation | async-start | bytes 393216 | tf_op jit(solution)/shard_map/all_to_all | solution.py:426
  13.4 5.2 %shard_map.75 = (bf16[128,256]{1,0:T(8,128)(2,1)}, bf16[128,256]{1,0:T(8,128)(2,1)}, bf16[2,512,256]{2,1,0:T(8,128)(2,1)S(1)}) custom-call(s32[1,10]{1,0:T(1,128)} %ranges.11, bf16[3,256,128]{2,1,0:T(8,128)(2,1)} %copy-done.2, bf16[15,256,128]{2,1,0:T(8,128)(2,1)} %history_hbm.3, bf16[15,256,1280]{2,1,0:T(8,128)(2,1)} %weights.3), custom_call_target="tpu_custom_call" | custom-call | tf_op jit(solution)/shard_map/pallas_call | solution.py:440
  18.6 6.9 %shard_map.76 = (bf16[128,256]{1,0:T(8,128)(2,1)}, bf16[128,256]{1,0:T(8,128)(2,1)}, f32[128,256]{1,0:T(8,128)S(1)}, bf16[3,512,256]{2,1,0:T(8,128)(2,1)S(1)}, b...) custom-call(s32[1,10]{1,0:T(1,128)} %ranges.11, bf16[3,256,128]{2,1,0:T(8,128)(2,1)} %copy-done.2, ...), custom_call_target="tpu_custom_call" | custom-call | tf_op jit(solution)/shard_map/pallas_call | solution.py:457
  25.7 3.8 %collective-permute-start.1 = (bf16[128,256]{1,0:T(8,128)(2,1)S(1)}, bf16[128,256]{1,0:T(8,128)(2,1)S(1)}, u32[]{:S(2)}, u32[]{:S(2)}) collective-permute-start(bf16[128,256]{1,0:T(8,128)(2,1)S(1)} %copy-done.4), channel_id=1, source_target_pairs={{0,28},{2,30},{4,8},{6,10},{8,4},{10,6},{12,16},{14,18},{16,12},{1... | collective-permute-start | bytes 196616 | tf_op jit(solution)/shard_map/ppermute | solution.py:484
  29.5 1.5 %collective-permute-start.3 = (bf16[128,256]{1,0:T(8,128)(2,1)}, bf16[128,256]{1,0:T(8,128)(2,1)S(1)}, u32[]{:S(2)}, u32[]{:S(2)}) collective-permute-start(bf16[128,256]{1,0:T(8,128)(2,1)} %get-tuple-element.40), channel_id=1, source_target_pairs={{0,4},{2,6},{4,0},{6,2},{8,12},{10,14},{12,8},{14,10},{16,20},{18,... | collective-permute-start | bytes 196616 | tf_op jit(solution)/shard_map/ppermute | solution.py:484
  31.0 1.7 %collective-permute-done.1.refs_0_ = bf16[128,256]{1,0:T(8,128)(2,1)S(1)} collective-permute-done((bf16[128,256]{1,0:T(8,128)(2,1)S(1)}, bf16[128,256]{1,0:T(8,128)(2,1)S(1)}, u32[]{:S(2)}, u32[]{:S(2)}) %collective-permute-start.1) | collective-permute-done | bytes 65568 | tf_op jit(solution)/shard_map/ppermute | solution.py:484
  32.7 3.1 %collective-permute-done.2.refs_1_ = bf16[128,256]{1,0:T(8,128)(2,1)S(1)} collective-permute-done((bf16[128,256]{1,0:T(8,128)(2,1)S(1)}, bf16[128,256]{1,0:T(8,128)(2,1)S(1)}, u32[]{:S(2)}, u32[]{:S(2)}) %collective-permute-start.2) | collective-permute-done | bytes 65568 | tf_op jit(solution)/shard_map/ppermute | solution.py:484
  36.6 1.9 %collective-permute-start.5 = (bf16[128,256]{1,0:T(8,128)(2,1)S(1)}, bf16[128,256]{1,0:T(8,128)(2,1)S(1)}, u32[]{:S(2)}, u32[]{:S(2)}) collective-permute-start(bf16[128,256]{1,0:T(8,128)(2,1)S(1)} %get-tuple-element.43), channel_id=1, source_target_pairs={{0,1},{1,0},{2,3},{3,2},{4,5},{5,4},{6,7},{7,6},{8,9},{9,8},{10,11... | collective-permute-start | bytes 196616 | tf_op jit(solution)/shard_map/ppermute | solution.py:491
  38.5 1.1 %shard_map.74.source = f32[256,256]{1,0:T(8,128)S(1)} custom-call(bf16[256,384]{1,0:T(8,128)(2,1)} %bitcast.3.arrived_ref), custom_call_target="tpu_custom_call" | custom-call | tf_op jit(solution)/shard_map/pallas_call | solution.py:433
  39.6 1.2 %collective-permute-done.5.refs_0_ = bf16[128,256]{1,0:T(8,128)(2,1)S(1)} collective-permute-done((bf16[128,256]{1,0:T(8,128)(2,1)S(1)}, bf16[128,256]{1,0:T(8,128)(2,1)S(1)}, u32[]{:S(2)}, u32[]{:S(2)}) %collective-permute-start.5) | collective-permute-done | bytes 65568 | tf_op jit(solution)/shard_map/ppermute | solution.py:491
  40.8 1.5 %shard_map.78 = (bf16[128,256]{1,0:T(8,128)(2,1)S(1)}, f32[128,256]{1,0:T(8,128)S(1)}, bf16[128,256]{1,0:T(8,128)(2,1)S(1)}, bf16[128,256]{1,0:T(8,128)(2,1)S(1)...) custom-call(s32[1,10]{1,0:T(1,128)S(1)} %copy-done.1, ...), custom_call_target="tpu_custom_call" | custom-call | tf_op jit(solution)/shard_map/pallas_call | solution.py:517
  42.3 2.6 %collective-permute-start.7 = (bf16[128,256]{1,0:T(8,128)(2,1)S(1)}, bf16[128,256]{1,0:T(8,128)(2,1)S(1)}, u32[]{:S(2)}, u32[]{:S(2)}) collective-permute-start(bf16[128,256]{1,0:T(8,128)(2,1)S(1)} %get-tuple-element.49), channel_id=1, source_target_pairs={{0,28},{2,30},{4,8},{6,10},{8,4},{10,6},{12,16},{14,18},{16,12},{1... | collective-permute-start | bytes 196616 | tf_op jit(solution)/shard_map/ppermute | solution.py:484
  45.2 4.2 %collective-permute-done.7.refs_0_ = bf16[128,256]{1,0:T(8,128)(2,1)S(1)} collective-permute-done((bf16[128,256]{1,0:T(8,128)(2,1)S(1)}, bf16[128,256]{1,0:T(8,128)(2,1)S(1)}, u32[]{:S(2)}, u32[]{:S(2)}) %collective-permute-start.7) | collective-permute-done | bytes 65568 | tf_op jit(solution)/shard_map/ppermute | solution.py:484
  49.5 1.8 %collective-permute-done.8.refs_1_ = bf16[128,256]{1,0:T(8,128)(2,1)S(1)} collective-permute-done((bf16[128,256]{1,0:T(8,128)(2,1)S(1)}, bf16[128,256]{1,0:T(8,128)(2,1)S(1)}, u32[]{:S(2)}, u32[]{:S(2)}) %collective-permute-start.8) | collective-permute-done | bytes 65568 | tf_op jit(solution)/shard_map/ppermute | solution.py:484
  51.3 1.0 %shard_map.79 = (bf16[128,256]{1,0:T(8,128)(2,1)S(1)}, f32[128,256]{1,0:T(8,128)S(1)}, bf16[128,256]{1,0:T(8,128)(2,1)S(1)}, bf16[128,256]{1,0:T(8,128)(2,1)S(1)...) custom-call(s32[1,10]{1,0:T(1,128)S(1)} %copy-done.1, ...), custom_call_target="tpu_custom_call" | custom-call | tf_op jit(solution)/shard_map/pallas_call | solution.py:517
  52.3 1.9 %collective-permute-start.11 = (bf16[128,256]{1,0:T(8,128)(2,1)S(1)}, bf16[128,256]{1,0:T(8,128)(2,1)S(1)}, u32[]{:S(2)}, u32[]{:S(2)}) collective-permute-start(bf16[128,256]{1,0:T(8,128)(2,1)S(1)} %get-tuple-element.56), channel_id=1, source_target_pairs={{0,28},{2,30},{4,8},{6,10},{8,4},{10,6},{12,16},{14,18},{16,12},{1... | collective-permute-start | bytes 196616 | tf_op jit(solution)/shard_map/ppermute | solution.py:484
  54.3 1.6 %collective-permute-start.13 = (bf16[128,256]{1,0:T(8,128)(2,1)S(1)}, bf16[128,256]{1,0:T(8,128)(2,1)S(1)}, u32[]{:S(2)}, u32[]{:S(2)}) collective-permute-start(bf16[128,256]{1,0:T(8,128)(2,1)S(1)} %get-tuple-element.58), channel_id=1, source_target_pairs={{0,4},{2,6},{4,0},{6,2},{8,12},{10,14},{12,8},{14,10},{16,20},{18,... | collective-permute-start | bytes 196616 | tf_op jit(solution)/shard_map/ppermute | solution.py:484
  55.9 1.4 %collective-permute-start.15 = (bf16[128,256]{1,0:T(8,128)(2,1)S(1)}, bf16[128,256]{1,0:T(8,128)(2,1)S(1)}, u32[]{:S(2)}, u32[]{:S(2)}) collective-permute-start(bf16[128,256]{1,0:T(8,128)(2,1)S(1)} %get-tuple-element.54.refs_1_), channel_id=1, source_target_pairs={{0,1},{1,0},{2,3},{3,2},{4,5},{5,4},{6,7},{7,6},{8,9},{9,8},{10,11... | collective-permute-start | bytes 196616 | tf_op jit(solution)/shard_map/ppermute | solution.py:500
  57.3 2.1 %collective-permute-done.11.refs_0_ = bf16[128,256]{1,0:T(8,128)(2,1)S(1)} collective-permute-done((bf16[128,256]{1,0:T(8,128)(2,1)S(1)}, bf16[128,256]{1,0:T(8,128)(2,1)S(1)}, u32[]{:S(2)}, u32[]{:S(2)}) %collective-permute-start.11) | collective-permute-done | bytes 65568 | tf_op jit(solution)/shard_map/ppermute | solution.py:484
  59.5 1.2 %collective-permute-done.12.refs_1_ = bf16[128,256]{1,0:T(8,128)(2,1)S(1)} collective-permute-done((bf16[128,256]{1,0:T(8,128)(2,1)S(1)}, bf16[128,256]{1,0:T(8,128)(2,1)S(1)}, u32[]{:S(2)}, u32[]{:S(2)}) %collective-permute-start.12) | collective-permute-done | bytes 65568 | tf_op jit(solution)/shard_map/ppermute | solution.py:484
  60.7 1.1 %shard_map.80 = (bf16[128,256]{1,0:T(8,128)(2,1)S(1)}, f32[128,256]{1,0:T(8,128)S(1)}, bf16[128,256]{1,0:T(8,128)(2,1)S(1)}, bf16[128,256]{1,0:T(8,128)(2,1)S(1)...) custom-call(s32[1,10]{1,0:T(1,128)S(1)} %copy-done.1, f32[256,256]{1,0:T(8,128)S(1)} %shard_map.74.source, ...), custom_call_target="tpu_custom_call" | custom-call | tf_op jit(solution)/shard_map/pallas_call | solution.py:517
  61.8 1.3 %collective-permute-start.17 = (bf16[128,256]{1,0:T(8,128)(2,1)S(1)}, bf16[128,256]{1,0:T(8,128)(2,1)S(1)}, u32[]{:S(2)}, u32[]{:S(2)}) collective-permute-start(bf16[128,256]{1,0:T(8,128)(2,1)S(1)} %get-tuple-element.61.refs_2_), channel_id=1, source_target_pairs={{0,1},{1,0},{2,3},{3,2},{4,5},{5,4},{6,7},{7,6},{8,9},{9,8},{10,11... | collective-permute-start | bytes 196616 | tf_op jit(solution)/shard_map/ppermute | solution.py:500
  63.1 3.0 %collective-permute-start.18 = (bf16[128,256]{1,0:T(8,128)(2,1)S(1)}, bf16[128,256]{1,0:T(8,128)(2,1)S(1)}, u32[]{:S(2)}, u32[]{:S(2)}) collective-permute-start(bf16[128,256]{1,0:T(8,128)(2,1)S(1)} %get-tuple-element.63), channel_id=1, source_target_pairs={{0,28},{2,30},{4,8},{6,10},{8,4},{10,6},{12,16},{14,18},{16,12},{1... | collective-permute-start | bytes 196616 | tf_op jit(solution)/shard_map/ppermute | solution.py:484
  67.2 0.9 %collective-permute-start.16 = (bf16[128,256]{1,0:T(8,128)(2,1)S(1)}, bf16[128,256]{1,0:T(8,128)(2,1)S(1)}, u32[]{:S(2)}, u32[]{:S(2)}) collective-permute-start(bf16[128,256]{1,0:T(8,128)(2,1)S(1)} %get-tuple-element.47.refs_0_), channel_id=1, source_target_pairs={{0,1},{1,0},{2,3},{3,2},{4,5},{5,4},{6,7},{7,6},{8,9},{9,8},{10,11... | collective-permute-start | bytes 196616 | tf_op jit(solution)/shard_map/ppermute | solution.py:500
  68.2 2.0 %collective-permute-done.18.refs_0_ = bf16[128,256]{1,0:T(8,128)(2,1)S(1)} collective-permute-done((bf16[128,256]{1,0:T(8,128)(2,1)S(1)}, bf16[128,256]{1,0:T(8,128)(2,1)S(1)}, u32[]{:S(2)}, u32[]{:S(2)}) %collective-permute-start.18) | collective-permute-done | bytes 65568 | tf_op jit(solution)/shard_map/ppermute | solution.py:484
  70.2 2.3 %collective-permute-done.19.refs_1_ = bf16[128,256]{1,0:T(8,128)(2,1)S(1)} collective-permute-done((bf16[128,256]{1,0:T(8,128)(2,1)S(1)}, bf16[128,256]{1,0:T(8,128)(2,1)S(1)}, u32[]{:S(2)}, u32[]{:S(2)}) %collective-permute-start.19) | collective-permute-done | bytes 65568 | tf_op jit(solution)/shard_map/ppermute | solution.py:484
  73.8 0.8 %shard_map.81.begun = bf16[4,256,128]{2,1,0:T(8,128)(2,1)} custom-call(bf16[128,256]{1,0:T(8,128)(2,1)S(1)} %get-tuple-element.47.refs_0_, bf16[128,256]{1,0:T(8,128)(2,1)S(1)} %get-tuple-element.54.refs_1_, bf16[128,256]{1,0:T(8,128)(2,1)S(1)} %get-tuple-element.61.refs_2_, bf16[128,256]{1,0:T(8,128)(2,1)S(1)} %collective-permute-done.16.refs_3_, ...), custom_call_target="tpu_custom_call" | custom-call | tf_op jit(solution)/shard_map/pallas_call | solution.py:536
  74.7 2.9 %collective-permute-done.22.far = bf16[128,256]{1,0:T(8,128)(2,1)S(1)} collective-permute-done((bf16[128,256]{1,0:T(8,128)(2,1)S(1)}, bf16[128,256]{1,0:T(8,128)(2,1)S(1)}, u32[]{:S(2)}, u32[]{:S(2)}) %collective-permute-start.22) | collective-permute-done | bytes 65568 | tf_op jit(solution)/shard_map/ppermute | solution.py:500
  (39 shorter events, 5.1 us)
Async XLA Ops:
  0.9 11.8 %collective-permute-start = (bf16[3,256,128]{2,1,0:T(8,128)(2,1)S(1)}, bf16[3,256,128]{2,1,0:T(8,128)(2,1)S(1)}, u32[]{:S(2)}, u32[]{:S(2)}) collective-permute-start(bf16[3,256,128]{2,1,0:T(8,128)(2,1)S(1)} %slice.3), channel_id=1, source_target_pairs={{0,1},{1,0},{2,3},{3,2},{4,5},{5,4},{6,7},{7,6},{8,9},{9,8},{10,11... | collective-permute-start | bytes 589832 | tf_op jit(solution)/shard_map/ppermute | solution.py:411
  6.7 31.8 %all-to-all-start = ((bf16[16,16,384]{2,1,0:T(8,128)(2,1)}), bf16[16,16,384]{2,1,0:T(8,128)(2,1)}, u32[]{:S(2)}, u32[]{:S(2)}) async-start(bf16[16,16,384]{2,1,0:T(8,128)(2,1)} %bitcast.9), calls=%async_computation | async-start | bytes 393216 | tf_op jit(solution)/shard_map/all_to_all | solution.py:426
  12.7 28.1 %copy-start.1 = (s32[1,10]{1,0:T(1,128)S(1)}, s32[1,10]{1,0:T(1,128)}, u32[]{:S(2)}) copy-start(s32[1,10]{1,0:T(1,128)} %ranges.11) | copy-start | bytes 124
  12.7 0.7 copy-start.2
  18.6 7.1 %copy-start.4 = (bf16[128,256]{1,0:T(8,128)(2,1)S(1)}, bf16[128,256]{1,0:T(8,128)(2,1)}, u32[]{:S(2)}) copy-start(bf16[128,256]{1,0:T(8,128)(2,1)} %get-tuple-element.38) | copy-start | bytes 196612
  18.6 10.8 %copy-start.3 = (bf16[128,256]{1,0:T(8,128)(2,1)S(1)}, bf16[128,256]{1,0:T(8,128)(2,1)}, u32[]{:S(2)}) copy-start(bf16[128,256]{1,0:T(8,128)(2,1)} %get-tuple-element.39) | copy-start | bytes 196612
  18.6 32.7 %copy-start = (bf16[256,256]{1,0:T(8,128)(2,1)S(1)}, bf16[256,256]{1,0:T(8,128)(2,1)}, u32[]{:S(2)}) copy-start(bf16[256,256]{1,0:T(8,128)(2,1)} %inverse.7) | copy-start | bytes 393220
  25.6 15.2 %collective-permute-start.6 = (bf16[640,256]{1,0:T(8,128)(2,1)}, bf16[640,256]{1,0:T(8,128)(2,1)}, u32[]{:S(2)}, u32[]{:S(2)}) collective-permute-start(bf16[640,256]{1,0:T(8,128)(2,1)} %get-tuple-element.46), channel_id=1, source_target_pairs={{0,1},{1,0},{2,3},{3,2},{4,5},{5,4},{6,7},{7,6},{8,9},{9,8},{10,11... | collective-permute-start | bytes 983048 | tf_op jit(solution)/shard_map/ppermute | solution.py:383
  25.7 7.0 %collective-permute-start.1 = (bf16[128,256]{1,0:T(8,128)(2,1)S(1)}, bf16[128,256]{1,0:T(8,128)(2,1)S(1)}, u32[]{:S(2)}, u32[]{:S(2)}) collective-permute-start(bf16[128,256]{1,0:T(8,128)(2,1)S(1)} %copy-done.4), channel_id=1, source_target_pairs={{0,28},{2,30},{4,8},{6,10},{8,4},{10,6},{12,16},{14,18},{16,12},{1... | collective-permute-start | bytes 196616 | tf_op jit(solution)/shard_map/ppermute | solution.py:484
  29.5 6.4 %collective-permute-start.2 = (bf16[128,256]{1,0:T(8,128)(2,1)S(1)}, bf16[128,256]{1,0:T(8,128)(2,1)S(1)}, u32[]{:S(2)}, u32[]{:S(2)}) collective-permute-start(bf16[128,256]{1,0:T(8,128)(2,1)S(1)} %copy-done.3), channel_id=1, source_target_pairs={{0,30},{2,4},{4,2},{6,8},{8,6},{10,12},{12,10},{14,16},{16,14},{18... | collective-permute-start | bytes 196616 | tf_op jit(solution)/shard_map/ppermute | solution.py:484
  29.5 6.4 %collective-permute-start.3 = (bf16[128,256]{1,0:T(8,128)(2,1)}, bf16[128,256]{1,0:T(8,128)(2,1)S(1)}, u32[]{:S(2)}, u32[]{:S(2)}) collective-permute-start(bf16[128,256]{1,0:T(8,128)(2,1)} %get-tuple-element.40), channel_id=1, source_target_pairs={{0,4},{2,6},{4,0},{6,2},{8,12},{10,14},{12,8},{14,10},{16,20},{18,... | collective-permute-start | bytes 196616 | tf_op jit(solution)/shard_map/ppermute | solution.py:484
  31.0 4.9 %collective-permute-start.4 = (bf16[128,256]{1,0:T(8,128)(2,1)}, bf16[128,256]{1,0:T(8,128)(2,1)S(1)}, u32[]{:S(2)}, u32[]{:S(2)}) collective-permute-start(bf16[128,256]{1,0:T(8,128)(2,1)} %get-tuple-element.41), channel_id=1, source_target_pairs={{0,2},{2,0},{4,6},{6,4},{8,10},{10,8},{12,14},{14,12},{16,18},{18,... | collective-permute-start | bytes 196616 | tf_op jit(solution)/shard_map/ppermute | solution.py:484
  36.6 4.3 %collective-permute-start.5 = (bf16[128,256]{1,0:T(8,128)(2,1)S(1)}, bf16[128,256]{1,0:T(8,128)(2,1)S(1)}, u32[]{:S(2)}, u32[]{:S(2)}) collective-permute-start(bf16[128,256]{1,0:T(8,128)(2,1)S(1)} %get-tuple-element.43), channel_id=1, source_target_pairs={{0,1},{1,0},{2,3},{3,2},{4,5},{5,4},{6,7},{7,6},{8,9},{9,8},{10,11... | collective-permute-start | bytes 196616 | tf_op jit(solution)/shard_map/ppermute | solution.py:491
  42.3 7.1 %collective-permute-start.7 = (bf16[128,256]{1,0:T(8,128)(2,1)S(1)}, bf16[128,256]{1,0:T(8,128)(2,1)S(1)}, u32[]{:S(2)}, u32[]{:S(2)}) collective-permute-start(bf16[128,256]{1,0:T(8,128)(2,1)S(1)} %get-tuple-element.49), channel_id=1, source_target_pairs={{0,28},{2,30},{4,8},{6,10},{8,4},{10,6},{12,16},{14,18},{16,12},{1... | collective-permute-start | bytes 196616 | tf_op jit(solution)/shard_map/ppermute | solution.py:484
  44.9 6.4 %collective-permute-start.8 = (bf16[128,256]{1,0:T(8,128)(2,1)S(1)}, bf16[128,256]{1,0:T(8,128)(2,1)S(1)}, u32[]{:S(2)}, u32[]{:S(2)}) collective-permute-start(bf16[128,256]{1,0:T(8,128)(2,1)S(1)} %get-tuple-element.50), channel_id=1, source_target_pairs={{0,30},{2,4},{4,2},{6,8},{8,6},{10,12},{12,10},{14,16},{16,14},{18... | collective-permute-start | bytes 196616 | tf_op jit(solution)/shard_map/ppermute | solution.py:484
  44.9 6.4 %collective-permute-start.9 = (bf16[128,256]{1,0:T(8,128)(2,1)S(1)}, bf16[128,256]{1,0:T(8,128)(2,1)S(1)}, u32[]{:S(2)}, u32[]{:S(2)}) collective-permute-start(bf16[128,256]{1,0:T(8,128)(2,1)S(1)} %get-tuple-element.51), channel_id=1, source_target_pairs={{0,4},{2,6},{4,0},{6,2},{8,12},{10,14},{12,8},{14,10},{16,20},{18,... | collective-permute-start | bytes 196616 | tf_op jit(solution)/shard_map/ppermute | solution.py:484
  45.2 6.1 %collective-permute-start.10 = (bf16[128,256]{1,0:T(8,128)(2,1)S(1)}, bf16[128,256]{1,0:T(8,128)(2,1)S(1)}, u32[]{:S(2)}, u32[]{:S(2)}) collective-permute-start(bf16[128,256]{1,0:T(8,128)(2,1)S(1)} %get-tuple-element.52), channel_id=1, source_target_pairs={{0,2},{2,0},{4,6},{6,4},{8,10},{10,8},{12,14},{14,12},{16,18},{18,... | collective-permute-start | bytes 196616 | tf_op jit(solution)/shard_map/ppermute | solution.py:484
  52.3 7.1 %collective-permute-start.11 = (bf16[128,256]{1,0:T(8,128)(2,1)S(1)}, bf16[128,256]{1,0:T(8,128)(2,1)S(1)}, u32[]{:S(2)}, u32[]{:S(2)}) collective-permute-start(bf16[128,256]{1,0:T(8,128)(2,1)S(1)} %get-tuple-element.56), channel_id=1, source_target_pairs={{0,28},{2,30},{4,8},{6,10},{8,4},{10,6},{12,16},{14,18},{16,12},{1... | collective-permute-start | bytes 196616 | tf_op jit(solution)/shard_map/ppermute | solution.py:484
  54.3 6.4 %collective-permute-start.12 = (bf16[128,256]{1,0:T(8,128)(2,1)S(1)}, bf16[128,256]{1,0:T(8,128)(2,1)S(1)}, u32[]{:S(2)}, u32[]{:S(2)}) collective-permute-start(bf16[128,256]{1,0:T(8,128)(2,1)S(1)} %get-tuple-element.57), channel_id=1, source_target_pairs={{0,30},{2,4},{4,2},{6,8},{8,6},{10,12},{12,10},{14,16},{16,14},{18... | collective-permute-start | bytes 196616 | tf_op jit(solution)/shard_map/ppermute | solution.py:484
  54.3 6.4 %collective-permute-start.13 = (bf16[128,256]{1,0:T(8,128)(2,1)S(1)}, bf16[128,256]{1,0:T(8,128)(2,1)S(1)}, u32[]{:S(2)}, u32[]{:S(2)}) collective-permute-start(bf16[128,256]{1,0:T(8,128)(2,1)S(1)} %get-tuple-element.58), channel_id=1, source_target_pairs={{0,4},{2,6},{4,0},{6,2},{8,12},{10,14},{12,8},{14,10},{16,20},{18,... | collective-permute-start | bytes 196616 | tf_op jit(solution)/shard_map/ppermute | solution.py:484
  55.9 4.8 %collective-permute-start.14 = (bf16[128,256]{1,0:T(8,128)(2,1)S(1)}, bf16[128,256]{1,0:T(8,128)(2,1)S(1)}, u32[]{:S(2)}, u32[]{:S(2)}) collective-permute-start(bf16[128,256]{1,0:T(8,128)(2,1)S(1)} %get-tuple-element.59), channel_id=1, source_target_pairs={{0,2},{2,0},{4,6},{6,4},{8,10},{10,8},{12,14},{14,12},{16,18},{18,... | collective-permute-start | bytes 196616 | tf_op jit(solution)/shard_map/ppermute | solution.py:484
  55.9 4.8 %collective-permute-start.15 = (bf16[128,256]{1,0:T(8,128)(2,1)S(1)}, bf16[128,256]{1,0:T(8,128)(2,1)S(1)}, u32[]{:S(2)}, u32[]{:S(2)}) collective-permute-start(bf16[128,256]{1,0:T(8,128)(2,1)S(1)} %get-tuple-element.54.refs_1_), channel_id=1, source_target_pairs={{0,1},{1,0},{2,3},{3,2},{4,5},{5,4},{6,7},{7,6},{8,9},{9,8},{10,11... | collective-permute-start | bytes 196616 | tf_op jit(solution)/shard_map/ppermute | solution.py:500
  61.8 5.4 %collective-permute-start.17 = (bf16[128,256]{1,0:T(8,128)(2,1)S(1)}, bf16[128,256]{1,0:T(8,128)(2,1)S(1)}, u32[]{:S(2)}, u32[]{:S(2)}) collective-permute-start(bf16[128,256]{1,0:T(8,128)(2,1)S(1)} %get-tuple-element.61.refs_2_), channel_id=1, source_target_pairs={{0,1},{1,0},{2,3},{3,2},{4,5},{5,4},{6,7},{7,6},{8,9},{9,8},{10,11... | collective-permute-start | bytes 196616 | tf_op jit(solution)/shard_map/ppermute | solution.py:500
  63.1 7.1 %collective-permute-start.18 = (bf16[128,256]{1,0:T(8,128)(2,1)S(1)}, bf16[128,256]{1,0:T(8,128)(2,1)S(1)}, u32[]{:S(2)}, u32[]{:S(2)}) collective-permute-start(bf16[128,256]{1,0:T(8,128)(2,1)S(1)} %get-tuple-element.63), channel_id=1, source_target_pairs={{0,28},{2,30},{4,8},{6,10},{8,4},{10,6},{12,16},{14,18},{16,12},{1... | collective-permute-start | bytes 196616 | tf_op jit(solution)/shard_map/ppermute | solution.py:484
  66.1 6.4 %collective-permute-start.19 = (bf16[128,256]{1,0:T(8,128)(2,1)S(1)}, bf16[128,256]{1,0:T(8,128)(2,1)S(1)}, u32[]{:S(2)}, u32[]{:S(2)}) collective-permute-start(bf16[128,256]{1,0:T(8,128)(2,1)S(1)} %get-tuple-element.64), channel_id=1, source_target_pairs={{0,30},{2,4},{4,2},{6,8},{8,6},{10,12},{12,10},{14,16},{16,14},{18... | collective-permute-start | bytes 196616 | tf_op jit(solution)/shard_map/ppermute | solution.py:484
  66.4 6.0 %collective-permute-start.20 = (bf16[128,256]{1,0:T(8,128)(2,1)S(1)}, bf16[128,256]{1,0:T(8,128)(2,1)S(1)}, u32[]{:S(2)}, u32[]{:S(2)}) collective-permute-start(bf16[128,256]{1,0:T(8,128)(2,1)S(1)} %get-tuple-element.65), channel_id=1, source_target_pairs={{0,4},{2,6},{4,0},{6,2},{8,12},{10,14},{12,8},{14,10},{16,20},{18,... | collective-permute-start | bytes 196616 | tf_op jit(solution)/shard_map/ppermute | solution.py:484
  67.2 5.2 %collective-permute-start.21 = (bf16[128,256]{1,0:T(8,128)(2,1)S(1)}, bf16[128,256]{1,0:T(8,128)(2,1)S(1)}, u32[]{:S(2)}, u32[]{:S(2)}) collective-permute-start(bf16[128,256]{1,0:T(8,128)(2,1)S(1)} %get-tuple-element.66), channel_id=1, source_target_pairs={{0,2},{2,0},{4,6},{6,4},{8,10},{10,8},{12,14},{14,12},{16,18},{18,... | collective-permute-start | bytes 196616 | tf_op jit(solution)/shard_map/ppermute | solution.py:484
  67.2 6.6 %collective-permute-start.16 = (bf16[128,256]{1,0:T(8,128)(2,1)S(1)}, bf16[128,256]{1,0:T(8,128)(2,1)S(1)}, u32[]{:S(2)}, u32[]{:S(2)}) collective-permute-start(bf16[128,256]{1,0:T(8,128)(2,1)S(1)} %get-tuple-element.47.refs_0_), channel_id=1, source_target_pairs={{0,1},{1,0},{2,3},{3,2},{4,5},{5,4},{6,7},{7,6},{8,9},{9,8},{10,11... | collective-permute-start | bytes 196616 | tf_op jit(solution)/shard_map/ppermute | solution.py:500
  73.2 4.3 %collective-permute-start.22 = (bf16[128,256]{1,0:T(8,128)(2,1)S(1)}, bf16[128,256]{1,0:T(8,128)(2,1)S(1)}, u32[]{:S(2)}, u32[]{:S(2)}) collective-permute-start(bf16[128,256]{1,0:T(8,128)(2,1)S(1)} %shard_map.82.mine), channel_id=1, source_target_pairs={{0,1},{1,0},{2,3},{3,2},{4,5},{5,4},{6,7},{7,6},{8,9},{9,8},{10,11... | collective-permute-start | bytes 196616 | tf_op jit(solution)/shard_map/ppermute | solution.py:500

commit v7 on v3

--- a/solution.py
+++ b/solution.py
@@ -209,10 +209,11 @@
     rest_far = refs[2] if step == 0 else None
     refs = refs[3 if step == 0 else 2 :]
     olders, outs = refs[:step], refs[step:]
-    density_ref, cross, next_own = outs[:3]
-    messages = outs[3:]
+    cross, next_own = outs[:2]
+    messages = outs[2 : NEAR + 1]
     band_zero = lax.axis_index("lag") == 0
-    density_ref[...] = rounded
+    for density_ref in outs[NEAR + 1 :]:
+        density_ref[...] = rounded
     cross[...] = jnp.where(band_zero, density, total).astype(jnp.bfloat16)
     recent = [rounded] + [ref[...] for ref in olders]
     steps = stage.shape[1] // shots
@@ -338,7 +339,7 @@
     source = call(source_kernel, [(block, f32, VMEM)] * steps, [VMEM])(arrived)
     source = [near_memory(s) for s in source]
 
-    sizes = [*range(2, band, 2), band]
+    sizes = [*range(1, band + 1)]
     older = call(
         functools.partial(older_kernel, steps, sizes),
         [(block, bf16)] * (NEAR - 1)
@@ -393,8 +394,8 @@
         outs = [(block, bf16)]
         if not last_step:
             inputs += [recent, stage] + [there] * (step == 0) + densities[::-1]
-            outs = [(block, bf16, VMEM), (block, bf16), (block, f32, VMEM)]
-            outs += [(block, bf16)] * (NEAR - 1)
+            outs = [(block, bf16), (block, f32, VMEM)] + [(block, bf16)] * (NEAR - 1)
+            outs += [(block, bf16, VMEM)] * (step < steps - 2)
         results = call(
             functools.partial(step_kernel, step, last_step),
             outs,
@@ -403,15 +404,15 @@
         if last_step:
             ends, _ = cross_bands(results[0])
         else:
-            densities.append(near_memory(results[0]))
-            sent, back = cross_bands(results[1])
+            densities += [near_memory(r) for r in results[NEAR + 1 :]]
+            sent, back = cross_bands(results[0])
             outward.append(sent)
             if step == 0:
                 inward = [far]
             else:
                 inward.append(back)
-            own = near_memory(results[2])
-            received = exchange(results[3:])
+            own = near_memory(results[1])
+            received = exchange(results[2 : NEAR + 1])
     whole = ((steps, tile_len, shots), bf16)
     pairs = [mine for mine, _ in outward] + [theirs for _, theirs in outward]
     (begun,) = call(

time: 81.2 us -> 80.8 us (level)
  no operation moved by 1% of the time
where the time goes in v7:
time: 80.8 us; the launch traced here: 80.5 us
  starting transfers between devices  30.9 us (38%)
  waiting for transfers between devices  29.2 us (36%)
  Pallas kernels  17.9 us (22%)
  local copies, waits for them, and re-layouts  1.67 us (2%)
    ppermute x16, waiting for transfers between devices, exchange(): gone.append(lax.ppermute(b, 'patch', r))  17.5 us
    ppermute x16, starting transfers between devices, exchange(): gone.append(lax.ppermute(b, 'patch', r))  16.7 us
    pallas_call x1, Pallas kernels, local(): call(functools.partial(older_kernel, steps, sizes), [(block, bf16)] * (NE...  9.01 us
    all_to_all x1, starting transfers between devices, local(): lax.all_to_all(outgoing.reshape(patches, CAP, width + LANES), 'patch', sp...  7.47 us
    ppermute x1, waiting for transfers between devices, local(): rim = lax.ppermute(edge, 'lag', [(i, (i + 1) % lags) for i in range(lags)])  5.68 us
    pallas_call x4, Pallas kernels, local(): call(functools.partial(step_kernel, step, last_step), outs, [pltpu.SMEM]...  4.3 us
    ppermute x4, starting transfers between devices, cross_bands(): swapped = lax.ppermute(block, 'lag', lag_partners(lags, 1))  3.8 us
    ppermute x2, waiting for transfers between devices, lag_sum(): lax.ppermute(block.astype(jnp.bfloat16), 'lag', lag_partners(lags, distan...  3.55 us
  transfers between devices with their start and end apart: 24, of which 10 were waited for; matrix products, arithmetic and copies ran while one was open for 1% of the time, Pallas kernels for 15%

profile of v7, /device:TPU:0, one launch (start us, length us, event | category | flops | bytes accessed | tf_op | source)
XLA Modules:
  0.0 80.5 jit_solution(6243499437243138647)
XLA Ops:
  0.0 1.0 %copy.11 = bf16[32,8,4,128]{3,1,2,0:T(8,128)(2,1)S(1)} copy(bf16[32,8,4,128]{3,2,1,0:T(4,128)(2,1)} %bitcast.9) | data formatting | bytes 524288
  1.0 1.8 %shard_map.73 = (bf16[256,640]{1,0:T(8,128)(2,1)}, bf16[3,256,128]{2,1,0:T(8,128)(2,1)S(1)}) custom-call(s32[1,256]{1,0:T(1,128)} %bitcast.10, s32[1,256]{1,0:T(1,128)} %bitcast.11, bf16[15,256,128]{2,1,0:T(8,128)(2,1)} %history.3, bf16[256,512]{1,0:T(8,128)(2,1)S(1)} %bitcast.8), custom_call_target="tpu_custom_call" | custom-call | tf_op jit(solution)/shard_map/pallas_call | solution.py:319
  2.8 7.5 %all-to-all-start = ((bf16[16,16,640]{2,1,0:T(8,128)(2,1)}), bf16[16,16,640]{2,1,0:T(8,128)(2,1)}, u32[]{:S(2)}, u32[]{:S(2)}) async-start(bf16[16,16,640]{2,1,0:T(8,128)(2,1)} %bitcast.2), calls=%async_computation | async-start | bytes 655360 | tf_op jit(solution)/shard_map/all_to_all | solution.py:332
  10.3 1.6 %collective-permute-start = (bf16[3,256,128]{2,1,0:T(8,128)(2,1)S(1)}, bf16[3,256,128]{2,1,0:T(8,128)(2,1)S(1)}, u32[]{:S(2)}, u32[]{:S(2)}) collective-permute-start(bf16[3,256,128]{2,1,0:T(8,128)(2,1)S(1)} %get-tuple-element.42), channel_id=1, source_target_pairs={{0,1},{1,0},{2,3},{3,2},{4,5},{5,4},{6,7},{7,6},{8,9},{9,8},{10,11... | collective-permute-start | bytes 589832 | tf_op jit(solution)/shard_map/ppermute | solution.py:331
  11.9 5.7 %collective-permute-done.rim = bf16[3,256,128]{2,1,0:T(8,128)(2,1)S(1)} collective-permute-done((bf16[3,256,128]{2,1,0:T(8,128)(2,1)S(1)}, bf16[3,256,128]{2,1,0:T(8,128)(2,1)S(1)}, u32[]{:S(2)}, u32[]{:S(2)}) %collective-permute-start) | collective-permute-done | bytes 196640 | tf_op jit(solution)/shard_map/ppermute | solution.py:331
  18.2 9.0 %shard_map.75 = (bf16[128,256]{1,0:T(8,128)(2,1)}, bf16[128,256]{1,0:T(8,128)(2,1)}, bf16[128,256]{1,0:T(8,128)(2,1)}, bf16[128,256]{1,0:T(8,128)(2,1)}, f32[128...) custom-call(s32[1,10]{1,0:T(1,128)} %ranges.9, ...), custom_call_target="tpu_custom_call" | custom-call | tf_op jit(solution)/shard_map/pallas_call | solution.py:343
  27.2 3.8 %collective-permute-start.1 = (bf16[128,256]{1,0:T(8,128)(2,1)}, bf16[128,256]{1,0:T(8,128)(2,1)S(1)}, u32[]{:S(2)}, u32[]{:S(2)}) collective-permute-start(bf16[128,256]{1,0:T(8,128)(2,1)} %get-tuple-element.45), channel_id=1, source_target_pairs={{0,28},{2,30},{4,8},{6,10},{8,4},{10,6},{12,16},{14,18},{16,12},{1... | collective-permute-start | bytes 196616 | tf_op jit(solution)/shard_map/ppermute | solution.py:369
  31.4 1.4 %collective-permute-start.6 = (bf16[640,256]{1,0:T(8,128)(2,1)}, bf16[640,256]{1,0:T(8,128)(2,1)}, u32[]{:S(2)}, u32[]{:S(2)}) collective-permute-start(bf16[640,256]{1,0:T(8,128)(2,1)} %get-tuple-element.51), channel_id=1, source_target_pairs={{0,1},{1,0},{2,3},{3,2},{4,5},{5,4},{6,7},{7,6},{8,9},{9,8},{10,11... | collective-permute-start | bytes 983048 | tf_op jit(solution)/shard_map/ppermute | solution.py:292
  32.8 1.7 %collective-permute-done.1 = bf16[128,256]{1,0:T(8,128)(2,1)S(1)} collective-permute-done((bf16[128,256]{1,0:T(8,128)(2,1)}, bf16[128,256]{1,0:T(8,128)(2,1)S(1)}, u32[]{:S(2)}, u32[]{:S(2)}) %collective-permute-start.1) | collective-permute-done | bytes 65568 | tf_op jit(solution)/shard_map/ppermute | solution.py:369
  34.5 3.1 %collective-permute-done.2 = bf16[128,256]{1,0:T(8,128)(2,1)S(1)} collective-permute-done((bf16[128,256]{1,0:T(8,128)(2,1)}, bf16[128,256]{1,0:T(8,128)(2,1)S(1)}, u32[]{:S(2)}, u32[]{:S(2)}) %collective-permute-start.2) | collective-permute-done | bytes 65568 | tf_op jit(solution)/shard_map/ppermute | solution.py:369
  38.3 1.2 %shard_map.74 = (f32[128,256]{1,0:T(8,128)S(1)}, f32[128,256]{1,0:T(8,128)S(1)}, f32[128,256]{1,0:T(8,128)S(1)}, f32[128,256]{1,0:T(8,128)S(1)}) custom-call(bf16[256,640]{1,0:T(8,128)(2,1)} %bitcast.3.arrived_ref), custom_call_target="tpu_custom_call" | custom-call | tf_op jit(solution)/shard_map/pallas_call | solution.py:339
  39.6 3.5 %collective-permute-done.5.refs_0_ = bf16[128,256]{1,0:T(8,128)(2,1)} collective-permute-done((bf16[128,256]{1,0:T(8,128)(2,1)}, bf16[128,256]{1,0:T(8,128)(2,1)}, u32[]{:S(2)}, u32[]{:S(2)}) %collective-permute-start.5) | collective-permute-done | bytes 65568 | tf_op jit(solution)/shard_map/ppermute | solution.py:292
  43.1 1.4 %shard_map.76 = (bf16[128,256]{1,0:T(8,128)(2,1)S(1)}, f32[128,256]{1,0:T(8,128)S(1)}, bf16[128,256]{1,0:T(8,128)(2,1)S(1)}, bf16[128,256]{1,0:T(8,128)(2,1)S(1)...) custom-call(s32[1,10]{1,0:T(1,128)S(1)} %copy-done, ...), custom_call_target="tpu_custom_call" | custom-call | tf_op jit(solution)/shard_map/pallas_call | solution.py:399
  44.5 4.2 %collective-permute-start.7 = (bf16[128,256]{1,0:T(8,128)(2,1)S(1)}, bf16[128,256]{1,0:T(8,128)(2,1)S(1)}, u32[]{:S(2)}, u32[]{:S(2)}) collective-permute-start(bf16[128,256]{1,0:T(8,128)(2,1)S(1)} %get-tuple-element.55), channel_id=1, source_target_pairs={{0,28},{2,30},{4,8},{6,10},{8,4},{10,6},{12,16},{14,18},{16,12},{1... | collective-permute-start | bytes 196616 | tf_op jit(solution)/shard_map/ppermute | solution.py:369
  49.2 2.5 %collective-permute-done.7.refs_0_ = bf16[128,256]{1,0:T(8,128)(2,1)S(1)} collective-permute-done((bf16[128,256]{1,0:T(8,128)(2,1)S(1)}, bf16[128,256]{1,0:T(8,128)(2,1)S(1)}, u32[]{:S(2)}, u32[]{:S(2)}) %collective-permute-start.7) | collective-permute-done | bytes 65568 | tf_op jit(solution)/shard_map/ppermute | solution.py:369
  51.7 3.4 %collective-permute-done.8.refs_1_ = bf16[128,256]{1,0:T(8,128)(2,1)S(1)} collective-permute-done((bf16[128,256]{1,0:T(8,128)(2,1)S(1)}, bf16[128,256]{1,0:T(8,128)(2,1)S(1)}, u32[]{:S(2)}, u32[]{:S(2)}) %collective-permute-start.8) | collective-permute-done | bytes 65568 | tf_op jit(solution)/shard_map/ppermute | solution.py:369
  55.1 1.0 %shard_map.77 = (bf16[128,256]{1,0:T(8,128)(2,1)S(1)}, f32[128,256]{1,0:T(8,128)S(1)}, bf16[128,256]{1,0:T(8,128)(2,1)S(1)}, bf16[128,256]{1,0:T(8,128)(2,1)S(1)...) custom-call(s32[1,10]{1,0:T(1,128)S(1)} %copy-done, ...), custom_call_target="tpu_custom_call" | custom-call | tf_op jit(solution)/shard_map/pallas_call | solution.py:399
  56.8 0.9 %collective-permute-start.12 = (bf16[128,256]{1,0:T(8,128)(2,1)S(1)}, bf16[128,256]{1,0:T(8,128)(2,1)S(1)}, u32[]{:S(2)}, u32[]{:S(2)}) collective-permute-start(bf16[128,256]{1,0:T(8,128)(2,1)S(1)} %get-tuple-element.64), channel_id=1, source_target_pairs={{0,30},{2,4},{4,2},{6,8},{8,6},{10,12},{12,10},{14,16},{16,14},{18... | collective-permute-start | bytes 196616 | tf_op jit(solution)/shard_map/ppermute | solution.py:369
  57.7 1.7 %collective-permute-start.13 = (bf16[128,256]{1,0:T(8,128)(2,1)S(1)}, bf16[128,256]{1,0:T(8,128)(2,1)S(1)}, u32[]{:S(2)}, u32[]{:S(2)}) collective-permute-start(bf16[128,256]{1,0:T(8,128)(2,1)S(1)} %get-tuple-element.65), channel_id=1, source_target_pairs={{0,4},{2,6},{4,0},{6,2},{8,12},{10,14},{12,8},{14,10},{16,20},{18,... | collective-permute-start | bytes 196616 | tf_op jit(solution)/shard_map/ppermute | solution.py:369
  59.3 0.8 %collective-permute-start.15 = (bf16[128,256]{1,0:T(8,128)(2,1)S(1)}, bf16[128,256]{1,0:T(8,128)(2,1)S(1)}, u32[]{:S(2)}, u32[]{:S(2)}) collective-permute-start(bf16[128,256]{1,0:T(8,128)(2,1)S(1)} %get-tuple-element.60.refs_1_), channel_id=1, source_target_pairs={{0,1},{1,0},{2,3},{3,2},{4,5},{5,4},{6,7},{7,6},{8,9},{9,8},{10,11... | collective-permute-start | bytes 196616 | tf_op jit(solution)/shard_map/ppermute | solution.py:381
  60.2 3.7 %collective-permute-done.11.refs_0_ = bf16[128,256]{1,0:T(8,128)(2,1)S(1)} collective-permute-done((bf16[128,256]{1,0:T(8,128)(2,1)S(1)}, bf16[128,256]{1,0:T(8,128)(2,1)S(1)}, u32[]{:S(2)}, u32[]{:S(2)}) %collective-permute-start.11) | collective-permute-done | bytes 65568 | tf_op jit(solution)/shard_map/ppermute | solution.py:369
  63.9 1.1 %shard_map.78 = (bf16[128,256]{1,0:T(8,128)(2,1)S(1)}, f32[128,256]{1,0:T(8,128)S(1)}, bf16[128,256]{1,0:T(8,128)(2,1)S(1)}, bf16[128,256]{1,0:T(8,128)(2,1)S(1)...) custom-call(s32[1,10]{1,0:T(1,128)S(1)} %copy-done, f32[128,256]{1,0:T(8,128)S(1)} %get-tuple-element.61.source, ...), custom_call_target="tpu_custom_call" | custom-call | tf_op jit(solution)/shard_map/pallas_call | solution.py:399
  65.0 3.2 %collective-permute-start.18 = (bf16[128,256]{1,0:T(8,128)(2,1)S(1)}, bf16[128,256]{1,0:T(8,128)(2,1)S(1)}, u32[]{:S(2)}, u32[]{:S(2)}) collective-permute-start(bf16[128,256]{1,0:T(8,128)(2,1)S(1)} %get-tuple-element.71), channel_id=1, source_target_pairs={{0,28},{2,30},{4,8},{6,10},{8,4},{10,6},{12,16},{14,18},{16,12},{1... | collective-permute-start | bytes 196616 | tf_op jit(solution)/shard_map/ppermute | solution.py:369
  68.7 1.0 %collective-permute-start.20 = (bf16[128,256]{1,0:T(8,128)(2,1)S(1)}, bf16[128,256]{1,0:T(8,128)(2,1)S(1)}, u32[]{:S(2)}, u32[]{:S(2)}) collective-permute-start(bf16[128,256]{1,0:T(8,128)(2,1)S(1)} %get-tuple-element.73), channel_id=1, source_target_pairs={{0,4},{2,6},{4,0},{6,2},{8,12},{10,14},{12,8},{14,10},{16,20},{18,... | collective-permute-start | bytes 196616 | tf_op jit(solution)/shard_map/ppermute | solution.py:369
  69.7 1.0 %collective-permute-start.17 = (bf16[128,256]{1,0:T(8,128)(2,1)S(1)}, bf16[128,256]{1,0:T(8,128)(2,1)S(1)}, u32[]{:S(2)}, u32[]{:S(2)}) collective-permute-start(bf16[128,256]{1,0:T(8,128)(2,1)S(1)} %get-tuple-element.68.refs_2_), channel_id=1, source_target_pairs={{0,1},{1,0},{2,3},{3,2},{4,5},{5,4},{6,7},{7,6},{8,9},{9,8},{10,11... | collective-permute-start | bytes 196616 | tf_op jit(solution)/shard_map/ppermute | solution.py:381
  70.7 1.4 %collective-permute-done.18.refs_0_ = bf16[128,256]{1,0:T(8,128)(2,1)S(1)} collective-permute-done((bf16[128,256]{1,0:T(8,128)(2,1)S(1)}, bf16[128,256]{1,0:T(8,128)(2,1)S(1)}, u32[]{:S(2)}, u32[]{:S(2)}) %collective-permute-start.18) | collective-permute-done | bytes 65568 | tf_op jit(solution)/shard_map/ppermute | solution.py:369
  72.1 0.9 %collective-permute-start.16 = (bf16[128,256]{1,0:T(8,128)(2,1)S(1)}, bf16[128,256]{1,0:T(8,128)(2,1)S(1)}, u32[]{:S(2)}, u32[]{:S(2)}) collective-permute-start(bf16[128,256]{1,0:T(8,128)(2,1)S(1)} %get-tuple-element.52.refs_0_), channel_id=1, source_target_pairs={{0,1},{1,0},{2,3},{3,2},{4,5},{5,4},{6,7},{7,6},{8,9},{9,8},{10,11... | collective-permute-start | bytes 196616 | tf_op jit(solution)/shard_map/ppermute | solution.py:381
  73.0 1.6 %collective-permute-done.19.refs_1_ = bf16[128,256]{1,0:T(8,128)(2,1)S(1)} collective-permute-done((bf16[128,256]{1,0:T(8,128)(2,1)S(1)}, bf16[128,256]{1,0:T(8,128)(2,1)S(1)}, u32[]{:S(2)}, u32[]{:S(2)}) %collective-permute-start.19) | collective-permute-done | bytes 65568 | tf_op jit(solution)/shard_map/ppermute | solution.py:369
  75.4 1.1 %collective-permute-start.22 = (bf16[128,256]{1,0:T(8,128)(2,1)S(1)}, bf16[128,256]{1,0:T(8,128)(2,1)S(1)}, u32[]{:S(2)}, u32[]{:S(2)}) collective-permute-start(bf16[128,256]{1,0:T(8,128)(2,1)S(1)} %shard_map.80.mine), channel_id=1, source_target_pairs={{0,1},{1,0},{2,3},{3,2},{4,5},{5,4},{6,7},{7,6},{8,9},{9,8},{10,11... | collective-permute-start | bytes 196616 | tf_op jit(solution)/shard_map/ppermute | solution.py:381
  76.5 0.8 %shard_map.79.begun = bf16[4,256,128]{2,1,0:T(8,128)(2,1)} custom-call(bf16[128,256]{1,0:T(8,128)(2,1)S(1)} %get-tuple-element.52.refs_0_, bf16[128,256]{1,0:T(8,128)(2,1)S(1)} %get-tuple-element.60.refs_1_, bf16[128,256]{1,0:T(8,128)(2,1)S(1)} %get-tuple-element.68.refs_2_, bf16[128,256]{1,0:T(8,128)(2,1)S(1)} %collective-permute-done.16.refs_3_, ...), custom_call_target="tpu_custom_call" | custom-call | tf_op jit(solution)/shard_map/pallas_call | solution.py:418
  77.3 2.4 %collective-permute-done.22.far = bf16[128,256]{1,0:T(8,128)(2,1)S(1)} collective-permute-done((bf16[128,256]{1,0:T(8,128)(2,1)S(1)}, bf16[128,256]{1,0:T(8,128)(2,1)S(1)}, u32[]{:S(2)}, u32[]{:S(2)}) %collective-permute-start.22) | collective-permute-done | bytes 65568 | tf_op jit(solution)/shard_map/ppermute | solution.py:381
  79.8 0.7 shard_map.81
  (31 shorter events, 4.2 us)
Async XLA Ops:
  2.8 35.5 %all-to-all-start = ((bf16[16,16,640]{2,1,0:T(8,128)(2,1)}), bf16[16,16,640]{2,1,0:T(8,128)(2,1)}, u32[]{:S(2)}, u32[]{:S(2)}) async-start(bf16[16,16,640]{2,1,0:T(8,128)(2,1)} %bitcast.2), calls=%async_computation | async-start | bytes 655360 | tf_op jit(solution)/shard_map/all_to_all | solution.py:332
  10.3 32.8 %copy-start = (s32[1,10]{1,0:T(1,128)S(1)}, s32[1,10]{1,0:T(1,128)}, u32[]{:S(2)}) copy-start(s32[1,10]{1,0:T(1,128)} %ranges.9) | copy-start | bytes 124
  10.3 7.2 %collective-permute-start = (bf16[3,256,128]{2,1,0:T(8,128)(2,1)S(1)}, bf16[3,256,128]{2,1,0:T(8,128)(2,1)S(1)}, u32[]{:S(2)}, u32[]{:S(2)}) collective-permute-start(bf16[3,256,128]{2,1,0:T(8,128)(2,1)S(1)} %get-tuple-element.42), channel_id=1, source_target_pairs={{0,1},{1,0},{2,3},{3,2},{4,5},{5,4},{6,7},{7,6},{8,9},{9,8},{10,11... | collective-permute-start | bytes 589832 | tf_op jit(solution)/shard_map/ppermute | solution.py:331
  17.6 0.7 copy-start.1
  27.2 7.3 %collective-permute-start.1 = (bf16[128,256]{1,0:T(8,128)(2,1)}, bf16[128,256]{1,0:T(8,128)(2,1)S(1)}, u32[]{:S(2)}, u32[]{:S(2)}) collective-permute-start(bf16[128,256]{1,0:T(8,128)(2,1)} %get-tuple-element.45), channel_id=1, source_target_pairs={{0,28},{2,30},{4,8},{6,10},{8,4},{10,6},{12,16},{14,18},{16,12},{1... | collective-permute-start | bytes 196616 | tf_op jit(solution)/shard_map/ppermute | solution.py:369
  31.0 6.6 %collective-permute-start.2 = (bf16[128,256]{1,0:T(8,128)(2,1)}, bf16[128,256]{1,0:T(8,128)(2,1)S(1)}, u32[]{:S(2)}, u32[]{:S(2)}) collective-permute-start(bf16[128,256]{1,0:T(8,128)(2,1)} %get-tuple-element.46), channel_id=1, source_target_pairs={{0,30},{2,4},{4,2},{6,8},{8,6},{10,12},{12,10},{14,16},{16,14},{18... | collective-permute-start | bytes 196616 | tf_op jit(solution)/shard_map/ppermute | solution.py:369
  31.0 6.6 %collective-permute-start.3 = (bf16[128,256]{1,0:T(8,128)(2,1)}, bf16[128,256]{1,0:T(8,128)(2,1)S(1)}, u32[]{:S(2)}, u32[]{:S(2)}) collective-permute-start(bf16[128,256]{1,0:T(8,128)(2,1)} %get-tuple-element.47), channel_id=1, source_target_pairs={{0,4},{2,6},{4,0},{6,2},{8,12},{10,14},{12,8},{14,10},{16,20},{18,... | collective-permute-start | bytes 196616 | tf_op jit(solution)/shard_map/ppermute | solution.py:369
  31.3 6.4 %collective-permute-start.4 = (bf16[128,256]{1,0:T(8,128)(2,1)}, bf16[128,256]{1,0:T(8,128)(2,1)S(1)}, u32[]{:S(2)}, u32[]{:S(2)}) collective-permute-start(bf16[128,256]{1,0:T(8,128)(2,1)} %get-tuple-element.48), channel_id=1, source_target_pairs={{0,2},{2,0},{4,6},{6,4},{8,10},{10,8},{12,14},{14,12},{16,18},{18,... | collective-permute-start | bytes 196616 | tf_op jit(solution)/shard_map/ppermute | solution.py:369
  31.4 11.7 %collective-permute-start.6 = (bf16[640,256]{1,0:T(8,128)(2,1)}, bf16[640,256]{1,0:T(8,128)(2,1)}, u32[]{:S(2)}, u32[]{:S(2)}) collective-permute-start(bf16[640,256]{1,0:T(8,128)(2,1)} %get-tuple-element.51), channel_id=1, source_target_pairs={{0,1},{1,0},{2,3},{3,2},{4,5},{5,4},{6,7},{7,6},{8,9},{9,8},{10,11... | collective-permute-start | bytes 983048 | tf_op jit(solution)/shard_map/ppermute | solution.py:292
  38.3 4.8 %collective-permute-start.5 = (bf16[128,256]{1,0:T(8,128)(2,1)}, bf16[128,256]{1,0:T(8,128)(2,1)}, u32[]{:S(2)}, u32[]{:S(2)}) collective-permute-start(bf16[128,256]{1,0:T(8,128)(2,1)} %get-tuple-element.75), channel_id=1, source_target_pairs={{0,1},{1,0},{2,3},{3,2},{4,5},{5,4},{6,7},{7,6},{8,9},{9,8},{10,11... | collective-permute-start | bytes 196616 | tf_op jit(solution)/shard_map/ppermute | solution.py:292
  44.5 7.1 %collective-permute-start.7 = (bf16[128,256]{1,0:T(8,128)(2,1)S(1)}, bf16[128,256]{1,0:T(8,128)(2,1)S(1)}, u32[]{:S(2)}, u32[]{:S(2)}) collective-permute-start(bf16[128,256]{1,0:T(8,128)(2,1)S(1)} %get-tuple-element.55), channel_id=1, source_target_pairs={{0,28},{2,30},{4,8},{6,10},{8,4},{10,6},{12,16},{14,18},{16,12},{1... | collective-permute-start | bytes 196616 | tf_op jit(solution)/shard_map/ppermute | solution.py:369
  48.7 6.4 %collective-permute-start.8 = (bf16[128,256]{1,0:T(8,128)(2,1)S(1)}, bf16[128,256]{1,0:T(8,128)(2,1)S(1)}, u32[]{:S(2)}, u32[]{:S(2)}) collective-permute-start(bf16[128,256]{1,0:T(8,128)(2,1)S(1)} %get-tuple-element.56), channel_id=1, source_target_pairs={{0,30},{2,4},{4,2},{6,8},{8,6},{10,12},{12,10},{14,16},{16,14},{18... | collective-permute-start | bytes 196616 | tf_op jit(solution)/shard_map/ppermute | solution.py:369
  48.7 6.4 %collective-permute-start.9 = (bf16[128,256]{1,0:T(8,128)(2,1)S(1)}, bf16[128,256]{1,0:T(8,128)(2,1)S(1)}, u32[]{:S(2)}, u32[]{:S(2)}) collective-permute-start(bf16[128,256]{1,0:T(8,128)(2,1)S(1)} %get-tuple-element.57), channel_id=1, source_target_pairs={{0,4},{2,6},{4,0},{6,2},{8,12},{10,14},{12,8},{14,10},{16,20},{18,... | collective-permute-start | bytes 196616 | tf_op jit(solution)/shard_map/ppermute | solution.py:369
  49.2 5.9 %collective-permute-start.10 = (bf16[128,256]{1,0:T(8,128)(2,1)S(1)}, bf16[128,256]{1,0:T(8,128)(2,1)S(1)}, u32[]{:S(2)}, u32[]{:S(2)}) collective-permute-start(bf16[128,256]{1,0:T(8,128)(2,1)S(1)} %get-tuple-element.58), channel_id=1, source_target_pairs={{0,2},{2,0},{4,6},{6,4},{8,10},{10,8},{12,14},{14,12},{16,18},{18,... | collective-permute-start | bytes 196616 | tf_op jit(solution)/shard_map/ppermute | solution.py:369
  56.1 7.7 %collective-permute-start.11 = (bf16[128,256]{1,0:T(8,128)(2,1)S(1)}, bf16[128,256]{1,0:T(8,128)(2,1)S(1)}, u32[]{:S(2)}, u32[]{:S(2)}) collective-permute-start(bf16[128,256]{1,0:T(8,128)(2,1)S(1)} %get-tuple-element.63), channel_id=1, source_target_pairs={{0,28},{2,30},{4,8},{6,10},{8,4},{10,6},{12,16},{14,18},{16,12},{1... | collective-permute-start | bytes 196616 | tf_op jit(solution)/shard_map/ppermute | solution.py:369
  56.8 7.1 %collective-permute-start.12 = (bf16[128,256]{1,0:T(8,128)(2,1)S(1)}, bf16[128,256]{1,0:T(8,128)(2,1)S(1)}, u32[]{:S(2)}, u32[]{:S(2)}) collective-permute-start(bf16[128,256]{1,0:T(8,128)(2,1)S(1)} %get-tuple-element.64), channel_id=1, source_target_pairs={{0,30},{2,4},{4,2},{6,8},{8,6},{10,12},{12,10},{14,16},{16,14},{18... | collective-permute-start | bytes 196616 | tf_op jit(solution)/shard_map/ppermute | solution.py:369
  57.7 6.2 %collective-permute-start.13 = (bf16[128,256]{1,0:T(8,128)(2,1)S(1)}, bf16[128,256]{1,0:T(8,128)(2,1)S(1)}, u32[]{:S(2)}, u32[]{:S(2)}) collective-permute-start(bf16[128,256]{1,0:T(8,128)(2,1)S(1)} %get-tuple-element.65), channel_id=1, source_target_pairs={{0,4},{2,6},{4,0},{6,2},{8,12},{10,14},{12,8},{14,10},{16,20},{18,... | collective-permute-start | bytes 196616 | tf_op jit(solution)/shard_map/ppermute | solution.py:369
  59.3 4.5 %collective-permute-start.14 = (bf16[128,256]{1,0:T(8,128)(2,1)S(1)}, bf16[128,256]{1,0:T(8,128)(2,1)S(1)}, u32[]{:S(2)}, u32[]{:S(2)}) collective-permute-start(bf16[128,256]{1,0:T(8,128)(2,1)S(1)} %get-tuple-element.66), channel_id=1, source_target_pairs={{0,2},{2,0},{4,6},{6,4},{8,10},{10,8},{12,14},{14,12},{16,18},{18,... | collective-permute-start | bytes 196616 | tf_op jit(solution)/shard_map/ppermute | solution.py:369
  59.3 4.5 %collective-permute-start.15 = (bf16[128,256]{1,0:T(8,128)(2,1)S(1)}, bf16[128,256]{1,0:T(8,128)(2,1)S(1)}, u32[]{:S(2)}, u32[]{:S(2)}) collective-permute-start(bf16[128,256]{1,0:T(8,128)(2,1)S(1)} %get-tuple-element.60.refs_1_), channel_id=1, source_target_pairs={{0,1},{1,0},{2,3},{3,2},{4,5},{5,4},{6,7},{7,6},{8,9},{9,8},{10,11... | collective-permute-start | bytes 196616 | tf_op jit(solution)/shard_map/ppermute | solution.py:381
  65.0 7.1 %collective-permute-start.18 = (bf16[128,256]{1,0:T(8,128)(2,1)S(1)}, bf16[128,256]{1,0:T(8,128)(2,1)S(1)}, u32[]{:S(2)}, u32[]{:S(2)}) collective-permute-start(bf16[128,256]{1,0:T(8,128)(2,1)S(1)} %get-tuple-element.71), channel_id=1, source_target_pairs={{0,28},{2,30},{4,8},{6,10},{8,4},{10,6},{12,16},{14,18},{16,12},{1... | collective-permute-start | bytes 196616 | tf_op jit(solution)/shard_map/ppermute | solution.py:369
  68.2 6.4 %collective-permute-start.19 = (bf16[128,256]{1,0:T(8,128)(2,1)S(1)}, bf16[128,256]{1,0:T(8,128)(2,1)S(1)}, u32[]{:S(2)}, u32[]{:S(2)}) collective-permute-start(bf16[128,256]{1,0:T(8,128)(2,1)S(1)} %get-tuple-element.72), channel_id=1, source_target_pairs={{0,30},{2,4},{4,2},{6,8},{8,6},{10,12},{12,10},{14,16},{16,14},{18... | collective-permute-start | bytes 196616 | tf_op jit(solution)/shard_map/ppermute | solution.py:369
  68.7 5.9 %collective-permute-start.20 = (bf16[128,256]{1,0:T(8,128)(2,1)S(1)}, bf16[128,256]{1,0:T(8,128)(2,1)S(1)}, u32[]{:S(2)}, u32[]{:S(2)}) collective-permute-start(bf16[128,256]{1,0:T(8,128)(2,1)S(1)} %get-tuple-element.73), channel_id=1, source_target_pairs={{0,4},{2,6},{4,0},{6,2},{8,12},{10,14},{12,8},{14,10},{16,20},{18,... | collective-permute-start | bytes 196616 | tf_op jit(solution)/shard_map/ppermute | solution.py:369
  69.7 4.9 %collective-permute-start.21 = (bf16[128,256]{1,0:T(8,128)(2,1)S(1)}, bf16[128,256]{1,0:T(8,128)(2,1)S(1)}, u32[]{:S(2)}, u32[]{:S(2)}) collective-permute-start(bf16[128,256]{1,0:T(8,128)(2,1)S(1)} %get-tuple-element.74), channel_id=1, source_target_pairs={{0,2},{2,0},{4,6},{6,4},{8,10},{10,8},{12,14},{14,12},{16,18},{18,... | collective-permute-start | bytes 196616 | tf_op jit(solution)/shard_map/ppermute | solution.py:369
  69.7 5.0 %collective-permute-start.17 = (bf16[128,256]{1,0:T(8,128)(2,1)S(1)}, bf16[128,256]{1,0:T(8,128)(2,1)S(1)}, u32[]{:S(2)}, u32[]{:S(2)}) collective-permute-start(bf16[128,256]{1,0:T(8,128)(2,1)S(1)} %get-tuple-element.68.refs_2_), channel_id=1, source_target_pairs={{0,1},{1,0},{2,3},{3,2},{4,5},{5,4},{6,7},{7,6},{8,9},{9,8},{10,11... | collective-permute-start | bytes 196616 | tf_op jit(solution)/shard_map/ppermute | solution.py:381
  72.1 4.3 %collective-permute-start.16 = (bf16[128,256]{1,0:T(8,128)(2,1)S(1)}, bf16[128,256]{1,0:T(8,128)(2,1)S(1)}, u32[]{:S(2)}, u32[]{:S(2)}) collective-permute-start(bf16[128,256]{1,0:T(8,128)(2,1)S(1)} %get-tuple-element.52.refs_0_), channel_id=1, source_target_pairs={{0,1},{1,0},{2,3},{3,2},{4,5},{5,4},{6,7},{7,6},{8,9},{9,8},{10,11... | collective-permute-start | bytes 196616 | tf_op jit(solution)/shard_map/ppermute | solution.py:381
  75.4 4.3 %collective-permute-start.22 = (bf16[128,256]{1,0:T(8,128)(2,1)S(1)}, bf16[128,256]{1,0:T(8,128)(2,1)S(1)}, u32[]{:S(2)}, u32[]{:S(2)}) collective-permute-start(bf16[128,256]{1,0:T(8,128)(2,1)S(1)} %shard_map.80.mine), channel_id=1, source_target_pairs={{0,1},{1,0},{2,3},{3,2},{4,5},{5,4},{6,7},{7,6},{8,9},{9,8},{10,11... | collective-permute-start | bytes 196616 | tf_op jit(solution)/shard_map/ppermute | solution.py:381
